TPU v7x, 32 devices: a whole 2x2x4 slice. The times are simulated.
32 devices in a mesh: ia: 2 (over x), ja: 4 (over y, core), ka: 4 (over z).
Axes of the slice: x: 2, y: 2, z: 4, core: 2. Of those that a mesh axis runs over, the one named last changes fastest.
Arguments:
- tensor: bfloat16 [512, 512, 512], P('ia', 'ja', 'ka'), may hold values from 0 to 122880
- matrix: bfloat16 [512, 32768], P(None, ('ia', 'ja', 'ka')), may hold values from 0 to 4096000
- first_factor: bfloat16 [512, 256], P('ia'), may hold values from 0.05 to 2
- second_factor: bfloat16 [512, 256], P('ja'), may hold values from 0.05 to 2
- time_factor: bfloat16 [512, 256], P('ka'), may hold values from 0.05 to 2
- column_factor: bfloat16 [32768, 256], P(('ia', 'ja', 'ka')), may hold values from 0.05 to 2
Outputs:
- first_new: bfloat16 [512, 256], P('ia')
- second_new: bfloat16 [512, 256], P('ja')
- time_new: bfloat16 [512, 256], P('ka')
All inputs are finite; a program needn't handle non-finite values.
Results may differ from a plain program's by a relative error of at most 0.00075.
The roundings to bfloat16 on the way count: a program that leaves them out, or rounds other values in their place, can miss the bound.
Values may be sent and summed in bfloat16 or wider, within the bound.
No kernel may reach another device: no remote copies, remote signals or barrier semaphores. Data moves between devices by JAX's collectives and lax.ppermute only.
A program may use at most 128 MiB of HBM per device.

v0:
```python
import functools

import jax
import jax.numpy as jnp
from jax import lax
from jax.experimental import pallas as pl
from jax.experimental.pallas import tpu as pltpu
from jax.sharding import PartitionSpec as P


ANY = pl.BlockSpec(memory_space=pl.ANY)
VMEM = pl.BlockSpec(memory_space=pltpu.VMEM)
LIMIT = 32 << 20


def in_hbm(values):
    return pltpu.with_memory_space_constraint(values, pltpu.HBM)


def chunk_of(length, most):
    size = min(length, most)
    while length % size:
        size //= 2
    return size


def kernel_call(kernel, flops, nbytes, **kwargs):
    return pl.pallas_call(
        kernel,
        cost_estimate=pl.CostEstimate(flops=flops, bytes_accessed=nbytes, transcendentals=0),
        compiler_params=pltpu.CompilerParams(vmem_limit_bytes=LIMIT),
        **kwargs,
    )


def local_kernel(matrix, column, second, time, coupled, grams, gram_time):
    f32 = jnp.float32
    rank = column.shape[1]
    turned = column[...].T
    grams[:, :rank] = jnp.dot(turned, column[...], preferred_element_type=f32)
    coupled[...] = lax.dot_general(
        turned, matrix[...], (((1,), (1,)), ((), ())), preferred_element_type=f32
    )
    grams[:, rank:] = jnp.dot(second[...].T, second[...], preferred_element_type=f32)
    gram_time[...] = jnp.dot(time[...].T, time[...], preferred_element_type=f32)


def local_products(matrix, column, second, time):
    rank = column.shape[1]
    rows, width = matrix.shape
    f32 = jnp.float32
    return kernel_call(
        local_kernel,
        2 * width * rank * (rows + rank),
        2 * width * (rows + rank),
        out_shape=(
            jax.ShapeDtypeStruct((rank, rows), f32),
            jax.ShapeDtypeStruct((rank, 2 * rank), f32),
            jax.ShapeDtypeStruct((rank, rank), f32),
        ),
        in_specs=[VMEM] * 4,
        out_specs=(VMEM,) * 3,
    )(matrix, column, second, time)


def slab_kernel(chunk, steps, tensor, second, time, total, turned, read, read_sem, ready, ready_sem, added):
    def fetch(step):
        source = tensor.at[:, pl.ds(step * chunk, chunk)]
        return pltpu.make_async_copy(source, read.at[step], read_sem.at[step])

    def put(step):
        target = turned.at[pl.ds(step * chunk, chunk)]
        return pltpu.make_async_copy(ready.at[step], target, ready_sem.at[step])

    for step in range(steps):
        fetch(step).start()
    time_wide = time[...].astype(jnp.float32)
    added[...] = jnp.zeros_like(added)

    def body(step, carry):
        fetch(step).wait()
        block = jnp.swapaxes(read[step], 0, 1)
        for j in range(chunk):
            ready[step, j] = block[j].T
        put(step).start()
        row = pl.multiple_of(step * chunk, chunk)
        weights = second[pl.ds(row, chunk), :].astype(jnp.float32)
        khatri = jnp.concatenate(
            [(weights[j : j + 1, :] * time_wide).astype(jnp.bfloat16) for j in range(chunk)], 0
        )
        tiles = jnp.concatenate([block[j] for j in range(chunk)], 1)
        added[...] += jnp.dot(tiles, khatri, preferred_element_type=jnp.float32)
        return carry

    lax.fori_loop(0, steps, body, 0)
    total[...] = added[...].T

    def finish(step, carry):
        put(step).wait()
        return carry

    lax.fori_loop(0, steps, finish, 0)


def slab_and_turn(tensor, second, time):
    tile_i, tile_j, tile_k = tensor.shape
    rank = time.shape[1]
    chunk = chunk_of(tile_j, 16)
    steps = tile_j // chunk
    return kernel_call(
        functools.partial(slab_kernel, chunk, steps),
        2 * tile_i * tile_j * tile_k * rank,
        4 * tile_i * tile_j * tile_k,
        out_shape=(
            jax.ShapeDtypeStruct((rank, tile_i), jnp.float32),
            pltpu.HBM((tile_j, tile_k, tile_i), tensor.dtype),
        ),
        in_specs=[ANY, VMEM, VMEM],
        out_specs=(VMEM, ANY),
        scratch_shapes=[
            pltpu.VMEM((steps, tile_i, chunk, tile_k), tensor.dtype),
            pltpu.SemaphoreType.DMA((steps,)),
            pltpu.VMEM((steps, chunk, tile_k, tile_i), tensor.dtype),
            pltpu.SemaphoreType.DMA((steps,)),
            pltpu.VMEM((tile_i, rank), jnp.float32),
        ],
    )(in_hbm(tensor), second, time)


def fetcher(turned, read, read_sem, chunk):
    def fetch(step):
        source = turned.at[pl.ds(step * chunk, chunk)]
        return pltpu.make_async_copy(source, read.at[step], read_sem.at[step])

    for step in range(read.shape[0]):
        fetch(step).start()
    return fetch


def plane_kernel(chunk, turned, first_turned, time, total, first, read, read_sem):
    fetch = fetcher(turned, read, read_sem, chunk)
    first[...] = first_turned[...].T
    shared = first[...]

    def body(step, carry):
        fetch(step).wait()
        sums = []
        for j in range(chunk):
            weighted = jnp.dot(read[step, j], shared, preferred_element_type=jnp.float32)
            scaled = weighted * time[...].astype(jnp.float32)
            sums.append(jnp.sum(scaled, axis=0, keepdims=True))
        row = pl.multiple_of(step * chunk, chunk)
        total[pl.ds(row, chunk), :] = jnp.concatenate(sums, 0)
        return carry

    lax.fori_loop(0, read.shape[0], body, 0)


def time_kernel(chunk, turned, first, second, total, read, read_sem, wide):
    fetch = fetcher(turned, read, read_sem, chunk)
    wide[...] = second[...].astype(jnp.float32)
    total[...] = jnp.zeros_like(total)
    shared = first[...]

    def body(step, carry):
        fetch(step).wait()
        part = total[...]
        for j in range(chunk):
            weighted = jnp.dot(read[step, j], shared, preferred_element_type=jnp.float32)
            part = part + weighted * wide[pl.ds(step * chunk + j, 1), :]
        total[...] = part
        return carry

    lax.fori_loop(0, read.shape[0], body, 0)


def weighted_call(kernel, turned, args, outs, extra=()):
    tile_j, tile_k, tile_i = turned.shape
    chunk = chunk_of(tile_j, 16)
    steps = tile_j // chunk
    rank = args[0].shape[0]
    return kernel_call(
        functools.partial(kernel, chunk),
        2 * tile_i * tile_j * tile_k * rank,
        2 * tile_i * tile_j * tile_k,
        out_shape=outs,
        in_specs=[ANY] + [VMEM] * len(args),
        out_specs=(VMEM,) * len(outs),
        scratch_shapes=[
            pltpu.VMEM((steps, chunk, tile_k, tile_i), turned.dtype),
            pltpu.SemaphoreType.DMA((steps,)),
            *extra,
        ],
    )(in_hbm(turned), *args)


def cross_product(values):
    return lax.dot_general(
        values, values, (((0,), (0,)), ((), ())), preferred_element_type=jnp.float32
    )


def row_product(values):
    return lax.dot_general(
        values, values, (((1,), (1,)), ((), ())), preferred_element_type=jnp.float32
    )


def swap(values, axis, size, mask):
    return lax.ppermute(values, axis, [(i, i ^ mask) for i in range(size)])


def halve(values, axis, size, mask, dim=0):
    half = values.shape[dim] // 2
    bit = (lax.axis_index(axis) & mask) // mask
    kept = lax.dynamic_slice_in_dim(values, bit * half, half, dim)
    sent = lax.dynamic_slice_in_dim(values, (1 - bit) * half, half, dim)
    return kept + swap(sent, axis, size, mask)


def double(values, axis, size, mask):
    other = swap(values, axis, size, mask)
    bit = (lax.axis_index(axis) & mask) // mask
    return jnp.where(
        bit == 0,
        jnp.concatenate([values, other], 0),
        jnp.concatenate([other, values], 0),
    )


def tree_sum(terms):
    while len(terms) > 1:
        terms = [terms[i] + terms[i + 1] for i in range(0, len(terms), 2)]
    return terms[0]


def masks_of(size):
    return [1 << b for b in range(size.bit_length() - 1)]


def spread(values, axis, size, step=1):
    return [values] + [swap(values, axis, size, d) for d in range(step, size, step)]


def all_sum(values, axis, size, step=1):
    return tree_sum(spread(values, axis, size, step))


def full_dot(left, right, dims):
    return lax.dot_general(
        left, right, (dims, ((), ())), precision=lax.Precision.HIGHEST,
        preferred_element_type=jnp.float32,
    )


def on_device(
    size_i, size_j, size_k, tensor, matrix, first_factor, second_factor, time_factor, column_factor
):
    f32 = jnp.float32
    tile_i, tile_j, tile_k = tensor.shape
    rank = first_factor.shape[1]
    share = rank // size_j
    part = 0
    for mask in masks_of(size_j):
        part = 2 * part + (lax.axis_index("ja") & mask) // mask

    coupled, grams, gram_time = local_products(matrix, column_factor, second_factor, time_factor)
    for mask in masks_of(size_j):
        grams = halve(grams, "ja", size_j, mask)
    gram_second = grams[:, rank:]
    time_rows = lax.dynamic_slice_in_dim(gram_time, part * share, share, 0)
    grams = jnp.concatenate([grams[:, :rank], time_rows], 1)
    for mask in masks_of(size_k):
        grams = grams + swap(grams, "ka", size_k, mask)
    gram_column, time_rows = grams[:, :rank], grams[:, rank:]
    gram_column = all_sum(gram_column, "ia", size_i)
    gram_total = gram_second * time_rows + gram_column
    first_wide = first_factor.astype(f32)
    denominator = full_dot(gram_total, first_wide, ((1,), (1,)))

    for mask in reversed(masks_of(size_i)):
        coupled = halve(coupled, "ia", size_i, mask, 1)
    slab, turned = slab_and_turn(tensor, second_factor, time_factor)
    numerator = slab + coupled
    for mask in masks_of(size_j):
        numerator = halve(numerator, "ja", size_j, mask)
    numerator = all_sum(numerator, "ka", size_k)
    own = lax.dynamic_slice_in_dim(first_wide.T, part * share, share, 0)
    first_new = (own * numerator / denominator).astype(jnp.bfloat16)
    for mask in reversed(masks_of(size_j)):
        first_new = double(first_new, "ja", size_j, mask)

    firsts = spread(first_new, "ia", size_i)
    gram_first = tree_sum([row_product(piece) for piece in firsts])
    times = time_factor
    for mask in masks_of(size_k):
        times = double(times, "ka", size_k, mask)
    gram_time = cross_product(times)
    plane_sum, first_out = weighted_call(
        plane_kernel,
        turned,
        (first_new, time_factor),
        (
            jax.ShapeDtypeStruct((tile_j, rank), f32),
            jax.ShapeDtypeStruct((tile_i, rank), jnp.bfloat16),
        ),
    )
    for mask in reversed(masks_of(size_i)):
        plane_sum = halve(plane_sum, "ia", size_i, mask)
    plane_sum = all_sum(plane_sum, "ka", size_k)
    rows = tile_j // size_i
    own = lax.dynamic_slice_in_dim(second_factor, lax.axis_index("ia") * rows, rows, 0).astype(f32)
    denominator = full_dot(own, gram_first * gram_time, ((1,), (0,)))
    second_new = (own * plane_sum / denominator).astype(jnp.bfloat16)
    for mask in masks_of(size_i):
        second_new = double(second_new, "ia", size_i, mask)

    seconds = second_new
    for mask in reversed(masks_of(size_j)):
        seconds = double(seconds, "ja", size_j, mask)
    gram_new = cross_product(seconds)
    (time_sum,) = weighted_call(
        time_kernel,
        turned,
        (first_out, second_new),
        (jax.ShapeDtypeStruct((tile_k, rank), f32),),
        (pltpu.VMEM((tile_j, rank), f32),),
    )
    time_sum = halve(time_sum, "ja", size_j, 1)
    time_sum = all_sum(time_sum, "ja", size_j, 2)
    time_sum = all_sum(time_sum, "ia", size_i)
    rows = tile_k // 2
    own = lax.dynamic_slice_in_dim(
        time_factor, (lax.axis_index("ja") % 2) * rows, rows, 0
    ).astype(f32)
    denominator = full_dot(own, gram_first * gram_new, ((1,), (0,)))
    time_new = (own * time_sum / denominator).astype(jnp.bfloat16)
    time_new = double(time_new, "ja", size_j, 1)
    return (first_out, second_new, time_new)


def in_layer(sizes, *args):
    return on_device(*sizes, *args)


def solution(mesh):
    sizes = (mesh.shape["ia"], mesh.shape["ja"], mesh.shape["ka"])
    return jax.shard_map(
        functools.partial(in_layer, sizes),
        mesh=mesh,
        in_specs=(
            P("ia", "ja", "ka"),
            P(None, ("ia", "ja", "ka")),
            P("ia", None),
            P("ja", None),
            P("ka", None),
            P(("ia", "ja", "ka"), None),
        ),
        out_specs=(P("ia", None), P("ja", None), P("ka", None)),
        check_vma=False,
    )
```

profile of v0, /device:TPU:0, one launch (start us, length us, event | category | flops | bytes accessed | tf_op | source)
XLA Modules:
  0.0 94.1 jit_solution(2284085847825481028)
XLA Ops:
  1.5 1.2 %copy-done.4 = bf16[512,1024]{1,0:T(8,128)(2,1)S(1)} copy-done((bf16[512,1024]{1,0:T(8,128)(2,1)S(1)}, bf16[512,1024]{1,0:T(8,128)(2,1)}, u32[]{:S(2)}) %copy-start.4) | copy-done | bytes 1048600
  3.6 1.0 %copy-done.9 = bf16[1024,256]{1,0:T(8,128)(2,1)S(1)} copy-done((bf16[1024,256]{1,0:T(8,128)(2,1)S(1)}, bf16[1024,256]{1,0:T(8,128)(2,1)}, u32[]{:S(2)}) %copy-start.9) | copy-done | bytes 524312
  5.9 2.6 %collective-permute-start = (f32[256,256]{1,0:T(8,128)S(1)}, f32[256,256]{1,0:T(8,128)S(1)}, u32[]{:S(2)}, u32[]{:S(2)}) collective-permute-start(f32[256,256]{1,0:T(8,128)S(1)} %constant_dynamic-slice_fusion.7), channel_id=1, source_target_pairs={{0,16},{16,0},{1,17},{17,1},{2,18},{18,2},{3,19},{19,3},{4,20},{20... | collective-permute-start | bytes 786440 | tf_op jit(solution)/shard_map/ppermute | solution.py:210
  10.2 7.8 %shard_map.85 = (f32[256,256]{1,0:T(8,128)S(1)}, bf16[128,128,256]{2,1,0:T(8,128)(2,1)}) custom-call(bf16[256,128,128]{2,1,0:T(8,128)(2,1)} %tensor.1, bf16[128,256]{1,0:T(8,128)(2,1)S(1)} %copy-done.7, bf16[128,256]{1,0:T(8,128)(2,1)S(1)} %copy-done.2), custom_call_target="tpu_custom_call" | custom-call | flops 2147483648 | bytes 16777216 | tf_op jit(solution)/shard_map/pallas_call | solution.py:110
  18.1 1.6 %collective-permute-start.7 = (f32[64,512]{1,0:T(8,128)S(1)}, f32[64,512]{1,0:T(8,128)S(1)}, u32[]{:S(2)}, u32[]{:S(2)}) collective-permute-start(f32[64,512]{1,0:T(8,128)S(1)} %constant_dynamic-slice_fusion.3), channel_id=1, source_target_pairs={{0,8},{4,12},{8,0},{12,4},{1,9},{5,13},{9,1},{13,5},{2,10},{6,14},... | collective-permute-start | bytes 393224 | tf_op jit(solution)/shard_map/ppermute | solution.py:210
  19.9 3.9 %collective-permute-done.7 = f32[64,512]{1,0:T(8,128)S(1)} collective-permute-done((f32[64,512]{1,0:T(8,128)S(1)}, f32[64,512]{1,0:T(8,128)S(1)}, u32[]{:S(2)}, u32[]{:S(2)}) %collective-permute-start.7) | collective-permute-done | bytes 131104 | tf_op jit(solution)/shard_map/ppermute | solution.py:210
  23.8 1.6 %collective-permute-start.8 = (f32[64,512]{1,0:T(8,128)S(1)}, f32[64,512]{1,0:T(8,128)S(1)}, u32[]{:S(2)}, u32[]{:S(2)}) collective-permute-start(f32[64,512]{1,0:T(8,128)S(1)} %pad_maximum_fusion), channel_id=1, source_target_pairs={{0,1},{1,0},{2,3},{3,2},{4,5},{5,4},{6,7},{7,6},{8,9},{9,8},{10,11... | collective-permute-start | bytes 393224 | tf_op jit(solution)/shard_map/ppermute | solution.py:210
  25.5 1.6 %collective-permute-start.2 = (f32[64,256]{1,0:T(8,128)S(1)}, f32[64,256]{1,0:T(8,128)S(1)}, u32[]{:S(2)}, u32[]{:S(2)}) collective-permute-start(f32[64,256]{1,0:T(8,128)S(1)} %constant_dynamic-slice_fusion.5), channel_id=1, source_target_pairs={{0,8},{4,12},{8,0},{12,4},{1,9},{5,13},{9,1},{13,5},{2,10},{6,14},... | collective-permute-start | bytes 196616 | tf_op jit(solution)/shard_map/ppermute | solution.py:210
  27.1 1.8 %collective-permute-done.8 = f32[64,512]{1,0:T(8,128)S(1)} collective-permute-done((f32[64,512]{1,0:T(8,128)S(1)}, f32[64,512]{1,0:T(8,128)S(1)}, u32[]{:S(2)}, u32[]{:S(2)}) %collective-permute-start.8) | collective-permute-done | bytes 131104 | tf_op jit(solution)/shard_map/ppermute | solution.py:210
  28.9 2.7 %collective-permute-start.9 = (f32[64,512]{1,0:T(8,128)S(1)}, f32[64,512]{1,0:T(8,128)S(1)}, u32[]{:S(2)}, u32[]{:S(2)}) collective-permute-start(f32[64,512]{1,0:T(8,128)S(1)} %fusion.30), channel_id=1, source_target_pairs={{0,2},{1,3},{2,0},{3,1},{4,6},{5,7},{6,4},{7,5},{8,10},{9,11},{10,... | collective-permute-start | bytes 393224 | tf_op jit(solution)/shard_map/ppermute | solution.py:210
  31.5 1.0 %collective-permute-start.4 = (f32[64,256]{1,0:T(8,128)S(1)}, f32[64,256]{1,0:T(8,128)S(1)}, u32[]{:S(2)}, u32[]{:S(2)}) collective-permute-start(f32[64,256]{1,0:T(8,128)S(1)} %dynamic-slice_add_fusion.5), channel_id=1, source_target_pairs={{0,2},{1,3},{2,0},{3,1},{4,6},{5,7},{6,4},{7,5},{8,10},{9,11},{10,... | collective-permute-start | bytes 196616 | tf_op jit(solution)/shard_map/ppermute | solution.py:210
  32.5 3.0 %collective-permute-start.5 = (f32[64,256]{1,0:T(8,128)S(1)}, f32[64,256]{1,0:T(8,128)S(1)}, u32[]{:S(2)}, u32[]{:S(2)}) collective-permute-start(f32[64,256]{1,0:T(8,128)S(1)} %dynamic-slice_add_fusion.5), channel_id=1, source_target_pairs={{0,3},{1,2},{2,1},{3,0},{4,7},{5,6},{6,5},{7,4},{8,11},{9,10},{10,... | collective-permute-start | bytes 196616 | tf_op jit(solution)/shard_map/ppermute | solution.py:210
  35.6 4.9 %collective-permute-done.9 = f32[64,512]{1,0:T(8,128)S(1)} collective-permute-done((f32[64,512]{1,0:T(8,128)S(1)}, f32[64,512]{1,0:T(8,128)S(1)}, u32[]{:S(2)}, u32[]{:S(2)}) %collective-permute-start.9) | collective-permute-done | bytes 131104 | tf_op jit(solution)/shard_map/ppermute | solution.py:210
  41.2 3.6 %collective-permute-done.10 = f32[64,256]{1,0:T(8,128)S(1)} collective-permute-done((f32[64,256]{1,0:T(8,128)S(1)}, f32[64,256]{1,0:T(8,128)S(1)}, u32[]{:S(2)}, u32[]{:S(2)}) %collective-permute-start.10) | collective-permute-done | bytes 65568 | tf_op jit(solution)/shard_map/ppermute | solution.py:210
  45.1 1.6 %collective-permute-start.11 = (bf16[64,256]{1,0:T(8,128)(2,1)S(1)}, bf16[64,256]{1,0:T(8,128)(2,1)S(1)}, u32[]{:S(2)}, u32[]{:S(2)}) collective-permute-start(bf16[64,256]{1,0:T(8,128)(2,1)S(1)} %fusion.17), channel_id=1, source_target_pairs={{0,8},{4,12},{8,0},{12,4},{1,9},{5,13},{9,1},{13,5},{2,10},{6,14},... | collective-permute-start | bytes 98312 | tf_op jit(solution)/shard_map/ppermute | solution.py:210
  46.7 2.4 %collective-permute-done.11 = bf16[64,256]{1,0:T(8,128)(2,1)S(1)} collective-permute-done((bf16[64,256]{1,0:T(8,128)(2,1)S(1)}, bf16[64,256]{1,0:T(8,128)(2,1)S(1)}, u32[]{:S(2)}, u32[]{:S(2)}) %collective-permute-start.11) | collective-permute-done | bytes 32800 | tf_op jit(solution)/shard_map/ppermute | solution.py:210
  49.3 1.1 %collective-permute-done.12 = bf16[128,256]{1,0:T(8,128)(2,1)S(1)} collective-permute-done((bf16[128,256]{1,0:T(8,128)(2,1)S(1)}, bf16[128,256]{1,0:T(8,128)(2,1)S(1)}, u32[]{:S(2)}, u32[]{:S(2)}) %collective-permute-start.12) | collective-permute-done | bytes 65568 | tf_op jit(solution)/shard_map/ppermute | solution.py:210
  50.4 5.5 %shard_map.87 = (f32[128,256]{1,0:T(8,128)S(1)}, bf16[256,256]{1,0:T(8,128)(2,1)}) custom-call(bf16[128,128,256]{2,1,0:T(8,128)(2,1)} %get-tuple-element.10.turned, bf16[256,256]{1,0:T(8,128)(2,1)S(1)} %maximum_select_fusion.4.first_turned, bf16[128,256]{1,0:T(8,128)(2,1)S(1)} %copy-done.3), custom_call_target="tpu_custom_call" | custom-call | flops 2147483648 | bytes 8388608 | tf_op jit(solution)/shard_map/pallas_call | solution.py:182
  56.5 2.5 %collective-permute-start.19 = (bf16[256,256]{1,0:T(8,128)(2,1)S(1)}, bf16[256,256]{1,0:T(8,128)(2,1)S(1)}, u32[]{:S(2)}, u32[]{:S(2)}) collective-permute-start(bf16[256,256]{1,0:T(8,128)(2,1)S(1)} %maximum_select_fusion.5), channel_id=1, source_target_pairs={{0,2},{1,3},{2,0},{3,1},{4,6},{5,7},{6,4},{7,5},{8,10},{9,11},{10,... | collective-permute-start | bytes 393224 | tf_op jit(solution)/shard_map/ppermute | solution.py:210
  59.0 1.5 %collective-permute-start.17 = (bf16[256,256]{1,0:T(8,128)(2,1)S(1)}, bf16[256,256]{1,0:T(8,128)(2,1)S(1)}, u32[]{:S(2)}, u32[]{:S(2)}) collective-permute-start(bf16[256,256]{1,0:T(8,128)(2,1)S(1)} %maximum_select_fusion.4.first_turned), channel_id=1, source_target_pairs={{0,16},{16,0},{1,17},{17,1},{2,18},{18,2},{3,19},{19,3},{4,20},{20... | collective-permute-start | bytes 393224 | tf_op jit(solution)/shard_map/ppermute | solution.py:210
  60.5 2.9 %collective-permute-start.15 = (f32[64,256]{1,0:T(8,128)S(1)}, f32[64,256]{1,0:T(8,128)S(1)}, u32[]{:S(2)}, u32[]{:S(2)}) collective-permute-start(f32[64,256]{1,0:T(8,128)S(1)} %dynamic-slice_add_fusion.4), channel_id=1, source_target_pairs={{0,2},{1,3},{2,0},{3,1},{4,6},{5,7},{6,4},{7,5},{8,10},{9,11},{10,... | collective-permute-start | bytes 196616 | tf_op jit(solution)/shard_map/ppermute | solution.py:210
  65.1 3.1 %collective-permute-done.19 = bf16[256,256]{1,0:T(8,128)(2,1)S(1)} collective-permute-done((bf16[256,256]{1,0:T(8,128)(2,1)S(1)}, bf16[256,256]{1,0:T(8,128)(2,1)S(1)}, u32[]{:S(2)}, u32[]{:S(2)}) %collective-permute-start.19) | collective-permute-done | bytes 131104 | tf_op jit(solution)/shard_map/ppermute | solution.py:210
  68.7 1.6 %collective-permute-done.15 = f32[64,256]{1,0:T(8,128)S(1)} collective-permute-done((f32[64,256]{1,0:T(8,128)S(1)}, f32[64,256]{1,0:T(8,128)S(1)}, u32[]{:S(2)}, u32[]{:S(2)}) %collective-permute-start.15) | collective-permute-done | bytes 65568 | tf_op jit(solution)/shard_map/ppermute | solution.py:210
  70.5 1.7 %collective-permute-start.20 = (bf16[64,256]{1,0:T(8,128)(2,1)S(1)}, bf16[64,256]{1,0:T(8,128)(2,1)S(1)}, u32[]{:S(2)}, u32[]{:S(2)}) collective-permute-start(bf16[64,256]{1,0:T(8,128)(2,1)S(1)} %divide_convert_fusion.1), channel_id=1, source_target_pairs={{0,16},{16,0},{1,17},{17,1},{2,18},{18,2},{3,19},{19,3},{4,20},{20... | collective-permute-start | bytes 98312 | tf_op jit(solution)/shard_map/ppermute | solution.py:210
  72.2 2.3 %collective-permute-done.20 = bf16[64,256]{1,0:T(8,128)(2,1)S(1)} collective-permute-done((bf16[64,256]{1,0:T(8,128)(2,1)S(1)}, bf16[64,256]{1,0:T(8,128)(2,1)S(1)}, u32[]{:S(2)}, u32[]{:S(2)}) %collective-permute-start.20) | collective-permute-done | bytes 32800 | tf_op jit(solution)/shard_map/ppermute | solution.py:210
  74.5 1.7 %collective-permute-start.24 = (bf16[128,256]{1,0:T(8,128)(2,1)S(1)}, bf16[128,256]{1,0:T(8,128)(2,1)S(1)}, u32[]{:S(2)}, u32[]{:S(2)}) collective-permute-start(bf16[128,256]{1,0:T(8,128)(2,1)S(1)} %maximum_select_fusion.8.second), channel_id=1, source_target_pairs={{0,8},{4,12},{8,0},{12,4},{1,9},{5,13},{9,1},{13,5},{2,10},{6,14},... | collective-permute-start | bytes 196616 | tf_op jit(solution)/shard_map/ppermute | solution.py:210
  76.2 0.9 copy-done.10
  77.1 5.0 %shard_map.88 = f32[128,256]{1,0:T(8,128)S(1)} custom-call(bf16[128,128,256]{2,1,0:T(8,128)(2,1)} %get-tuple-element.10.turned, bf16[256,256]{1,0:T(8,128)(2,1)S(1)} %copy-done.10, bf16[128,256]{1,0:T(8,128)(2,1)S(1)} %maximum_select_fusion.8.second), custom_call_target="tpu_custom_call" | custom-call | flops 2147483648 | bytes 8388608 | tf_op jit(solution)/shard_map/pallas_call | solution.py:182
  83.9 3.9 %collective-permute-done.22 = f32[64,256]{1,0:T(8,128)S(1)} collective-permute-done((f32[64,256]{1,0:T(8,128)S(1)}, f32[64,256]{1,0:T(8,128)S(1)}, u32[]{:S(2)}, u32[]{:S(2)}) %collective-permute-start.22) | collective-permute-done | bytes 65568 | tf_op jit(solution)/shard_map/ppermute | solution.py:210
  87.8 1.6 %collective-permute-start.23 = (f32[64,256]{1,0:T(8,128)S(1)}, f32[64,256]{1,0:T(8,128)S(1)}, u32[]{:S(2)}, u32[]{:S(2)}) collective-permute-start(f32[64,256]{1,0:T(8,128)S(1)} %add.153), channel_id=1, source_target_pairs={{0,16},{16,0},{1,17},{17,1},{2,18},{18,2},{3,19},{19,3},{4,20},{20... | collective-permute-start | bytes 196616 | tf_op jit(solution)/shard_map/ppermute | solution.py:210
  89.9 2.2 %collective-permute-done.23 = f32[64,256]{1,0:T(8,128)S(1)} collective-permute-done((f32[64,256]{1,0:T(8,128)S(1)}, f32[64,256]{1,0:T(8,128)S(1)}, u32[]{:S(2)}, u32[]{:S(2)}) %collective-permute-start.23) | collective-permute-done | bytes 65568 | tf_op jit(solution)/shard_map/ppermute | solution.py:210
  92.2 1.2 %collective-permute-done.26 = bf16[64,256]{1,0:T(8,128)(2,1)S(1)} collective-permute-done((bf16[64,256]{1,0:T(8,128)(2,1)S(1)}, bf16[64,256]{1,0:T(8,128)(2,1)S(1)}, u32[]{:S(2)}, u32[]{:S(2)}) %collective-permute-start.26) | collective-permute-done | bytes 32800 | tf_op jit(solution)/shard_map/ppermute | solution.py:210
  (86 shorter events, 12.2 us)
Async XLA Ops:
  0.6 40.3 %copy-start = (bf16[256,256]{1,0:T(8,128)(2,1)S(1)}, bf16[256,256]{1,0:T(8,128)(2,1)}, u32[]{:S(2)}) copy-start(bf16[256,256]{1,0:T(8,128)(2,1)} %param.8) | copy-start | bytes 393220
  1.5 1.2 %copy-start.4 = (bf16[512,1024]{1,0:T(8,128)(2,1)S(1)}, bf16[512,1024]{1,0:T(8,128)(2,1)}, u32[]{:S(2)}) copy-start(bf16[512,1024]{1,0:T(8,128)(2,1)} %matrix.1) | copy-start | bytes 3145732
  4.6 44.5 %copy-start.3 = (bf16[128,256]{1,0:T(8,128)(2,1)S(1)}, bf16[128,256]{1,0:T(8,128)(2,1)}, u32[]{:S(2)}) copy-start(bf16[128,256]{1,0:T(8,128)(2,1)} %time.5) | copy-start | bytes 196612
  5.4 12.7 %collective-permute-start.6 = (f32[128,512]{1,0:T(8,128)S(1)}, f32[128,512]{1,0:T(8,128)S(1)}, u32[]{:S(2)}, u32[]{:S(2)}) collective-permute-start(f32[128,512]{1,0:T(8,128)S(1)} %constant_dynamic-slice_fusion.4), channel_id=1, source_target_pairs={{0,4},{4,0},{8,12},{12,8},{1,5},{5,1},{9,13},{13,9},{2,6},{6,2},{1... | collective-permute-start | bytes 786440 | tf_op jit(solution)/shard_map/ppermute | solution.py:210
  5.9 13.7 %collective-permute-start = (f32[256,256]{1,0:T(8,128)S(1)}, f32[256,256]{1,0:T(8,128)S(1)}, u32[]{:S(2)}, u32[]{:S(2)}) collective-permute-start(f32[256,256]{1,0:T(8,128)S(1)} %constant_dynamic-slice_fusion.7), channel_id=1, source_target_pairs={{0,16},{16,0},{1,17},{17,1},{2,18},{18,2},{3,19},{19,3},{4,20},{20... | collective-permute-start | bytes 786440 | tf_op jit(solution)/shard_map/ppermute | solution.py:210
  18.1 5.7 %collective-permute-start.7 = (f32[64,512]{1,0:T(8,128)S(1)}, f32[64,512]{1,0:T(8,128)S(1)}, u32[]{:S(2)}, u32[]{:S(2)}) collective-permute-start(f32[64,512]{1,0:T(8,128)S(1)} %constant_dynamic-slice_fusion.3), channel_id=1, source_target_pairs={{0,8},{4,12},{8,0},{12,4},{1,9},{5,13},{9,1},{13,5},{2,10},{6,14},... | collective-permute-start | bytes 393224 | tf_op jit(solution)/shard_map/ppermute | solution.py:210
  19.7 48.8 %copy-start.8 = (bf16[128,256]{1,0:T(8,128)(2,1)S(1)}, bf16[128,256]{1,0:T(8,128)(2,1)}, u32[]{:S(2)}) copy-start(bf16[128,256]{1,0:T(8,128)(2,1)} %second.3) | copy-start | bytes 196612
  19.8 5.7 %collective-permute-start.1 = (f32[128,256]{1,0:T(8,128)S(1)}, f32[128,256]{1,0:T(8,128)S(1)}, u32[]{:S(2)}, u32[]{:S(2)}) collective-permute-start(f32[128,256]{1,0:T(8,128)S(1)} %constant_dynamic-slice_fusion.6), channel_id=1, source_target_pairs={{0,4},{4,0},{8,12},{12,8},{1,5},{5,1},{9,13},{13,9},{2,6},{6,2},{1... | collective-permute-start | bytes 393224 | tf_op jit(solution)/shard_map/ppermute | solution.py:210
  23.8 5.0 %collective-permute-start.8 = (f32[64,512]{1,0:T(8,128)S(1)}, f32[64,512]{1,0:T(8,128)S(1)}, u32[]{:S(2)}, u32[]{:S(2)}) collective-permute-start(f32[64,512]{1,0:T(8,128)S(1)} %pad_maximum_fusion), channel_id=1, source_target_pairs={{0,1},{1,0},{2,3},{3,2},{4,5},{5,4},{6,7},{7,6},{8,9},{9,8},{10,11... | collective-permute-start | bytes 393224 | tf_op jit(solution)/shard_map/ppermute | solution.py:210
  25.5 6.0 %collective-permute-start.2 = (f32[64,256]{1,0:T(8,128)S(1)}, f32[64,256]{1,0:T(8,128)S(1)}, u32[]{:S(2)}, u32[]{:S(2)}) collective-permute-start(f32[64,256]{1,0:T(8,128)S(1)} %constant_dynamic-slice_fusion.5), channel_id=1, source_target_pairs={{0,8},{4,12},{8,0},{12,4},{1,9},{5,13},{9,1},{13,5},{2,10},{6,14},... | collective-permute-start | bytes 196616 | tf_op jit(solution)/shard_map/ppermute | solution.py:210
  28.9 11.5 %collective-permute-start.9 = (f32[64,512]{1,0:T(8,128)S(1)}, f32[64,512]{1,0:T(8,128)S(1)}, u32[]{:S(2)}, u32[]{:S(2)}) collective-permute-start(f32[64,512]{1,0:T(8,128)S(1)} %fusion.30), channel_id=1, source_target_pairs={{0,2},{1,3},{2,0},{3,1},{4,6},{5,7},{6,4},{7,5},{8,10},{9,11},{10,... | collective-permute-start | bytes 393224 | tf_op jit(solution)/shard_map/ppermute | solution.py:210
  31.5 9.6 %collective-permute-start.4 = (f32[64,256]{1,0:T(8,128)S(1)}, f32[64,256]{1,0:T(8,128)S(1)}, u32[]{:S(2)}, u32[]{:S(2)}) collective-permute-start(f32[64,256]{1,0:T(8,128)S(1)} %dynamic-slice_add_fusion.5), channel_id=1, source_target_pairs={{0,2},{1,3},{2,0},{3,1},{4,6},{5,7},{6,4},{7,5},{8,10},{9,11},{10,... | collective-permute-start | bytes 196616 | tf_op jit(solution)/shard_map/ppermute | solution.py:210
  32.5 8.7 %collective-permute-start.5 = (f32[64,256]{1,0:T(8,128)S(1)}, f32[64,256]{1,0:T(8,128)S(1)}, u32[]{:S(2)}, u32[]{:S(2)}) collective-permute-start(f32[64,256]{1,0:T(8,128)S(1)} %dynamic-slice_add_fusion.5), channel_id=1, source_target_pairs={{0,3},{1,2},{2,1},{3,0},{4,7},{5,6},{6,5},{7,4},{8,11},{9,10},{10,... | collective-permute-start | bytes 196616 | tf_op jit(solution)/shard_map/ppermute | solution.py:210
  35.6 5.6 %collective-permute-start.3 = (f32[64,256]{1,0:T(8,128)S(1)}, f32[64,256]{1,0:T(8,128)S(1)}, u32[]{:S(2)}, u32[]{:S(2)}) collective-permute-start(f32[64,256]{1,0:T(8,128)S(1)} %dynamic-slice_add_fusion.5), channel_id=1, source_target_pairs={{0,1},{1,0},{2,3},{3,2},{4,5},{5,4},{6,7},{7,6},{8,9},{9,8},{10,11... | collective-permute-start | bytes 196616 | tf_op jit(solution)/shard_map/ppermute | solution.py:210
  40.5 4.3 %collective-permute-start.10 = (f32[64,256]{1,0:T(8,128)S(1)}, f32[64,256]{1,0:T(8,128)S(1)}, u32[]{:S(2)}, u32[]{:S(2)}) collective-permute-start(f32[64,256]{1,0:T(8,128)S(1)} %slice.19), channel_id=1, source_target_pairs={{0,16},{16,0},{1,17},{17,1},{2,18},{18,2},{3,19},{19,3},{4,20},{20... | collective-permute-start | bytes 196616 | tf_op jit(solution)/shard_map/ppermute | solution.py:210
  45.1 4.0 %collective-permute-start.11 = (bf16[64,256]{1,0:T(8,128)(2,1)S(1)}, bf16[64,256]{1,0:T(8,128)(2,1)S(1)}, u32[]{:S(2)}, u32[]{:S(2)}) collective-permute-start(bf16[64,256]{1,0:T(8,128)(2,1)S(1)} %fusion.17), channel_id=1, source_target_pairs={{0,8},{4,12},{8,0},{12,4},{1,9},{5,13},{9,1},{13,5},{2,10},{6,14},... | collective-permute-start | bytes 98312 | tf_op jit(solution)/shard_map/ppermute | solution.py:210
  49.1 1.3 %collective-permute-start.12 = (bf16[128,256]{1,0:T(8,128)(2,1)S(1)}, bf16[128,256]{1,0:T(8,128)(2,1)S(1)}, u32[]{:S(2)}, u32[]{:S(2)}) collective-permute-start(bf16[128,256]{1,0:T(8,128)(2,1)S(1)} %maximum_select_fusion.7), channel_id=1, source_target_pairs={{0,4},{4,0},{8,12},{12,8},{1,5},{5,1},{9,13},{13,9},{2,6},{6,2},{1... | collective-permute-start | bytes 196616 | tf_op jit(solution)/shard_map/ppermute | solution.py:210
  49.2 7.3 %collective-permute-start.18 = (bf16[128,256]{1,0:T(8,128)(2,1)S(1)}, bf16[128,256]{1,0:T(8,128)(2,1)S(1)}, u32[]{:S(2)}, u32[]{:S(2)}) collective-permute-start(bf16[128,256]{1,0:T(8,128)(2,1)S(1)} %copy-done.3), channel_id=1, source_target_pairs={{0,1},{1,0},{2,3},{3,2},{4,5},{5,4},{6,7},{7,6},{8,9},{9,8},{10,11... | collective-permute-start | bytes 196616 | tf_op jit(solution)/shard_map/ppermute | solution.py:210
  56.0 4.5 %collective-permute-start.13 = (f32[64,256]{1,0:T(8,128)S(1)}, f32[64,256]{1,0:T(8,128)S(1)}, u32[]{:S(2)}, u32[]{:S(2)}) collective-permute-start(f32[64,256]{1,0:T(8,128)S(1)} %constant_dynamic-slice_fusion.1), channel_id=1, source_target_pairs={{0,16},{16,0},{1,17},{17,1},{2,18},{18,2},{3,19},{19,3},{4,20},{20... | collective-permute-start | bytes 196616 | tf_op jit(solution)/shard_map/ppermute | solution.py:210
  56.5 11.7 %collective-permute-start.19 = (bf16[256,256]{1,0:T(8,128)(2,1)S(1)}, bf16[256,256]{1,0:T(8,128)(2,1)S(1)}, u32[]{:S(2)}, u32[]{:S(2)}) collective-permute-start(bf16[256,256]{1,0:T(8,128)(2,1)S(1)} %maximum_select_fusion.5), channel_id=1, source_target_pairs={{0,2},{1,3},{2,0},{3,1},{4,6},{5,7},{6,4},{7,5},{8,10},{9,11},{10,... | collective-permute-start | bytes 393224 | tf_op jit(solution)/shard_map/ppermute | solution.py:210
  59.0 5.6 %collective-permute-start.17 = (bf16[256,256]{1,0:T(8,128)(2,1)S(1)}, bf16[256,256]{1,0:T(8,128)(2,1)S(1)}, u32[]{:S(2)}, u32[]{:S(2)}) collective-permute-start(bf16[256,256]{1,0:T(8,128)(2,1)S(1)} %maximum_select_fusion.4.first_turned), channel_id=1, source_target_pairs={{0,16},{16,0},{1,17},{17,1},{2,18},{18,2},{3,19},{19,3},{4,20},{20... | collective-permute-start | bytes 393224 | tf_op jit(solution)/shard_map/ppermute | solution.py:210
  60.5 9.8 %collective-permute-start.15 = (f32[64,256]{1,0:T(8,128)S(1)}, f32[64,256]{1,0:T(8,128)S(1)}, u32[]{:S(2)}, u32[]{:S(2)}) collective-permute-start(f32[64,256]{1,0:T(8,128)S(1)} %dynamic-slice_add_fusion.4), channel_id=1, source_target_pairs={{0,2},{1,3},{2,0},{3,1},{4,6},{5,7},{6,4},{7,5},{8,10},{9,11},{10,... | collective-permute-start | bytes 196616 | tf_op jit(solution)/shard_map/ppermute | solution.py:210
  63.4 6.9 %collective-permute-start.16 = (f32[64,256]{1,0:T(8,128)S(1)}, f32[64,256]{1,0:T(8,128)S(1)}, u32[]{:S(2)}, u32[]{:S(2)}) collective-permute-start(f32[64,256]{1,0:T(8,128)S(1)} %dynamic-slice_add_fusion.4), channel_id=1, source_target_pairs={{0,3},{1,2},{2,1},{3,0},{4,7},{5,6},{6,5},{7,4},{8,11},{9,10},{10,... | collective-permute-start | bytes 196616 | tf_op jit(solution)/shard_map/ppermute | solution.py:210
  64.1 6.3 %collective-permute-start.14 = (f32[64,256]{1,0:T(8,128)S(1)}, f32[64,256]{1,0:T(8,128)S(1)}, u32[]{:S(2)}, u32[]{:S(2)}) collective-permute-start(f32[64,256]{1,0:T(8,128)S(1)} %dynamic-slice_add_fusion.4), channel_id=1, source_target_pairs={{0,1},{1,0},{2,3},{3,2},{4,5},{5,4},{6,7},{7,6},{8,9},{9,8},{10,11... | collective-permute-start | bytes 196616 | tf_op jit(solution)/shard_map/ppermute | solution.py:210
  70.5 4.0 %collective-permute-start.20 = (bf16[64,256]{1,0:T(8,128)(2,1)S(1)}, bf16[64,256]{1,0:T(8,128)(2,1)S(1)}, u32[]{:S(2)}, u32[]{:S(2)}) collective-permute-start(bf16[64,256]{1,0:T(8,128)(2,1)S(1)} %divide_convert_fusion.1), channel_id=1, source_target_pairs={{0,16},{16,0},{1,17},{17,1},{2,18},{18,2},{3,19},{19,3},{4,20},{20... | collective-permute-start | bytes 98312 | tf_op jit(solution)/shard_map/ppermute | solution.py:210
  74.5 19.6 %copy-start.5 = (bf16[128,256]{1,0:T(8,128)(2,1)}, bf16[128,256]{1,0:T(8,128)(2,1)S(1)}, u32[]{:S(2)}) copy-start(bf16[128,256]{1,0:T(8,128)(2,1)S(1)} %maximum_select_fusion.8.second) | copy-start | bytes 196612
  74.5 7.7 %collective-permute-start.24 = (bf16[128,256]{1,0:T(8,128)(2,1)S(1)}, bf16[128,256]{1,0:T(8,128)(2,1)S(1)}, u32[]{:S(2)}, u32[]{:S(2)}) collective-permute-start(bf16[128,256]{1,0:T(8,128)(2,1)S(1)} %maximum_select_fusion.8.second), channel_id=1, source_target_pairs={{0,8},{4,12},{8,0},{12,4},{1,9},{5,13},{9,1},{13,5},{2,10},{6,14},... | collective-permute-start | bytes 196616 | tf_op jit(solution)/shard_map/ppermute | solution.py:210
  82.1 1.3 %collective-permute-start.21 = (f32[64,256]{1,0:T(8,128)S(1)}, f32[64,256]{1,0:T(8,128)S(1)}, u32[]{:S(2)}, u32[]{:S(2)}) collective-permute-start(f32[64,256]{1,0:T(8,128)S(1)} %constant_dynamic-slice_fusion), channel_id=1, source_target_pairs={{0,4},{4,0},{8,12},{12,8},{1,5},{5,1},{9,13},{13,9},{2,6},{6,2},{1... | collective-permute-start | bytes 196616 | tf_op jit(solution)/shard_map/ppermute | solution.py:210
  82.2 7.1 %collective-permute-start.25 = (bf16[256,256]{1,0:T(8,128)(2,1)S(1)}, bf16[256,256]{1,0:T(8,128)(2,1)S(1)}, u32[]{:S(2)}, u32[]{:S(2)}) collective-permute-start(bf16[256,256]{1,0:T(8,128)(2,1)S(1)} %maximum_select_fusion.6), channel_id=1, source_target_pairs={{0,4},{4,0},{8,12},{12,8},{1,5},{5,1},{9,13},{13,9},{2,6},{6,2},{1... | collective-permute-start | bytes 393224 | tf_op jit(solution)/shard_map/ppermute | solution.py:210
  83.4 4.3 %collective-permute-start.22 = (f32[64,256]{1,0:T(8,128)S(1)}, f32[64,256]{1,0:T(8,128)S(1)}, u32[]{:S(2)}, u32[]{:S(2)}) collective-permute-start(f32[64,256]{1,0:T(8,128)S(1)} %dynamic-slice_add_fusion.3), channel_id=1, source_target_pairs={{0,8},{4,12},{8,0},{12,4},{1,9},{5,13},{9,1},{13,5},{2,10},{6,14},... | collective-permute-start | bytes 196616 | tf_op jit(solution)/shard_map/ppermute | solution.py:210
  87.8 4.3 %collective-permute-start.23 = (f32[64,256]{1,0:T(8,128)S(1)}, f32[64,256]{1,0:T(8,128)S(1)}, u32[]{:S(2)}, u32[]{:S(2)}) collective-permute-start(f32[64,256]{1,0:T(8,128)S(1)} %add.153), channel_id=1, source_target_pairs={{0,16},{16,0},{1,17},{17,1},{2,18},{18,2},{3,19},{19,3},{4,20},{20... | collective-permute-start | bytes 196616 | tf_op jit(solution)/shard_map/ppermute | solution.py:210
  92.2 1.3 %collective-permute-start.26 = (bf16[64,256]{1,0:T(8,128)(2,1)S(1)}, bf16[64,256]{1,0:T(8,128)(2,1)S(1)}, u32[]{:S(2)}, u32[]{:S(2)}) collective-permute-start(bf16[64,256]{1,0:T(8,128)(2,1)S(1)} %divide_convert_fusion), channel_id=1, source_target_pairs={{0,4},{4,0},{8,12},{12,8},{1,5},{5,1},{9,13},{13,9},{2,6},{6,2},{1... | collective-permute-start | bytes 98312 | tf_op jit(solution)/shard_map/ppermute | solution.py:210
  (6 other events, 5.3 us)
where the time goes:
time: 94.4 us; the launch traced here: 94.1 us
  waiting for transfers between devices  32.8 us (35%)
  starting transfers between devices  31.6 us (33%)
  Pallas kernels  19 us (20%)
  local copies, waits for them, and re-layouts  6.9 us (7%)
  matrix products  1.75 us (2%)
  other arithmetic  1.03 us (1%)
  between operations  1 us (1%)
    ppermute x27, waiting for transfers between devices, swap(): return lax.ppermute(values, axis, [(i, i ^ mask) for i in range(size)])  32.8 us
    ppermute x27, starting transfers between devices, swap(): return lax.ppermute(values, axis, [(i, i ^ mask) for i in range(size)])  31.6 us
    pallas_call x2, Pallas kernels, weighted_call(): kernel_call(functools.partial(kernel, chunk), 2 * tile_i * tile_j * tile_...  10.5 us
    pallas_call x1, Pallas kernels, slab_and_turn(): kernel_call(functools.partial(slab_kernel, chunk, steps), 2 * tile_i * ti...  7.81 us
    unnamed x23, local copies, waits for them, and re-layouts  6.67 us
  transfers between devices with their start and end apart: 27, of which 15 were waited for; matrix products, arithmetic and copies ran while one was open for 2% of the time, Pallas kernels for 19%

commit v1 on v0

--- a/solution.py
+++ b/solution.py
@@ -33,16 +33,32 @@
     )
 
 
-def local_kernel(matrix, column, second, time, coupled, grams, gram_time):
+def bring(sources, targets, sem):
+    def copy(index):
+        return pltpu.make_async_copy(sources[index], targets[index], sem.at[index])
+
+    for index in range(len(sources)):
+        copy(index).start()
+    return lambda index: copy(index).wait()
+
+
+def local_kernel(matrix, column, second, time, coupled, grams, gram_time, *scratch):
     f32 = jnp.float32
+    *held, sem = scratch
+    wait = bring((column, second, time, matrix), held, sem)
     rank = column.shape[1]
-    turned = column[...].T
-    grams[:, :rank] = jnp.dot(turned, column[...], preferred_element_type=f32)
+    held_column, held_second, held_time, held_matrix = held
+    wait(0)
+    turned = held_column[...].T
+    grams[:, :rank] = jnp.dot(turned, held_column[...], preferred_element_type=f32)
+    wait(1)
+    grams[:, rank:] = jnp.dot(held_second[...].T, held_second[...], preferred_element_type=f32)
+    wait(2)
+    gram_time[...] = jnp.dot(held_time[...].T, held_time[...], preferred_element_type=f32)
+    wait(3)
     coupled[...] = lax.dot_general(
-        turned, matrix[...], (((1,), (1,)), ((), ())), preferred_element_type=f32
-    )
-    grams[:, rank:] = jnp.dot(second[...].T, second[...], preferred_element_type=f32)
-    gram_time[...] = jnp.dot(time[...].T, time[...], preferred_element_type=f32)
+        turned, held_matrix[...], (((1,), (1,)), ((), ())), preferred_element_type=f32
+    )
 
 
 def local_products(matrix, column, second, time):
@@ -58,12 +74,19 @@
             jax.ShapeDtypeStruct((rank, 2 * rank), f32),
             jax.ShapeDtypeStruct((rank, rank), f32),
         ),
-        in_specs=[VMEM] * 4,
+        in_specs=[ANY] * 4,
         out_specs=(VMEM,) * 3,
-    )(matrix, column, second, time)
-
-
-def slab_kernel(chunk, steps, tensor, second, time, total, turned, read, read_sem, ready, ready_sem, added):
+        scratch_shapes=[
+            *(pltpu.VMEM(a.shape, a.dtype) for a in (column, second, time, matrix)),
+            pltpu.SemaphoreType.DMA((4,)),
+        ],
+    )(*(in_hbm(a) for a in (matrix, column, second, time)))
+
+
+def slab_kernel(chunk, steps, tensor, second_in, time_in, total, turned, *scratch):
+    read, read_sem, ready, ready_sem, added, second, time, sem = scratch
+    wait = bring((second_in, time_in), (second, time), sem)
+
     def fetch(step):
         source = tensor.at[:, pl.ds(step * chunk, chunk)]
         return pltpu.make_async_copy(source, read.at[step], read_sem.at[step])
@@ -74,6 +97,8 @@
 
     for step in range(steps):
         fetch(step).start()
+    wait(0)
+    wait(1)
     time_wide = time[...].astype(jnp.float32)
     added[...] = jnp.zeros_like(added)
 
@@ -115,7 +140,7 @@
             jax.ShapeDtypeStruct((rank, tile_i), jnp.float32),
             pltpu.HBM((tile_j, tile_k, tile_i), tensor.dtype),
         ),
-        in_specs=[ANY, VMEM, VMEM],
+        in_specs=[ANY] * 3,
         out_specs=(VMEM, ANY),
         scratch_shapes=[
             pltpu.VMEM((steps, tile_i, chunk, tile_k), tensor.dtype),
@@ -123,8 +148,11 @@
             pltpu.VMEM((steps, chunk, tile_k, tile_i), tensor.dtype),
             pltpu.SemaphoreType.DMA((steps,)),
             pltpu.VMEM((tile_i, rank), jnp.float32),
+            pltpu.VMEM(second.shape, second.dtype),
+            pltpu.VMEM(time.shape, time.dtype),
+            pltpu.SemaphoreType.DMA((2,)),
         ],
-    )(in_hbm(tensor), second, time)
+    )(in_hbm(tensor), in_hbm(second), in_hbm(time))
 
 
 def fetcher(turned, read, read_sem, chunk):
@@ -156,10 +184,12 @@
     lax.fori_loop(0, read.shape[0], body, 0)
 
 
-def time_kernel(chunk, turned, first, second, total, read, read_sem, wide):
+def time_kernel(chunk, turned, first_in, second, total, read, read_sem, wide, first, sem):
+    wait = bring((first_in,), (first,), sem)
     fetch = fetcher(turned, read, read_sem, chunk)
     wide[...] = second[...].astype(jnp.float32)
     total[...] = jnp.zeros_like(total)
+    wait(0)
     shared = first[...]
 
     def body(step, carry):
@@ -174,7 +204,7 @@
     lax.fori_loop(0, read.shape[0], body, 0)
 
 
-def weighted_call(kernel, turned, args, outs, extra=()):
+def weighted_call(kernel, turned, args, specs, outs, extra=()):
     tile_j, tile_k, tile_i = turned.shape
     chunk = chunk_of(tile_j, 16)
     steps = tile_j // chunk
@@ -184,7 +214,7 @@
         2 * tile_i * tile_j * tile_k * rank,
         2 * tile_i * tile_j * tile_k,
         out_shape=outs,
-        in_specs=[ANY] + [VMEM] * len(args),
+        in_specs=[ANY, *specs],
         out_specs=(VMEM,) * len(outs),
         scratch_shapes=[
             pltpu.VMEM((steps, chunk, tile_k, tile_i), turned.dtype),
@@ -218,14 +248,15 @@
     return kept + swap(sent, axis, size, mask)
 
 
-def double(values, axis, size, mask):
-    other = swap(values, axis, size, mask)
+def in_order(own, other, axis, mask):
     bit = (lax.axis_index(axis) & mask) // mask
     return jnp.where(
-        bit == 0,
-        jnp.concatenate([values, other], 0),
-        jnp.concatenate([other, values], 0),
-    )
+        bit == 0, jnp.concatenate([own, other], 0), jnp.concatenate([other, own], 0)
+    )
+
+
+def double(values, axis, size, mask):
+    return in_order(values, swap(values, axis, size, mask), axis, mask)
 
 
 def tree_sum(terms):
@@ -270,8 +301,18 @@
     gram_second = grams[:, rank:]
     time_rows = lax.dynamic_slice_in_dim(gram_time, part * share, share, 0)
     grams = jnp.concatenate([grams[:, :rank], time_rows], 1)
+    times = time_factor
     for mask in masks_of(size_k):
-        grams = grams + swap(grams, "ka", size_k, mask)
+        if mask == 1:
+            wide = jnp.concatenate([times[: tile_k // 2], times[tile_k // 2 :]], 1)
+            sent = jnp.concatenate([grams, wide.astype(f32)], 0)
+            came = swap(sent, "ka", size_k, mask)
+            grams = grams + came[:share]
+            other = came[share:].astype(jnp.bfloat16)
+            other = jnp.concatenate([other[:, :rank], other[:, rank:]], 0)
+            times = in_order(times, other, "ka", mask)
+        else:
+            grams = grams + swap(grams, "ka", size_k, mask)
     gram_column, time_rows = grams[:, :rank], grams[:, rank:]
     gram_column = all_sum(gram_column, "ia", size_i)
     gram_total = gram_second * time_rows + gram_column
@@ -292,14 +333,14 @@
 
     firsts = spread(first_new, "ia", size_i)
     gram_first = tree_sum([row_product(piece) for piece in firsts])
-    times = time_factor
-    for mask in masks_of(size_k):
+    for mask in masks_of(size_k)[1:]:
         times = double(times, "ka", size_k, mask)
     gram_time = cross_product(times)
     plane_sum, first_out = weighted_call(
         plane_kernel,
         turned,
         (first_new, time_factor),
+        (VMEM, VMEM),
         (
             jax.ShapeDtypeStruct((tile_j, rank), f32),
             jax.ShapeDtypeStruct((tile_i, rank), jnp.bfloat16),
@@ -322,13 +363,17 @@
     (time_sum,) = weighted_call(
         time_kernel,
         turned,
-        (first_out, second_new),
+        (in_hbm(first_out), second_new),
+        (ANY, VMEM),
         (jax.ShapeDtypeStruct((tile_k, rank), f32),),
-        (pltpu.VMEM((tile_j, rank), f32),),
+        (
+            pltpu.VMEM((tile_j, rank), f32),
+            pltpu.VMEM((tile_i, rank), jnp.bfloat16),
+            pltpu.SemaphoreType.DMA((1,)),
+        ),
     )
     time_sum = halve(time_sum, "ja", size_j, 1)
-    time_sum = all_sum(time_sum, "ja", size_j, 2)
-    time_sum = all_sum(time_sum, "ia", size_i)
+    time_sum = all_sum(time_sum, ("ia", "ja"), size_i * size_j, 2)
     rows = tile_k // 2
     own = lax.dynamic_slice_in_dim(
         time_factor, (lax.axis_index("ja") % 2) * rows, rows, 0

time: 94.4 us -> 95.3 us (level)
  local copies, waits for them, and re-layouts: 6.9 us -> 1.14 us
  Pallas kernels: 19 us -> 24.6 us
  waiting for transfers between devices: 32.8 us -> 34.1 us
    unnamed x23 -> x9, local copies, waits for them, and re-layouts: 6.67 us -> 0.12 us
    pallas_call x1, Pallas kernels: 7.81 us -> 9.78 us  [slab_and_turn(): kernel_call(functools.partial(slab_kernel, chunk, steps), 2 * tile_i * ti...]
    pallas_call x2, Pallas kernels: 10.5 us -> 12.4 us  [weighted_call(): kernel_call(functools.partial(kernel, chunk), 2 * tile_i * tile_j * tile_...]
    pallas_call x1, Pallas kernels: 0.68 us -> 2.44 us  [local_products(): kernel_call(local_kernel, 2 * width * rank * (rows + rank), 2 * width * (...]
    ppermute x27, waiting for transfers between devices: 32.8 us -> 34.1 us  [swap(): return lax.ppermute(values, axis, [(i, i ^ mask) for i in range(size)])]
  transfers between devices with their start and end apart: 27 -> 27, of which waited for: 15 -> 16; matrix products, arithmetic and copies ran while one was open for 2% -> 3% of each run, Pallas kernels for 19% -> 17%
where the time goes in v1:
time: 95.3 us; the launch traced here: 95.1 us
  waiting for transfers between devices  34.1 us (36%)
  starting transfers between devices  31.4 us (33%)
  Pallas kernels  24.6 us (26%)
  matrix products  1.74 us (2%)
  local copies, waits for them, and re-layouts  1.14 us (1%)
  other arithmetic  1.08 us (1%)
  between operations  1.04 us (1%)
    ppermute x27, waiting for transfers between devices, swap(): return lax.ppermute(values, axis, [(i, i ^ mask) for i in range(size)])  34.1 us
    ppermute x27, starting transfers between devices, swap(): return lax.ppermute(values, axis, [(i, i ^ mask) for i in range(size)])  31.4 us
    pallas_call x2, Pallas kernels, weighted_call(): kernel_call(functools.partial(kernel, chunk), 2 * tile_i * tile_j * tile_...  12.4 us
    pallas_call x1, Pallas kernels, slab_and_turn(): kernel_call(functools.partial(slab_kernel, chunk, steps), 2 * tile_i * ti...  9.78 us
    pallas_call x1, Pallas kernels, local_products(): kernel_call(local_kernel, 2 * width * rank * (rows + rank), 2 * width * (...  2.44 us
  transfers between devices with their start and end apart: 27, of which 16 were waited for; matrix products, arithmetic and copies ran while one was open for 3% of the time, Pallas kernels for 17%

profile of v1, /device:TPU:0, one launch (start us, length us, event | category | flops | bytes accessed | tf_op | source)
XLA Modules:
  0.0 95.1 jit_solution(126739079573767095)
XLA Ops:
  0.7 2.4 %shard_map.86 = (f32[256,512]{1,0:T(8,128)S(1)}, f32[256,512]{1,0:T(8,128)S(1)}, f32[256,256]{1,0:T(8,128)S(1)}) custom-call(bf16[512,1024]{1,0:T(8,128)(2,1)} %matrix.1, bf16[1024,256]{1,0:T(8,128)(2,1)} %column.1, bf16[128,256]{1,0:T(8,128)(2,1)} %second.1, bf16[128,256]{1,0:T(8,128)(2,1)} %time.3), custom_call_target="tpu_custom_call" | custom-call | flops 402653184 | bytes 1572864 | tf_op jit(solution)/shard_map/pallas_call | solution.py:68
  3.7 2.6 %collective-permute-start = (f32[256,256]{1,0:T(8,128)S(1)}, f32[256,256]{1,0:T(8,128)S(1)}, u32[]{:S(2)}, u32[]{:S(2)}) collective-permute-start(f32[256,256]{1,0:T(8,128)S(1)} %constant_dynamic-slice_fusion.7), channel_id=1, source_target_pairs={{0,16},{16,0},{1,17},{17,1},{2,18},{18,2},{3,19},{19,3},{4,20},{20... | collective-permute-start | bytes 786440 | tf_op jit(solution)/shard_map/ppermute | solution.py:240
  7.1 9.8 %shard_map.85 = (f32[256,256]{1,0:T(8,128)S(1)}, bf16[128,128,256]{2,1,0:T(8,128)(2,1)}) custom-call(bf16[256,128,128]{2,1,0:T(8,128)(2,1)} %tensor.1, bf16[128,256]{1,0:T(8,128)(2,1)} %second.1, bf16[128,256]{1,0:T(8,128)(2,1)} %time.3), custom_call_target="tpu_custom_call" | custom-call | flops 2147483648 | bytes 16777216 | tf_op jit(solution)/shard_map/pallas_call | solution.py:135
  17.0 1.6 %collective-permute-start.7 = (f32[64,512]{1,0:T(8,128)S(1)}, f32[64,512]{1,0:T(8,128)S(1)}, u32[]{:S(2)}, u32[]{:S(2)}) collective-permute-start(f32[64,512]{1,0:T(8,128)S(1)} %constant_dynamic-slice_fusion.3), channel_id=1, source_target_pairs={{0,8},{4,12},{8,0},{12,4},{1,9},{5,13},{9,1},{13,5},{2,10},{6,14},... | collective-permute-start | bytes 393224 | tf_op jit(solution)/shard_map/ppermute | solution.py:240
  18.7 3.9 %collective-permute-done.7 = f32[64,512]{1,0:T(8,128)S(1)} collective-permute-done((f32[64,512]{1,0:T(8,128)S(1)}, f32[64,512]{1,0:T(8,128)S(1)}, u32[]{:S(2)}, u32[]{:S(2)}) %collective-permute-start.7) | collective-permute-done | bytes 131104 | tf_op jit(solution)/shard_map/ppermute | solution.py:240
  22.7 1.6 %collective-permute-start.8 = (f32[128,512]{1,0:T(8,128)S(1)}, f32[128,512]{1,0:T(8,128)S(1)}, u32[]{:S(2)}, u32[]{:S(2)}) collective-permute-start(f32[128,512]{1,0:T(8,128)S(1)} %pad_maximum_fusion), channel_id=1, source_target_pairs={{0,1},{1,0},{2,3},{3,2},{4,5},{5,4},{6,7},{7,6},{8,9},{9,8},{10,11... | collective-permute-start | bytes 786440 | tf_op jit(solution)/shard_map/ppermute | solution.py:240
  24.4 1.6 %collective-permute-start.2 = (f32[64,256]{1,0:T(8,128)S(1)}, f32[64,256]{1,0:T(8,128)S(1)}, u32[]{:S(2)}, u32[]{:S(2)}) collective-permute-start(f32[64,256]{1,0:T(8,128)S(1)} %constant_dynamic-slice_fusion.5), channel_id=1, source_target_pairs={{0,8},{4,12},{8,0},{12,4},{1,9},{5,13},{9,1},{13,5},{2,10},{6,14},... | collective-permute-start | bytes 196616 | tf_op jit(solution)/shard_map/ppermute | solution.py:240
  26.0 4.3 %collective-permute-done.8 = f32[128,512]{1,0:T(8,128)S(1)} collective-permute-done((f32[128,512]{1,0:T(8,128)S(1)}, f32[128,512]{1,0:T(8,128)S(1)}, u32[]{:S(2)}, u32[]{:S(2)}) %collective-permute-start.8) | collective-permute-done | bytes 262176 | tf_op jit(solution)/shard_map/ppermute | solution.py:240
  30.4 2.7 %collective-permute-start.9 = (f32[64,512]{1,0:T(8,128)S(1)}, f32[64,512]{1,0:T(8,128)S(1)}, u32[]{:S(2)}, u32[]{:S(2)}) collective-permute-start(f32[64,512]{1,0:T(8,128)S(1)} %slice_add_fusion), channel_id=1, source_target_pairs={{0,2},{1,3},{2,0},{3,1},{4,6},{5,7},{6,4},{7,5},{8,10},{9,11},{10,... | collective-permute-start | bytes 393224 | tf_op jit(solution)/shard_map/ppermute | solution.py:240
  33.0 1.4 %collective-permute-start.5 = (f32[64,256]{1,0:T(8,128)S(1)}, f32[64,256]{1,0:T(8,128)S(1)}, u32[]{:S(2)}, u32[]{:S(2)}) collective-permute-start(f32[64,256]{1,0:T(8,128)S(1)} %dynamic-slice_add_fusion.5), channel_id=1, source_target_pairs={{0,3},{1,2},{2,1},{3,0},{4,7},{5,6},{6,5},{7,4},{8,11},{9,10},{10,... | collective-permute-start | bytes 196616 | tf_op jit(solution)/shard_map/ppermute | solution.py:240
  34.4 1.7 %collective-permute-start.4 = (f32[64,256]{1,0:T(8,128)S(1)}, f32[64,256]{1,0:T(8,128)S(1)}, u32[]{:S(2)}, u32[]{:S(2)}) collective-permute-start(f32[64,256]{1,0:T(8,128)S(1)} %dynamic-slice_add_fusion.5), channel_id=1, source_target_pairs={{0,2},{1,3},{2,0},{3,1},{4,6},{5,7},{6,4},{7,5},{8,10},{9,11},{10,... | collective-permute-start | bytes 196616 | tf_op jit(solution)/shard_map/ppermute | solution.py:240
  36.1 1.3 %collective-permute-start.3 = (f32[64,256]{1,0:T(8,128)S(1)}, f32[64,256]{1,0:T(8,128)S(1)}, u32[]{:S(2)}, u32[]{:S(2)}) collective-permute-start(f32[64,256]{1,0:T(8,128)S(1)} %dynamic-slice_add_fusion.5), channel_id=1, source_target_pairs={{0,1},{1,0},{2,3},{3,2},{4,5},{5,4},{6,7},{7,6},{8,9},{9,8},{10,11... | collective-permute-start | bytes 196616 | tf_op jit(solution)/shard_map/ppermute | solution.py:240
  37.5 4.5 %collective-permute-done.9 = f32[64,512]{1,0:T(8,128)S(1)} collective-permute-done((f32[64,512]{1,0:T(8,128)S(1)}, f32[64,512]{1,0:T(8,128)S(1)}, u32[]{:S(2)}, u32[]{:S(2)}) %collective-permute-start.9) | collective-permute-done | bytes 131104 | tf_op jit(solution)/shard_map/ppermute | solution.py:240
  43.6 2.7 %collective-permute-done.10 = f32[64,256]{1,0:T(8,128)S(1)} collective-permute-done((f32[64,256]{1,0:T(8,128)S(1)}, f32[64,256]{1,0:T(8,128)S(1)}, u32[]{:S(2)}, u32[]{:S(2)}) %collective-permute-start.10) | collective-permute-done | bytes 65568 | tf_op jit(solution)/shard_map/ppermute | solution.py:240
  46.6 1.6 %collective-permute-start.11 = (bf16[64,256]{1,0:T(8,128)(2,1)S(1)}, bf16[64,256]{1,0:T(8,128)(2,1)S(1)}, u32[]{:S(2)}, u32[]{:S(2)}) collective-permute-start(bf16[64,256]{1,0:T(8,128)(2,1)S(1)} %fusion.17), channel_id=1, source_target_pairs={{0,8},{4,12},{8,0},{12,4},{1,9},{5,13},{9,1},{13,5},{2,10},{6,14},... | collective-permute-start | bytes 98312 | tf_op jit(solution)/shard_map/ppermute | solution.py:240
  48.2 2.4 %collective-permute-done.11 = bf16[64,256]{1,0:T(8,128)(2,1)S(1)} collective-permute-done((bf16[64,256]{1,0:T(8,128)(2,1)S(1)}, bf16[64,256]{1,0:T(8,128)(2,1)S(1)}, u32[]{:S(2)}, u32[]{:S(2)}) %collective-permute-start.11) | collective-permute-done | bytes 32800 | tf_op jit(solution)/shard_map/ppermute | solution.py:240
  50.7 1.2 %collective-permute-done.12 = bf16[128,256]{1,0:T(8,128)(2,1)S(1)} collective-permute-done((bf16[128,256]{1,0:T(8,128)(2,1)S(1)}, bf16[128,256]{1,0:T(8,128)(2,1)S(1)}, u32[]{:S(2)}, u32[]{:S(2)}) %collective-permute-start.12) | collective-permute-done | bytes 65568 | tf_op jit(solution)/shard_map/ppermute | solution.py:240
  52.0 5.5 %shard_map.87 = (f32[128,256]{1,0:T(8,128)S(1)}, bf16[256,256]{1,0:T(8,128)(2,1)}) custom-call(bf16[128,128,256]{2,1,0:T(8,128)(2,1)} %get-tuple-element.10.turned, bf16[256,256]{1,0:T(8,128)(2,1)S(1)} %maximum_select_fusion.4.first_turned, bf16[128,256]{1,0:T(8,128)(2,1)S(1)} %copy-done.1), custom_call_target="tpu_custom_call" | custom-call | flops 2147483648 | bytes 8388608 | tf_op jit(solution)/shard_map/pallas_call | solution.py:212
  58.3 1.5 %collective-permute-start.17 = (bf16[256,256]{1,0:T(8,128)(2,1)S(1)}, bf16[256,256]{1,0:T(8,128)(2,1)S(1)}, u32[]{:S(2)}, u32[]{:S(2)}) collective-permute-start(bf16[256,256]{1,0:T(8,128)(2,1)S(1)} %maximum_select_fusion.4.first_turned), channel_id=1, source_target_pairs={{0,16},{16,0},{1,17},{17,1},{2,18},{18,2},{3,19},{19,3},{4,20},{20... | collective-permute-start | bytes 393224 | tf_op jit(solution)/shard_map/ppermute | solution.py:240
  59.8 2.8 %collective-permute-done.13 = f32[64,256]{1,0:T(8,128)S(1)} collective-permute-done((f32[64,256]{1,0:T(8,128)S(1)}, f32[64,256]{1,0:T(8,128)S(1)}, u32[]{:S(2)}, u32[]{:S(2)}) %collective-permute-start.13) | collective-permute-done | bytes 65568 | tf_op jit(solution)/shard_map/ppermute | solution.py:240
  62.6 2.8 %collective-permute-start.16 = (f32[64,256]{1,0:T(8,128)S(1)}, f32[64,256]{1,0:T(8,128)S(1)}, u32[]{:S(2)}, u32[]{:S(2)}) collective-permute-start(f32[64,256]{1,0:T(8,128)S(1)} %dynamic-slice_add_fusion.4), channel_id=1, source_target_pairs={{0,3},{1,2},{2,1},{3,0},{4,7},{5,6},{6,5},{7,4},{8,11},{9,10},{10,... | collective-permute-start | bytes 196616 | tf_op jit(solution)/shard_map/ppermute | solution.py:240
  65.4 1.6 %collective-permute-start.14 = (f32[64,256]{1,0:T(8,128)S(1)}, f32[64,256]{1,0:T(8,128)S(1)}, u32[]{:S(2)}, u32[]{:S(2)}) collective-permute-start(f32[64,256]{1,0:T(8,128)S(1)} %dynamic-slice_add_fusion.4), channel_id=1, source_target_pairs={{0,1},{1,0},{2,3},{3,2},{4,5},{5,4},{6,7},{7,6},{8,9},{9,8},{10,11... | collective-permute-start | bytes 196616 | tf_op jit(solution)/shard_map/ppermute | solution.py:240
  67.5 2.8 %collective-permute-done.18 = bf16[256,256]{1,0:T(8,128)(2,1)S(1)} collective-permute-done((bf16[256,256]{1,0:T(8,128)(2,1)S(1)}, bf16[256,256]{1,0:T(8,128)(2,1)S(1)}, u32[]{:S(2)}, u32[]{:S(2)}) %collective-permute-start.18) | collective-permute-done | bytes 131104 | tf_op jit(solution)/shard_map/ppermute | solution.py:240
  70.8 2.1 %collective-permute-done.15 = f32[64,256]{1,0:T(8,128)S(1)} collective-permute-done((f32[64,256]{1,0:T(8,128)S(1)}, f32[64,256]{1,0:T(8,128)S(1)}, u32[]{:S(2)}, u32[]{:S(2)}) %collective-permute-start.15) | collective-permute-done | bytes 65568 | tf_op jit(solution)/shard_map/ppermute | solution.py:240
  72.9 1.5 %collective-permute-start.19 = (bf16[64,256]{1,0:T(8,128)(2,1)S(1)}, bf16[64,256]{1,0:T(8,128)(2,1)S(1)}, u32[]{:S(2)}, u32[]{:S(2)}) collective-permute-start(bf16[64,256]{1,0:T(8,128)(2,1)S(1)} %divide_convert_fusion.1), channel_id=1, source_target_pairs={{0,16},{16,0},{1,17},{17,1},{2,18},{18,2},{3,19},{19,3},{4,20},{20... | collective-permute-start | bytes 98312 | tf_op jit(solution)/shard_map/ppermute | solution.py:240
  74.4 2.5 %collective-permute-done.19 = bf16[64,256]{1,0:T(8,128)(2,1)S(1)} collective-permute-done((bf16[64,256]{1,0:T(8,128)(2,1)S(1)}, bf16[64,256]{1,0:T(8,128)(2,1)S(1)}, u32[]{:S(2)}, u32[]{:S(2)}) %collective-permute-start.19) | collective-permute-done | bytes 32800 | tf_op jit(solution)/shard_map/ppermute | solution.py:240
  76.9 1.5 %collective-permute-start.24 = (bf16[128,256]{1,0:T(8,128)(2,1)S(1)}, bf16[128,256]{1,0:T(8,128)(2,1)S(1)}, u32[]{:S(2)}, u32[]{:S(2)}) collective-permute-start(bf16[128,256]{1,0:T(8,128)(2,1)S(1)} %maximum_select_fusion.8.second), channel_id=1, source_target_pairs={{0,8},{4,12},{8,0},{12,4},{1,9},{5,13},{9,1},{13,5},{2,10},{6,14},... | collective-permute-start | bytes 196616 | tf_op jit(solution)/shard_map/ppermute | solution.py:240
  78.5 6.8 %shard_map.88 = f32[128,256]{1,0:T(8,128)S(1)} custom-call(bf16[128,128,256]{2,1,0:T(8,128)(2,1)} %get-tuple-element.10.turned, bf16[256,256]{1,0:T(8,128)(2,1)} %get-tuple-element.7.first_in, bf16[128,256]{1,0:T(8,128)(2,1)S(1)} %maximum_select_fusion.8.second), custom_call_target="tpu_custom_call" | custom-call | flops 2147483648 | bytes 8388608 | tf_op jit(solution)/shard_map/pallas_call | solution.py:212
  86.6 1.5 %collective-permute-start.23 = (f32[64,256]{1,0:T(8,128)S(1)}, f32[64,256]{1,0:T(8,128)S(1)}, u32[]{:S(2)}, u32[]{:S(2)}) collective-permute-start(f32[64,256]{1,0:T(8,128)S(1)} %dynamic-slice_add_fusion.3), channel_id=1, source_target_pairs={{0,24},{4,28},{8,16},{12,20},{16,8},{20,12},{24,0},{28,4},{1,25},{... | collective-permute-start | bytes 196616 | tf_op jit(solution)/shard_map/ppermute | solution.py:240
  88.7 1.5 %collective-permute-start.21 = (f32[64,256]{1,0:T(8,128)S(1)}, f32[64,256]{1,0:T(8,128)S(1)}, u32[]{:S(2)}, u32[]{:S(2)}) collective-permute-start(f32[64,256]{1,0:T(8,128)S(1)} %dynamic-slice_add_fusion.3), channel_id=1, source_target_pairs={{0,8},{4,12},{8,0},{12,4},{16,24},{20,28},{24,16},{28,20},{1,9},{5... | collective-permute-start | bytes 196616 | tf_op jit(solution)/shard_map/ppermute | solution.py:240
  90.7 1.4 %collective-permute-done.23 = f32[64,256]{1,0:T(8,128)S(1)} collective-permute-done((f32[64,256]{1,0:T(8,128)S(1)}, f32[64,256]{1,0:T(8,128)S(1)}, u32[]{:S(2)}, u32[]{:S(2)}) %collective-permute-start.23) | collective-permute-done | bytes 65568 | tf_op jit(solution)/shard_map/ppermute | solution.py:240
  93.3 1.2 %collective-permute-done.26 = bf16[64,256]{1,0:T(8,128)(2,1)S(1)} collective-permute-done((bf16[64,256]{1,0:T(8,128)(2,1)S(1)}, bf16[64,256]{1,0:T(8,128)(2,1)S(1)}, u32[]{:S(2)}, u32[]{:S(2)}) %collective-permute-start.26) | collective-permute-done | bytes 32800 | tf_op jit(solution)/shard_map/ppermute | solution.py:240
  (75 shorter events, 9.8 us)
Async XLA Ops:
  0.6 42.0 %copy-start = (bf16[256,256]{1,0:T(8,128)(2,1)S(1)}, bf16[256,256]{1,0:T(8,128)(2,1)}, u32[]{:S(2)}) copy-start(bf16[256,256]{1,0:T(8,128)(2,1)} %param.8) | copy-start | bytes 393220
  3.1 48.8 %copy-start.1 = (bf16[128,256]{1,0:T(8,128)(2,1)S(1)}, bf16[128,256]{1,0:T(8,128)(2,1)}, u32[]{:S(2)}) copy-start(bf16[128,256]{1,0:T(8,128)(2,1)} %time.3) | copy-start | bytes 196612
  3.1 13.8 %collective-permute-start.6 = (f32[128,512]{1,0:T(8,128)S(1)}, f32[128,512]{1,0:T(8,128)S(1)}, u32[]{:S(2)}, u32[]{:S(2)}) collective-permute-start(f32[128,512]{1,0:T(8,128)S(1)} %constant_dynamic-slice_fusion.4), channel_id=1, source_target_pairs={{0,4},{4,0},{8,12},{12,8},{1,5},{5,1},{9,13},{13,9},{2,6},{6,2},{1... | collective-permute-start | bytes 786440 | tf_op jit(solution)/shard_map/ppermute | solution.py:240
  3.7 14.8 %collective-permute-start = (f32[256,256]{1,0:T(8,128)S(1)}, f32[256,256]{1,0:T(8,128)S(1)}, u32[]{:S(2)}, u32[]{:S(2)}) collective-permute-start(f32[256,256]{1,0:T(8,128)S(1)} %constant_dynamic-slice_fusion.7), channel_id=1, source_target_pairs={{0,16},{16,0},{1,17},{17,1},{2,18},{18,2},{3,19},{19,3},{4,20},{20... | collective-permute-start | bytes 786440 | tf_op jit(solution)/shard_map/ppermute | solution.py:240
  17.0 5.7 %collective-permute-start.7 = (f32[64,512]{1,0:T(8,128)S(1)}, f32[64,512]{1,0:T(8,128)S(1)}, u32[]{:S(2)}, u32[]{:S(2)}) collective-permute-start(f32[64,512]{1,0:T(8,128)S(1)} %constant_dynamic-slice_fusion.3), channel_id=1, source_target_pairs={{0,8},{4,12},{8,0},{12,4},{1,9},{5,13},{9,1},{13,5},{2,10},{6,14},... | collective-permute-start | bytes 393224 | tf_op jit(solution)/shard_map/ppermute | solution.py:240
  18.6 51.9 %copy-start.3 = (bf16[128,256]{1,0:T(8,128)(2,1)S(1)}, bf16[128,256]{1,0:T(8,128)(2,1)}, u32[]{:S(2)}) copy-start(bf16[128,256]{1,0:T(8,128)(2,1)} %second.1) | copy-start | bytes 196612
  18.7 5.7 %collective-permute-start.1 = (f32[128,256]{1,0:T(8,128)S(1)}, f32[128,256]{1,0:T(8,128)S(1)}, u32[]{:S(2)}, u32[]{:S(2)}) collective-permute-start(f32[128,256]{1,0:T(8,128)S(1)} %constant_dynamic-slice_fusion.6), channel_id=1, source_target_pairs={{0,4},{4,0},{8,12},{12,8},{1,5},{5,1},{9,13},{13,9},{2,6},{6,2},{1... | collective-permute-start | bytes 393224 | tf_op jit(solution)/shard_map/ppermute | solution.py:240
  22.7 7.6 %collective-permute-start.8 = (f32[128,512]{1,0:T(8,128)S(1)}, f32[128,512]{1,0:T(8,128)S(1)}, u32[]{:S(2)}, u32[]{:S(2)}) collective-permute-start(f32[128,512]{1,0:T(8,128)S(1)} %pad_maximum_fusion), channel_id=1, source_target_pairs={{0,1},{1,0},{2,3},{3,2},{4,5},{5,4},{6,7},{7,6},{8,9},{9,8},{10,11... | collective-permute-start | bytes 786440 | tf_op jit(solution)/shard_map/ppermute | solution.py:240
  24.4 8.6 %collective-permute-start.2 = (f32[64,256]{1,0:T(8,128)S(1)}, f32[64,256]{1,0:T(8,128)S(1)}, u32[]{:S(2)}, u32[]{:S(2)}) collective-permute-start(f32[64,256]{1,0:T(8,128)S(1)} %constant_dynamic-slice_fusion.5), channel_id=1, source_target_pairs={{0,8},{4,12},{8,0},{12,4},{1,9},{5,13},{9,1},{13,5},{2,10},{6,14},... | collective-permute-start | bytes 196616 | tf_op jit(solution)/shard_map/ppermute | solution.py:240
  30.4 11.6 %collective-permute-start.9 = (f32[64,512]{1,0:T(8,128)S(1)}, f32[64,512]{1,0:T(8,128)S(1)}, u32[]{:S(2)}, u32[]{:S(2)}) collective-permute-start(f32[64,512]{1,0:T(8,128)S(1)} %slice_add_fusion), channel_id=1, source_target_pairs={{0,2},{1,3},{2,0},{3,1},{4,6},{5,7},{6,4},{7,5},{8,10},{9,11},{10,... | collective-permute-start | bytes 393224 | tf_op jit(solution)/shard_map/ppermute | solution.py:240
  33.0 9.8 %collective-permute-start.5 = (f32[64,256]{1,0:T(8,128)S(1)}, f32[64,256]{1,0:T(8,128)S(1)}, u32[]{:S(2)}, u32[]{:S(2)}) collective-permute-start(f32[64,256]{1,0:T(8,128)S(1)} %dynamic-slice_add_fusion.5), channel_id=1, source_target_pairs={{0,3},{1,2},{2,1},{3,0},{4,7},{5,6},{6,5},{7,4},{8,11},{9,10},{10,... | collective-permute-start | bytes 196616 | tf_op jit(solution)/shard_map/ppermute | solution.py:240
  34.4 9.2 %collective-permute-start.4 = (f32[64,256]{1,0:T(8,128)S(1)}, f32[64,256]{1,0:T(8,128)S(1)}, u32[]{:S(2)}, u32[]{:S(2)}) collective-permute-start(f32[64,256]{1,0:T(8,128)S(1)} %dynamic-slice_add_fusion.5), channel_id=1, source_target_pairs={{0,2},{1,3},{2,0},{3,1},{4,6},{5,7},{6,4},{7,5},{8,10},{9,11},{10,... | collective-permute-start | bytes 196616 | tf_op jit(solution)/shard_map/ppermute | solution.py:240
  36.1 7.5 %collective-permute-start.3 = (f32[64,256]{1,0:T(8,128)S(1)}, f32[64,256]{1,0:T(8,128)S(1)}, u32[]{:S(2)}, u32[]{:S(2)}) collective-permute-start(f32[64,256]{1,0:T(8,128)S(1)} %dynamic-slice_add_fusion.5), channel_id=1, source_target_pairs={{0,1},{1,0},{2,3},{3,2},{4,5},{5,4},{6,7},{7,6},{8,9},{9,8},{10,11... | collective-permute-start | bytes 196616 | tf_op jit(solution)/shard_map/ppermute | solution.py:240
  42.0 4.3 %collective-permute-start.10 = (f32[64,256]{1,0:T(8,128)S(1)}, f32[64,256]{1,0:T(8,128)S(1)}, u32[]{:S(2)}, u32[]{:S(2)}) collective-permute-start(f32[64,256]{1,0:T(8,128)S(1)} %slice.44), channel_id=1, source_target_pairs={{0,16},{16,0},{1,17},{17,1},{2,18},{18,2},{3,19},{19,3},{4,20},{20... | collective-permute-start | bytes 196616 | tf_op jit(solution)/shard_map/ppermute | solution.py:240
  46.6 4.0 %collective-permute-start.11 = (bf16[64,256]{1,0:T(8,128)(2,1)S(1)}, bf16[64,256]{1,0:T(8,128)(2,1)S(1)}, u32[]{:S(2)}, u32[]{:S(2)}) collective-permute-start(bf16[64,256]{1,0:T(8,128)(2,1)S(1)} %fusion.17), channel_id=1, source_target_pairs={{0,8},{4,12},{8,0},{12,4},{1,9},{5,13},{9,1},{13,5},{2,10},{6,14},... | collective-permute-start | bytes 98312 | tf_op jit(solution)/shard_map/ppermute | solution.py:240
  50.6 1.3 %collective-permute-start.12 = (bf16[128,256]{1,0:T(8,128)(2,1)S(1)}, bf16[128,256]{1,0:T(8,128)(2,1)S(1)}, u32[]{:S(2)}, u32[]{:S(2)}) collective-permute-start(bf16[128,256]{1,0:T(8,128)(2,1)S(1)} %maximum_select_fusion.7), channel_id=1, source_target_pairs={{0,4},{4,0},{8,12},{12,8},{1,5},{5,1},{9,13},{13,9},{2,6},{6,2},{1... | collective-permute-start | bytes 196616 | tf_op jit(solution)/shard_map/ppermute | solution.py:240
  57.5 5.0 %collective-permute-start.13 = (f32[64,256]{1,0:T(8,128)S(1)}, f32[64,256]{1,0:T(8,128)S(1)}, u32[]{:S(2)}, u32[]{:S(2)}) collective-permute-start(f32[64,256]{1,0:T(8,128)S(1)} %constant_dynamic-slice_fusion.1), channel_id=1, source_target_pairs={{0,16},{16,0},{1,17},{17,1},{2,18},{18,2},{3,19},{19,3},{4,20},{20... | collective-permute-start | bytes 196616 | tf_op jit(solution)/shard_map/ppermute | solution.py:240
  58.2 12.0 %collective-permute-start.18 = (bf16[256,256]{1,0:T(8,128)(2,1)S(1)}, bf16[256,256]{1,0:T(8,128)(2,1)S(1)}, u32[]{:S(2)}, u32[]{:S(2)}) collective-permute-start(bf16[256,256]{1,0:T(8,128)(2,1)S(1)} %maximum_select_fusion.5), channel_id=1, source_target_pairs={{0,2},{1,3},{2,0},{3,1},{4,6},{5,7},{6,4},{7,5},{8,10},{9,11},{10,... | collective-permute-start | bytes 393224 | tf_op jit(solution)/shard_map/ppermute | solution.py:240
  58.3 8.8 %collective-permute-start.17 = (bf16[256,256]{1,0:T(8,128)(2,1)S(1)}, bf16[256,256]{1,0:T(8,128)(2,1)S(1)}, u32[]{:S(2)}, u32[]{:S(2)}) collective-permute-start(bf16[256,256]{1,0:T(8,128)(2,1)S(1)} %maximum_select_fusion.4.first_turned), channel_id=1, source_target_pairs={{0,16},{16,0},{1,17},{17,1},{2,18},{18,2},{3,19},{19,3},{4,20},{20... | collective-permute-start | bytes 393224 | tf_op jit(solution)/shard_map/ppermute | solution.py:240
  62.6 8.2 %collective-permute-start.16 = (f32[64,256]{1,0:T(8,128)S(1)}, f32[64,256]{1,0:T(8,128)S(1)}, u32[]{:S(2)}, u32[]{:S(2)}) collective-permute-start(f32[64,256]{1,0:T(8,128)S(1)} %dynamic-slice_add_fusion.4), channel_id=1, source_target_pairs={{0,3},{1,2},{2,1},{3,0},{4,7},{5,6},{6,5},{7,4},{8,11},{9,10},{10,... | collective-permute-start | bytes 196616 | tf_op jit(solution)/shard_map/ppermute | solution.py:240
  65.4 7.5 %collective-permute-start.15 = (f32[64,256]{1,0:T(8,128)S(1)}, f32[64,256]{1,0:T(8,128)S(1)}, u32[]{:S(2)}, u32[]{:S(2)}) collective-permute-start(f32[64,256]{1,0:T(8,128)S(1)} %dynamic-slice_add_fusion.4), channel_id=1, source_target_pairs={{0,2},{1,3},{2,0},{3,1},{4,6},{5,7},{6,4},{7,5},{8,10},{9,11},{10,... | collective-permute-start | bytes 196616 | tf_op jit(solution)/shard_map/ppermute | solution.py:240
  65.4 7.5 %collective-permute-start.14 = (f32[64,256]{1,0:T(8,128)S(1)}, f32[64,256]{1,0:T(8,128)S(1)}, u32[]{:S(2)}, u32[]{:S(2)}) collective-permute-start(f32[64,256]{1,0:T(8,128)S(1)} %dynamic-slice_add_fusion.4), channel_id=1, source_target_pairs={{0,1},{1,0},{2,3},{3,2},{4,5},{5,4},{6,7},{7,6},{8,9},{9,8},{10,11... | collective-permute-start | bytes 196616 | tf_op jit(solution)/shard_map/ppermute | solution.py:240
  72.9 4.0 %collective-permute-start.19 = (bf16[64,256]{1,0:T(8,128)(2,1)S(1)}, bf16[64,256]{1,0:T(8,128)(2,1)S(1)}, u32[]{:S(2)}, u32[]{:S(2)}) collective-permute-start(bf16[64,256]{1,0:T(8,128)(2,1)S(1)} %divide_convert_fusion.1), channel_id=1, source_target_pairs={{0,16},{16,0},{1,17},{17,1},{2,18},{18,2},{3,19},{19,3},{4,20},{20... | collective-permute-start | bytes 98312 | tf_op jit(solution)/shard_map/ppermute | solution.py:240
  76.9 18.2 %copy-start.2 = (bf16[128,256]{1,0:T(8,128)(2,1)}, bf16[128,256]{1,0:T(8,128)(2,1)S(1)}, u32[]{:S(2)}) copy-start(bf16[128,256]{1,0:T(8,128)(2,1)S(1)} %maximum_select_fusion.8.second) | copy-start | bytes 196612
  76.9 8.5 %collective-permute-start.24 = (bf16[128,256]{1,0:T(8,128)(2,1)S(1)}, bf16[128,256]{1,0:T(8,128)(2,1)S(1)}, u32[]{:S(2)}, u32[]{:S(2)}) collective-permute-start(bf16[128,256]{1,0:T(8,128)(2,1)S(1)} %maximum_select_fusion.8.second), channel_id=1, source_target_pairs={{0,8},{4,12},{8,0},{12,4},{1,9},{5,13},{9,1},{13,5},{2,10},{6,14},... | collective-permute-start | bytes 196616 | tf_op jit(solution)/shard_map/ppermute | solution.py:240
  85.3 1.3 %collective-permute-start.20 = (f32[64,256]{1,0:T(8,128)S(1)}, f32[64,256]{1,0:T(8,128)S(1)}, u32[]{:S(2)}, u32[]{:S(2)}) collective-permute-start(f32[64,256]{1,0:T(8,128)S(1)} %constant_dynamic-slice_fusion), channel_id=1, source_target_pairs={{0,4},{4,0},{8,12},{12,8},{1,5},{5,1},{9,13},{13,9},{2,6},{6,2},{1... | collective-permute-start | bytes 196616 | tf_op jit(solution)/shard_map/ppermute | solution.py:240
  85.4 4.8 %collective-permute-start.25 = (bf16[256,256]{1,0:T(8,128)(2,1)S(1)}, bf16[256,256]{1,0:T(8,128)(2,1)S(1)}, u32[]{:S(2)}, u32[]{:S(2)}) collective-permute-start(bf16[256,256]{1,0:T(8,128)(2,1)S(1)} %maximum_select_fusion.6), channel_id=1, source_target_pairs={{0,4},{4,0},{8,12},{12,8},{1,5},{5,1},{9,13},{13,9},{2,6},{6,2},{1... | collective-permute-start | bytes 393224 | tf_op jit(solution)/shard_map/ppermute | solution.py:240
  86.6 5.5 %collective-permute-start.23 = (f32[64,256]{1,0:T(8,128)S(1)}, f32[64,256]{1,0:T(8,128)S(1)}, u32[]{:S(2)}, u32[]{:S(2)}) collective-permute-start(f32[64,256]{1,0:T(8,128)S(1)} %dynamic-slice_add_fusion.3), channel_id=1, source_target_pairs={{0,24},{4,28},{8,16},{12,20},{16,8},{20,12},{24,0},{28,4},{1,25},{... | collective-permute-start | bytes 196616 | tf_op jit(solution)/shard_map/ppermute | solution.py:240
  88.1 4.3 %collective-permute-start.22 = (f32[64,256]{1,0:T(8,128)S(1)}, f32[64,256]{1,0:T(8,128)S(1)}, u32[]{:S(2)}, u32[]{:S(2)}) collective-permute-start(f32[64,256]{1,0:T(8,128)S(1)} %dynamic-slice_add_fusion.3), channel_id=1, source_target_pairs={{0,16},{4,20},{8,24},{12,28},{16,0},{20,4},{24,8},{28,12},{1,17},{... | collective-permute-start | bytes 196616 | tf_op jit(solution)/shard_map/ppermute | solution.py:240
  88.7 4.5 %collective-permute-start.21 = (f32[64,256]{1,0:T(8,128)S(1)}, f32[64,256]{1,0:T(8,128)S(1)}, u32[]{:S(2)}, u32[]{:S(2)}) collective-permute-start(f32[64,256]{1,0:T(8,128)S(1)} %dynamic-slice_add_fusion.3), channel_id=1, source_target_pairs={{0,8},{4,12},{8,0},{12,4},{16,24},{20,28},{24,16},{28,20},{1,9},{5... | collective-permute-start | bytes 196616 | tf_op jit(solution)/shard_map/ppermute | solution.py:240
  93.2 1.3 %collective-permute-start.26 = (bf16[64,256]{1,0:T(8,128)(2,1)S(1)}, bf16[64,256]{1,0:T(8,128)(2,1)S(1)}, u32[]{:S(2)}, u32[]{:S(2)}) collective-permute-start(bf16[64,256]{1,0:T(8,128)(2,1)S(1)} %divide_convert_fusion), channel_id=1, source_target_pairs={{0,4},{4,0},{8,12},{12,8},{1,5},{5,1},{9,13},{13,9},{2,6},{6,2},{1... | collective-permute-start | bytes 98312 | tf_op jit(solution)/shard_map/ppermute | solution.py:240

commit v2 on v0

--- a/solution.py
+++ b/solution.py
@@ -33,57 +33,99 @@
     )
 
 
-def local_kernel(matrix, column, second, time, coupled, grams, gram_time):
+def bring(sources, targets, sem):
+    def copy(index):
+        return pltpu.make_async_copy(sources[index], targets[index], sem.at[index])
+
+    for index in range(len(sources)):
+        copy(index).start()
+    return lambda index: copy(index).wait()
+
+
+def gram_kernel(column, second, time, grams, gram_time, turned, second_out, time_out, held, sem):
     f32 = jnp.float32
+    wait = bring((column, second, time), (held, second_out, time_out), sem)
     rank = column.shape[1]
-    turned = column[...].T
-    grams[:, :rank] = jnp.dot(turned, column[...], preferred_element_type=f32)
-    coupled[...] = lax.dot_general(
-        turned, matrix[...], (((1,), (1,)), ((), ())), preferred_element_type=f32
-    )
-    grams[:, rank:] = jnp.dot(second[...].T, second[...], preferred_element_type=f32)
-    gram_time[...] = jnp.dot(time[...].T, time[...], preferred_element_type=f32)
-
-
-def local_products(matrix, column, second, time):
-    rank = column.shape[1]
-    rows, width = matrix.shape
+    wait(0)
+    turned[...] = held[...].T
+    grams[:, :rank] = jnp.dot(turned[...], held[...], preferred_element_type=f32)
+    wait(1)
+    grams[:, rank:] = jnp.dot(second_out[...].T, second_out[...], preferred_element_type=f32)
+    wait(2)
+    gram_time[...] = jnp.dot(time_out[...].T, time_out[...], preferred_element_type=f32)
+
+
+def local_grams(column, second, time):
+    width, rank = column.shape
     f32 = jnp.float32
     return kernel_call(
-        local_kernel,
-        2 * width * rank * (rows + rank),
-        2 * width * (rows + rank),
+        gram_kernel,
+        2 * width * rank * rank,
+        2 * width * rank,
         out_shape=(
-            jax.ShapeDtypeStruct((rank, rows), f32),
             jax.ShapeDtypeStruct((rank, 2 * rank), f32),
             jax.ShapeDtypeStruct((rank, rank), f32),
+            jax.ShapeDtypeStruct((rank, width), column.dtype),
+            jax.ShapeDtypeStruct(second.shape, second.dtype),
+            jax.ShapeDtypeStruct(time.shape, time.dtype),
         ),
-        in_specs=[VMEM] * 4,
-        out_specs=(VMEM,) * 3,
-    )(matrix, column, second, time)
-
-
-def slab_kernel(chunk, steps, tensor, second, time, total, turned, read, read_sem, ready, ready_sem, added):
+        in_specs=[ANY] * 3,
+        out_specs=(VMEM,) * 5,
+        scratch_shapes=[
+            pltpu.VMEM(column.shape, column.dtype),
+            pltpu.SemaphoreType.DMA((3,)),
+        ],
+    )(*(in_hbm(a) for a in (column, second, time)))
+
+
+def coupled_kernel(turned, matrix, coupled):
+    coupled[...] = lax.dot_general(
+        turned[...], matrix[...], (((1,), (1,)), ((), ())), preferred_element_type=jnp.float32
+    )
+
+
+def local_coupled(turned, matrix):
+    rank, width = turned.shape
+    rows = matrix.shape[0]
+    return kernel_call(
+        coupled_kernel,
+        2 * width * rank * rows,
+        2 * width * (rows + rank),
+        out_shape=jax.ShapeDtypeStruct((rank, rows), jnp.float32),
+        in_specs=[VMEM] * 2,
+        out_specs=VMEM,
+    )(turned, matrix)
+
+
+def slab_kernel(first, chunk, steps, tensor, second, time, *refs):
+    *start, total, turned, read, read_sem, ready, ready_sem, added = refs
+    ahead = min(3, steps)
+
     def fetch(step):
-        source = tensor.at[:, pl.ds(step * chunk, chunk)]
+        source = tensor.at[:, pl.ds(first + step * chunk, chunk)]
         return pltpu.make_async_copy(source, read.at[step], read_sem.at[step])
 
     def put(step):
         target = turned.at[pl.ds(step * chunk, chunk)]
         return pltpu.make_async_copy(ready.at[step], target, ready_sem.at[step])
 
-    for step in range(steps):
+    for step in range(ahead):
         fetch(step).start()
     time_wide = time[...].astype(jnp.float32)
-    added[...] = jnp.zeros_like(added)
+    added[...] = start[0][...] if start else jnp.zeros_like(added)
 
     def body(step, carry):
         fetch(step).wait()
+
+        @pl.when(step + ahead < steps)
+        def _():
+            fetch(step + ahead).start()
+
         block = jnp.swapaxes(read[step], 0, 1)
         for j in range(chunk):
             ready[step, j] = block[j].T
         put(step).start()
-        row = pl.multiple_of(step * chunk, chunk)
+        row = pl.multiple_of(first + step * chunk, chunk)
         weights = second[pl.ds(row, chunk), :].astype(jnp.float32)
         khatri = jnp.concatenate(
             [(weights[j : j + 1, :] * time_wide).astype(jnp.bfloat16) for j in range(chunk)], 0
@@ -93,7 +135,7 @@
         return carry
 
     lax.fori_loop(0, steps, body, 0)
-    total[...] = added[...].T
+    total[...] = added[...].T if start else added[...]
 
     def finish(step, carry):
         put(step).wait()
@@ -102,20 +144,20 @@
     lax.fori_loop(0, steps, finish, 0)
 
 
-def slab_and_turn(tensor, second, time):
-    tile_i, tile_j, tile_k = tensor.shape
+def slab_and_turn(tensor, second, time, first, count, start=()):
+    tile_i, _, tile_k = tensor.shape
     rank = time.shape[1]
-    chunk = chunk_of(tile_j, 16)
-    steps = tile_j // chunk
+    chunk = chunk_of(count, 8)
+    steps = count // chunk
     return kernel_call(
-        functools.partial(slab_kernel, chunk, steps),
-        2 * tile_i * tile_j * tile_k * rank,
-        4 * tile_i * tile_j * tile_k,
+        functools.partial(slab_kernel, first, chunk, steps),
+        2 * tile_i * count * tile_k * rank,
+        4 * tile_i * count * tile_k,
         out_shape=(
-            jax.ShapeDtypeStruct((rank, tile_i), jnp.float32),
-            pltpu.HBM((tile_j, tile_k, tile_i), tensor.dtype),
+            jax.ShapeDtypeStruct((rank, tile_i) if start else (tile_i, rank), jnp.float32),
+            pltpu.HBM((count, tile_k, tile_i), tensor.dtype),
         ),
-        in_specs=[ANY, VMEM, VMEM],
+        in_specs=[ANY] + [VMEM] * (2 + len(start)),
         out_specs=(VMEM, ANY),
         scratch_shapes=[
             pltpu.VMEM((steps, tile_i, chunk, tile_k), tensor.dtype),
@@ -124,74 +166,87 @@
             pltpu.SemaphoreType.DMA((steps,)),
             pltpu.VMEM((tile_i, rank), jnp.float32),
         ],
-    )(in_hbm(tensor), second, time)
-
-
-def fetcher(turned, read, read_sem, chunk):
-    def fetch(step):
-        source = turned.at[pl.ds(step * chunk, chunk)]
-        return pltpu.make_async_copy(source, read.at[step], read_sem.at[step])
-
-    for step in range(read.shape[0]):
-        fetch(step).start()
-    return fetch
-
-
-def plane_kernel(chunk, turned, first_turned, time, total, first, read, read_sem):
-    fetch = fetcher(turned, read, read_sem, chunk)
+    )(in_hbm(tensor), second, time, *start)
+
+
+def fetcher(parts, read, read_sem, chunk):
+    steps = parts[0].shape[0] // chunk
+
+    def fetch(part, step):
+        source = parts[part].at[pl.ds(step * chunk, chunk)]
+        slot = part * steps + step
+        return pltpu.make_async_copy(source, read.at[slot], read_sem.at[slot])
+
+    for part in range(len(parts)):
+        for step in range(steps):
+            fetch(part, step).start()
+    return fetch, steps
+
+
+def plane_kernel(chunk, parts, first_turned, time, total, first, read, read_sem):
+    fetch, steps = fetcher(parts, read, read_sem, chunk)
     first[...] = first_turned[...].T
     shared = first[...]
-
-    def body(step, carry):
-        fetch(step).wait()
-        sums = []
-        for j in range(chunk):
-            weighted = jnp.dot(read[step, j], shared, preferred_element_type=jnp.float32)
-            scaled = weighted * time[...].astype(jnp.float32)
-            sums.append(jnp.sum(scaled, axis=0, keepdims=True))
-        row = pl.multiple_of(step * chunk, chunk)
-        total[pl.ds(row, chunk), :] = jnp.concatenate(sums, 0)
-        return carry
-
-    lax.fori_loop(0, read.shape[0], body, 0)
-
-
-def time_kernel(chunk, turned, first, second, total, read, read_sem, wide):
-    fetch = fetcher(turned, read, read_sem, chunk)
+    for part in range(len(parts)):
+
+        def body(step, carry):
+            fetch(part, step).wait()
+            slot = part * steps + step
+            sums = []
+            for j in range(chunk):
+                weighted = jnp.dot(read[slot, j], shared, preferred_element_type=jnp.float32)
+                scaled = weighted * time[...].astype(jnp.float32)
+                sums.append(jnp.sum(scaled, axis=0, keepdims=True))
+            row = pl.multiple_of(slot * chunk, chunk)
+            total[pl.ds(row, chunk), :] = jnp.concatenate(sums, 0)
+            return carry
+
+        lax.fori_loop(0, steps, body, 0)
+
+
+def time_kernel(chunk, parts, first_turned, second, total, read, read_sem, wide, first):
+    fetch, steps = fetcher(parts, read, read_sem, chunk)
     wide[...] = second[...].astype(jnp.float32)
+    first[...] = first_turned[...].T
     total[...] = jnp.zeros_like(total)
     shared = first[...]
-
-    def body(step, carry):
-        fetch(step).wait()
-        part = total[...]
-        for j in range(chunk):
-            weighted = jnp.dot(read[step, j], shared, preferred_element_type=jnp.float32)
-            part = part + weighted * wide[pl.ds(step * chunk + j, 1), :]
-        total[...] = part
-        return carry
-
-    lax.fori_loop(0, read.shape[0], body, 0)
-
-
-def weighted_call(kernel, turned, args, outs, extra=()):
-    tile_j, tile_k, tile_i = turned.shape
-    chunk = chunk_of(tile_j, 16)
-    steps = tile_j // chunk
+    for part in range(len(parts)):
+
+        def body(step, carry):
+            fetch(part, step).wait()
+            slot = part * steps + step
+            sums = total[...]
+            for j in range(chunk):
+                weighted = jnp.dot(read[slot, j], shared, preferred_element_type=jnp.float32)
+                sums = sums + weighted * wide[pl.ds(slot * chunk + j, 1), :]
+            total[...] = sums
+            return carry
+
+        lax.fori_loop(0, steps, body, 0)
+
+
+def weighted_call(kernel, parts, args, outs, extra=()):
+    count, tile_k, tile_i = parts[0].shape
+    chunk = chunk_of(count, 16)
+    slots = len(parts) * count // chunk
     rank = args[0].shape[0]
+
+    def on_parts(*refs):
+        kernel(chunk, refs[: len(parts)], *refs[len(parts) :])
+
     return kernel_call(
-        functools.partial(kernel, chunk),
-        2 * tile_i * tile_j * tile_k * rank,
-        2 * tile_i * tile_j * tile_k,
+        on_parts,
+        2 * tile_i * len(parts) * count * tile_k * rank,
+        2 * tile_i * len(parts) * count * tile_k,
         out_shape=outs,
-        in_specs=[ANY] + [VMEM] * len(args),
+        in_specs=[ANY] * len(parts) + [VMEM] * len(args),
         out_specs=(VMEM,) * len(outs),
         scratch_shapes=[
-            pltpu.VMEM((steps, chunk, tile_k, tile_i), turned.dtype),
-            pltpu.SemaphoreType.DMA((steps,)),
+            pltpu.VMEM((slots, chunk, tile_k, tile_i), parts[0].dtype),
+            pltpu.SemaphoreType.DMA((slots,)),
             *extra,
         ],
-    )(in_hbm(turned), *args)
+    )(*(in_hbm(a) for a in parts), *args)
 
 
 def cross_product(values):
@@ -218,14 +273,15 @@
     return kept + swap(sent, axis, size, mask)
 
 
-def double(values, axis, size, mask):
-    other = swap(values, axis, size, mask)
+def in_order(own, other, axis, mask):
     bit = (lax.axis_index(axis) & mask) // mask
     return jnp.where(
-        bit == 0,
-        jnp.concatenate([values, other], 0),
-        jnp.concatenate([other, values], 0),
-    )
+        bit == 0, jnp.concatenate([own, other], 0), jnp.concatenate([other, own], 0)
+    )
+
+
+def double(values, axis, size, mask):
+    return in_order(values, swap(values, axis, size, mask), axis, mask)
 
 
 def tree_sum(terms):
@@ -264,23 +320,28 @@
     for mask in masks_of(size_j):
         part = 2 * part + (lax.axis_index("ja") & mask) // mask
 
-    coupled, grams, gram_time = local_products(matrix, column_factor, second_factor, time_factor)
+    grams, gram_time, column_turned, second_near, time_near = local_grams(
+        column_factor, second_factor, time_factor
+    )
     for mask in masks_of(size_j):
         grams = halve(grams, "ja", size_j, mask)
     gram_second = grams[:, rank:]
     time_rows = lax.dynamic_slice_in_dim(gram_time, part * share, share, 0)
     grams = jnp.concatenate([grams[:, :rank], time_rows], 1)
-    for mask in masks_of(size_k):
-        grams = grams + swap(grams, "ka", size_k, mask)
+    grams = all_sum(grams, "ka", size_k)
     gram_column, time_rows = grams[:, :rank], grams[:, rank:]
     gram_column = all_sum(gram_column, "ia", size_i)
     gram_total = gram_second * time_rows + gram_column
     first_wide = first_factor.astype(f32)
     denominator = full_dot(gram_total, first_wide, ((1,), (1,)))
 
+    coupled = local_coupled(column_turned, matrix)
     for mask in reversed(masks_of(size_i)):
         coupled = halve(coupled, "ia", size_i, mask, 1)
-    slab, turned = slab_and_turn(tensor, second_factor, time_factor)
+    half = tile_j // 2
+    slab, low = slab_and_turn(tensor, second_near, time_near, 0, half)
+    slab, high = slab_and_turn(tensor, second_near, time_near, half, half, (slab,))
+    turned = (low, high)
     numerator = slab + coupled
     for mask in masks_of(size_j):
         numerator = halve(numerator, "ja", size_j, mask)
@@ -322,13 +383,15 @@
     (time_sum,) = weighted_call(
         time_kernel,
         turned,
-        (first_out, second_new),
+        (first_new, second_new),
         (jax.ShapeDtypeStruct((tile_k, rank), f32),),
-        (pltpu.VMEM((tile_j, rank), f32),),
+        (
+            pltpu.VMEM((tile_j, rank), f32),
+            pltpu.VMEM((tile_i, rank), jnp.bfloat16),
+        ),
     )
     time_sum = halve(time_sum, "ja", size_j, 1)
-    time_sum = all_sum(time_sum, "ja", size_j, 2)
-    time_sum = all_sum(time_sum, "ia", size_i)
+    time_sum = all_sum(time_sum, ("ia", "ja"), size_i * size_j, 2)
     rows = tile_k // 2
     own = lax.dynamic_slice_in_dim(
         time_factor, (lax.axis_index("ja") % 2) * rows, rows, 0

time: 94.4 us -> 93.9 us (level)
  local copies, waits for them, and re-layouts: 6.9 us -> 1.59 us
  Pallas kernels: 19 us -> 23.2 us
  starting transfers between devices: 31.6 us -> 34.6 us
  waiting for transfers between devices: 32.8 us -> 30.3 us
    unnamed x23 -> x11, local copies, waits for them, and re-layouts: 6.67 us -> 1.34 us
    pallas_call x4 -> x6, Pallas kernels: 19 us -> 23.2 us  [the longest x2 10.4 us: weighted_call(): kernel_call(on_parts, 2 * tile_i * len(parts) * count * tile_k * rank, 2...]
    ppermute x27 -> x29, starting transfers between devices: 31.6 us -> 34.6 us  [swap(): return lax.ppermute(values, axis, [(i, i ^ mask) for i in range(size)])]
    ppermute x27 -> x29, waiting for transfers between devices: 32.8 us -> 30.3 us  [swap(): return lax.ppermute(values, axis, [(i, i ^ mask) for i in range(size)])]
  transfers between devices with their start and end apart: 27 -> 29, of which waited for: 15 -> 12; matrix products, arithmetic and copies ran while one was open for 2% -> 2% of each run, Pallas kernels for 19% -> 23%
where the time goes in v2:
time: 93.9 us; the launch traced here: 93.5 us
  starting transfers between devices  34.6 us (37%)
  waiting for transfers between devices  30.3 us (32%)
  Pallas kernels  23.2 us (25%)
  matrix products  1.75 us (2%)
  local copies, waits for them, and re-layouts  1.59 us (2%)
  between operations  1.08 us (1%)
  other arithmetic  1.03 us (1%)
    ppermute x29, starting transfers between devices, swap(): return lax.ppermute(values, axis, [(i, i ^ mask) for i in range(size)])  34.6 us
    ppermute x29, waiting for transfers between devices, swap(): return lax.ppermute(values, axis, [(i, i ^ mask) for i in range(size)])  30.3 us
    pallas_call x2, Pallas kernels, weighted_call(): kernel_call(on_parts, 2 * tile_i * len(parts) * count * tile_k * rank, 2...  10.4 us
    pallas_call x2, Pallas kernels, slab_and_turn(): kernel_call(functools.partial(slab_kernel, first, chunk, steps), 2 * tile...  10.3 us
    pallas_call x1, Pallas kernels, local_grams(): kernel_call(gram_kernel, 2 * width * rank * rank, 2 * width * rank, out_s...  1.95 us
  transfers between devices with their start and end apart: 29, of which 12 were waited for; matrix products, arithmetic and copies ran while one was open for 2% of the time, Pallas kernels for 23%

profile of v2, /device:TPU:0, one launch (start us, length us, event | category | flops | bytes accessed | tf_op | source)
XLA Modules:
  0.0 93.5 jit_solution(10694241809299364186)
XLA Ops:
  0.7 2.0 %shard_map.85 = (f32[256,512]{1,0:T(8,128)S(1)}, f32[256,256]{1,0:T(8,128)S(1)}, bf16[256,1024]{1,0:T(8,128)(2,1)S(1)}, bf16[128,256]{1,0:T(8,128)(2,1)S(1)}, bf16[128,256]{1,0:T(8,128)(2,1)S(1)}) custom-call(bf16[1024,256]{1,0:T(8,128)(2,1)} %column.1, bf16[128,256]{1,0:T(8,128)(2,1)} %second.1, bf16[128,256]{1,0:T(8,128)(2,1)} %refs_3_.1), custom_call_target="tpu_custom_call" | custom-call | flops 134217728 | bytes 524288 | tf_op jit(solution)/shard_map/pallas_call | solution.py:61
  3.2 1.2 %copy-done.2 = bf16[512,1024]{1,0:T(8,128)(2,1)S(1)} copy-done((bf16[512,1024]{1,0:T(8,128)(2,1)S(1)}, bf16[512,1024]{1,0:T(8,128)(2,1)}, u32[]{:S(2)}) %copy-start.2) | copy-done | bytes 1048600
  4.9 2.6 %collective-permute-start = (f32[256,256]{1,0:T(8,128)S(1)}, f32[256,256]{1,0:T(8,128)S(1)}, u32[]{:S(2)}, u32[]{:S(2)}) collective-permute-start(f32[256,256]{1,0:T(8,128)S(1)} %constant_dynamic-slice_fusion.7), channel_id=1, source_target_pairs={{0,16},{16,0},{1,17},{17,1},{2,18},{18,2},{3,19},{19,3},{4,20},{20... | collective-permute-start | bytes 786440 | tf_op jit(solution)/shard_map/ppermute | solution.py:265
  7.5 5.1 %shard_map.86 = (f32[256,256]{1,0:T(8,128)S(1)}, bf16[64,128,256]{2,1,0:T(8,128)(2,1)}) custom-call(bf16[256,128,128]{2,1,0:T(8,128)(2,1)} %tensor.3, bf16[128,256]{1,0:T(8,128)(2,1)S(1)} %get-tuple-element.14.second, bf16[128,256]{1,0:T(8,128)(2,1)S(1)} %get-tuple-element.15.time), custom_call_target="tpu_custom_call" | custom-call | flops 1073741824 | bytes 8388608 | tf_op jit(solution)/shard_map/pallas_call | solution.py:152
  12.7 5.2 %shard_map.87 = (f32[256,256]{1,0:T(8,128)S(1)}, bf16[64,128,256]{2,1,0:T(8,128)(2,1)}) custom-call(bf16[256,128,128]{2,1,0:T(8,128)(2,1)} %tensor.3, bf16[128,256]{1,0:T(8,128)(2,1)S(1)} %get-tuple-element.14.second, bf16[128,256]{1,0:T(8,128)(2,1)S(1)} %get-tuple-element.15.time, f32[256,256]{1,0:T(8,128)S(1)} %get-tuple-element.17.refs_0_), custom_call_target="tpu_custom_call" | custom-call | flops 1073741824 | bytes 8388608 | tf_op jit(solution)/shard_map/pallas_call | solution.py:152
  18.0 1.6 %collective-permute-start.7 = (f32[64,512]{1,0:T(8,128)S(1)}, f32[64,512]{1,0:T(8,128)S(1)}, u32[]{:S(2)}, u32[]{:S(2)}) collective-permute-start(f32[64,512]{1,0:T(8,128)S(1)} %constant_dynamic-slice_fusion.3), channel_id=1, source_target_pairs={{0,8},{4,12},{8,0},{12,4},{1,9},{5,13},{9,1},{13,5},{2,10},{6,14},... | collective-permute-start | bytes 393224 | tf_op jit(solution)/shard_map/ppermute | solution.py:265
  19.7 3.9 %collective-permute-done.7 = f32[64,512]{1,0:T(8,128)S(1)} collective-permute-done((f32[64,512]{1,0:T(8,128)S(1)}, f32[64,512]{1,0:T(8,128)S(1)}, u32[]{:S(2)}, u32[]{:S(2)}) %collective-permute-start.7) | collective-permute-done | bytes 131104 | tf_op jit(solution)/shard_map/ppermute | solution.py:265
  23.8 1.6 %collective-permute-start.2 = (f32[64,256]{1,0:T(8,128)S(1)}, f32[64,256]{1,0:T(8,128)S(1)}, u32[]{:S(2)}, u32[]{:S(2)}) collective-permute-start(f32[64,256]{1,0:T(8,128)S(1)} %constant_dynamic-slice_fusion.5), channel_id=1, source_target_pairs={{0,8},{4,12},{8,0},{12,4},{1,9},{5,13},{9,1},{13,5},{2,10},{6,14},... | collective-permute-start | bytes 196616 | tf_op jit(solution)/shard_map/ppermute | solution.py:265
  25.4 2.7 %collective-permute-start.9 = (f32[64,512]{1,0:T(8,128)S(1)}, f32[64,512]{1,0:T(8,128)S(1)}, u32[]{:S(2)}, u32[]{:S(2)}) collective-permute-start(f32[64,512]{1,0:T(8,128)S(1)} %pad_maximum_fusion), channel_id=1, source_target_pairs={{0,2},{1,3},{2,0},{3,1},{4,6},{5,7},{6,4},{7,5},{8,10},{9,11},{10,... | collective-permute-start | bytes 393224 | tf_op jit(solution)/shard_map/ppermute | solution.py:265
  28.0 1.4 %collective-permute-start.10 = (f32[64,512]{1,0:T(8,128)S(1)}, f32[64,512]{1,0:T(8,128)S(1)}, u32[]{:S(2)}, u32[]{:S(2)}) collective-permute-start(f32[64,512]{1,0:T(8,128)S(1)} %pad_maximum_fusion), channel_id=1, source_target_pairs={{0,3},{1,2},{2,1},{3,0},{4,7},{5,6},{6,5},{7,4},{8,11},{9,10},{10,... | collective-permute-start | bytes 393224 | tf_op jit(solution)/shard_map/ppermute | solution.py:265
  29.6 2.9 %collective-permute-start.4 = (f32[64,256]{1,0:T(8,128)S(1)}, f32[64,256]{1,0:T(8,128)S(1)}, u32[]{:S(2)}, u32[]{:S(2)}) collective-permute-start(f32[64,256]{1,0:T(8,128)S(1)} %dynamic-slice_add_fusion.5), channel_id=1, source_target_pairs={{0,2},{1,3},{2,0},{3,1},{4,6},{5,7},{6,4},{7,5},{8,10},{9,11},{10,... | collective-permute-start | bytes 196616 | tf_op jit(solution)/shard_map/ppermute | solution.py:265
  32.5 1.4 %collective-permute-start.5 = (f32[64,256]{1,0:T(8,128)S(1)}, f32[64,256]{1,0:T(8,128)S(1)}, u32[]{:S(2)}, u32[]{:S(2)}) collective-permute-start(f32[64,256]{1,0:T(8,128)S(1)} %dynamic-slice_add_fusion.5), channel_id=1, source_target_pairs={{0,3},{1,2},{2,1},{3,0},{4,7},{5,6},{6,5},{7,4},{8,11},{9,10},{10,... | collective-permute-start | bytes 196616 | tf_op jit(solution)/shard_map/ppermute | solution.py:265
  33.8 4.4 %collective-permute-done.9 = f32[64,512]{1,0:T(8,128)S(1)} collective-permute-done((f32[64,512]{1,0:T(8,128)S(1)}, f32[64,512]{1,0:T(8,128)S(1)}, u32[]{:S(2)}, u32[]{:S(2)}) %collective-permute-start.9) | collective-permute-done | bytes 131104 | tf_op jit(solution)/shard_map/ppermute | solution.py:265
  39.4 4.8 %collective-permute-done.4 = f32[64,256]{1,0:T(8,128)S(1)} collective-permute-done((f32[64,256]{1,0:T(8,128)S(1)}, f32[64,256]{1,0:T(8,128)S(1)}, u32[]{:S(2)}, u32[]{:S(2)}) %collective-permute-start.4) | collective-permute-done | bytes 65568 | tf_op jit(solution)/shard_map/ppermute | solution.py:265
  45.0 3.4 %collective-permute-done.12 = bf16[64,256]{1,0:T(8,128)(2,1)S(1)} collective-permute-done((bf16[64,256]{1,0:T(8,128)(2,1)S(1)}, bf16[64,256]{1,0:T(8,128)(2,1)S(1)}, u32[]{:S(2)}, u32[]{:S(2)}) %collective-permute-start.12) | collective-permute-done | bytes 32800 | tf_op jit(solution)/shard_map/ppermute | solution.py:265
  48.5 4.0 %collective-permute-start.19 = (bf16[128,256]{1,0:T(8,128)(2,1)S(1)}, bf16[128,256]{1,0:T(8,128)(2,1)S(1)}, u32[]{:S(2)}, u32[]{:S(2)}) collective-permute-start(bf16[128,256]{1,0:T(8,128)(2,1)S(1)} %copy-done.1), channel_id=1, source_target_pairs={{0,1},{1,0},{2,3},{3,2},{4,5},{5,4},{6,7},{7,6},{8,9},{9,8},{10,11... | collective-permute-start | bytes 196616 | tf_op jit(solution)/shard_map/ppermute | solution.py:265
  52.6 5.5 %shard_map.89 = (f32[128,256]{1,0:T(8,128)S(1)}, bf16[256,256]{1,0:T(8,128)(2,1)}) custom-call(bf16[64,128,256]{2,1,0:T(8,128)(2,1)} %get-tuple-element.16.refs_0_, bf16[64,128,256]{2,1,0:T(8,128)(2,1)} %get-tuple-element.18.refs_1_, bf16[256,256]{1,0:T(8,128)(2,1)S(1)} %maximum_select_fusion.4.refs_2_, bf16[128,256]{1,0:T(8,128)(2,1)S(1)} %copy-done.1), custom_call_target="tpu_custom_call" | custom-call | flops 2147483648 | bytes 8388608 | tf_op jit(solution)/shard_map/pallas_call | solution.py:237
  58.8 2.3 %collective-permute-start.20 = (bf16[256,256]{1,0:T(8,128)(2,1)S(1)}, bf16[256,256]{1,0:T(8,128)(2,1)S(1)}, u32[]{:S(2)}, u32[]{:S(2)}) collective-permute-start(bf16[256,256]{1,0:T(8,128)(2,1)S(1)} %maximum_select_fusion.5), channel_id=1, source_target_pairs={{0,2},{1,3},{2,0},{3,1},{4,6},{5,7},{6,4},{7,5},{8,10},{9,11},{10,... | collective-permute-start | bytes 393224 | tf_op jit(solution)/shard_map/ppermute | solution.py:265
  61.0 1.5 %collective-permute-start.18 = (bf16[256,256]{1,0:T(8,128)(2,1)S(1)}, bf16[256,256]{1,0:T(8,128)(2,1)S(1)}, u32[]{:S(2)}, u32[]{:S(2)}) collective-permute-start(bf16[256,256]{1,0:T(8,128)(2,1)S(1)} %maximum_select_fusion.4.refs_2_), channel_id=1, source_target_pairs={{0,16},{16,0},{1,17},{17,1},{2,18},{18,2},{3,19},{19,3},{4,20},{20... | collective-permute-start | bytes 393224 | tf_op jit(solution)/shard_map/ppermute | solution.py:265
  62.5 2.9 %collective-permute-start.16 = (f32[64,256]{1,0:T(8,128)S(1)}, f32[64,256]{1,0:T(8,128)S(1)}, u32[]{:S(2)}, u32[]{:S(2)}) collective-permute-start(f32[64,256]{1,0:T(8,128)S(1)} %dynamic-slice_add_fusion.4), channel_id=1, source_target_pairs={{0,2},{1,3},{2,0},{3,1},{4,6},{5,7},{6,4},{7,5},{8,10},{9,11},{10,... | collective-permute-start | bytes 196616 | tf_op jit(solution)/shard_map/ppermute | solution.py:265
  65.4 0.7 collective-permute-start.17
  66.5 4.1 %collective-permute-done.20 = bf16[256,256]{1,0:T(8,128)(2,1)S(1)} collective-permute-done((bf16[256,256]{1,0:T(8,128)(2,1)S(1)}, bf16[256,256]{1,0:T(8,128)(2,1)S(1)}, u32[]{:S(2)}, u32[]{:S(2)}) %collective-permute-start.20) | collective-permute-done | bytes 131104 | tf_op jit(solution)/shard_map/ppermute | solution.py:265
  71.2 1.6 %collective-permute-done.16 = f32[64,256]{1,0:T(8,128)S(1)} collective-permute-done((f32[64,256]{1,0:T(8,128)S(1)}, f32[64,256]{1,0:T(8,128)S(1)}, u32[]{:S(2)}, u32[]{:S(2)}) %collective-permute-start.16) | collective-permute-done | bytes 65568 | tf_op jit(solution)/shard_map/ppermute | solution.py:265
  72.8 1.6 %collective-permute-start.21 = (bf16[64,256]{1,0:T(8,128)(2,1)S(1)}, bf16[64,256]{1,0:T(8,128)(2,1)S(1)}, u32[]{:S(2)}, u32[]{:S(2)}) collective-permute-start(bf16[64,256]{1,0:T(8,128)(2,1)S(1)} %divide_convert_fusion.1), channel_id=1, source_target_pairs={{0,16},{16,0},{1,17},{17,1},{2,18},{18,2},{3,19},{19,3},{4,20},{20... | collective-permute-start | bytes 98312 | tf_op jit(solution)/shard_map/ppermute | solution.py:265
  74.3 2.4 %collective-permute-done.21 = bf16[64,256]{1,0:T(8,128)(2,1)S(1)} collective-permute-done((bf16[64,256]{1,0:T(8,128)(2,1)S(1)}, bf16[64,256]{1,0:T(8,128)(2,1)S(1)}, u32[]{:S(2)}, u32[]{:S(2)}) %collective-permute-start.21) | collective-permute-done | bytes 32800 | tf_op jit(solution)/shard_map/ppermute | solution.py:265
  77.4 4.9 %shard_map.90 = f32[128,256]{1,0:T(8,128)S(1)} custom-call(bf16[64,128,256]{2,1,0:T(8,128)(2,1)} %get-tuple-element.16.refs_0_, bf16[64,128,256]{2,1,0:T(8,128)(2,1)} %get-tuple-element.18.refs_1_, bf16[256,256]{1,0:T(8,128)(2,1)S(1)} %maximum_select_fusion.4.refs_2_, bf16[128,256]{1,0:T(8,128)(2,1)S(1)} %maximum_select_fusion.8.refs_3_), custom_call_target="tpu_custom_call" | custom-call | flops 2147483648 | bytes 8388608 | tf_op jit(solution)/shard_map/pallas_call | solution.py:237
  83.6 1.6 %collective-permute-start.24 = (f32[64,256]{1,0:T(8,128)S(1)}, f32[64,256]{1,0:T(8,128)S(1)}, u32[]{:S(2)}, u32[]{:S(2)}) collective-permute-start(f32[64,256]{1,0:T(8,128)S(1)} %dynamic-slice_add_fusion.3), channel_id=1, source_target_pairs={{0,16},{4,20},{8,24},{12,28},{16,0},{20,4},{24,8},{28,12},{1,17},{... | collective-permute-start | bytes 196616 | tf_op jit(solution)/shard_map/ppermute | solution.py:265
  85.2 1.5 %collective-permute-start.25 = (f32[64,256]{1,0:T(8,128)S(1)}, f32[64,256]{1,0:T(8,128)S(1)}, u32[]{:S(2)}, u32[]{:S(2)}) collective-permute-start(f32[64,256]{1,0:T(8,128)S(1)} %dynamic-slice_add_fusion.3), channel_id=1, source_target_pairs={{0,24},{4,28},{8,16},{12,20},{16,8},{20,12},{24,0},{28,4},{1,25},{... | collective-permute-start | bytes 196616 | tf_op jit(solution)/shard_map/ppermute | solution.py:265
  88.0 2.5 %collective-permute-done.25 = f32[64,256]{1,0:T(8,128)S(1)} collective-permute-done((f32[64,256]{1,0:T(8,128)S(1)}, f32[64,256]{1,0:T(8,128)S(1)}, u32[]{:S(2)}, u32[]{:S(2)}) %collective-permute-start.25) | collective-permute-done | bytes 65568 | tf_op jit(solution)/shard_map/ppermute | solution.py:265
  90.4 1.1 %collective-permute-done.23 = f32[64,256]{1,0:T(8,128)S(1)} collective-permute-done((f32[64,256]{1,0:T(8,128)S(1)}, f32[64,256]{1,0:T(8,128)S(1)}, u32[]{:S(2)}, u32[]{:S(2)}) %collective-permute-start.23) | collective-permute-done | bytes 65568 | tf_op jit(solution)/shard_map/ppermute | solution.py:265
  91.7 1.2 %collective-permute-done.28 = bf16[64,256]{1,0:T(8,128)(2,1)S(1)} collective-permute-done((bf16[64,256]{1,0:T(8,128)(2,1)S(1)}, bf16[64,256]{1,0:T(8,128)(2,1)S(1)}, u32[]{:S(2)}, u32[]{:S(2)}) %collective-permute-start.28) | collective-permute-done | bytes 32800 | tf_op jit(solution)/shard_map/ppermute | solution.py:265
  92.9 0.6 maximum_select_fusion.9
  (78 shorter events, 8.7 us)
Async XLA Ops:
  0.6 38.6 %copy-start = (bf16[256,256]{1,0:T(8,128)(2,1)S(1)}, bf16[256,256]{1,0:T(8,128)(2,1)}, u32[]{:S(2)}) copy-start(bf16[256,256]{1,0:T(8,128)(2,1)} %param.8) | copy-start | bytes 393220
  2.7 15.3 %collective-permute-start.6 = (f32[128,512]{1,0:T(8,128)S(1)}, f32[128,512]{1,0:T(8,128)S(1)}, u32[]{:S(2)}, u32[]{:S(2)}) collective-permute-start(f32[128,512]{1,0:T(8,128)S(1)} %constant_dynamic-slice_fusion.4), channel_id=1, source_target_pairs={{0,4},{4,0},{8,12},{12,8},{1,5},{5,1},{9,13},{13,9},{2,6},{6,2},{1... | collective-permute-start | bytes 786440 | tf_op jit(solution)/shard_map/ppermute | solution.py:265
  4.9 14.6 %collective-permute-start = (f32[256,256]{1,0:T(8,128)S(1)}, f32[256,256]{1,0:T(8,128)S(1)}, u32[]{:S(2)}, u32[]{:S(2)}) collective-permute-start(f32[256,256]{1,0:T(8,128)S(1)} %constant_dynamic-slice_fusion.7), channel_id=1, source_target_pairs={{0,16},{16,0},{1,17},{17,1},{2,18},{18,2},{3,19},{19,3},{4,20},{20... | collective-permute-start | bytes 786440 | tf_op jit(solution)/shard_map/ppermute | solution.py:265
  17.9 30.6 %copy-start.1 = (bf16[128,256]{1,0:T(8,128)(2,1)S(1)}, bf16[128,256]{1,0:T(8,128)(2,1)}, u32[]{:S(2)}) copy-start(bf16[128,256]{1,0:T(8,128)(2,1)} %refs_3_.1) | copy-start | bytes 196612
  18.0 5.7 %collective-permute-start.7 = (f32[64,512]{1,0:T(8,128)S(1)}, f32[64,512]{1,0:T(8,128)S(1)}, u32[]{:S(2)}, u32[]{:S(2)}) collective-permute-start(f32[64,512]{1,0:T(8,128)S(1)} %constant_dynamic-slice_fusion.3), channel_id=1, source_target_pairs={{0,8},{4,12},{8,0},{12,4},{1,9},{5,13},{9,1},{13,5},{2,10},{6,14},... | collective-permute-start | bytes 393224 | tf_op jit(solution)/shard_map/ppermute | solution.py:265
  19.7 4.0 %collective-permute-start.1 = (f32[128,256]{1,0:T(8,128)S(1)}, f32[128,256]{1,0:T(8,128)S(1)}, u32[]{:S(2)}, u32[]{:S(2)}) collective-permute-start(f32[128,256]{1,0:T(8,128)S(1)} %constant_dynamic-slice_fusion.6), channel_id=1, source_target_pairs={{0,4},{4,0},{8,12},{12,8},{1,5},{5,1},{9,13},{13,9},{2,6},{6,2},{1... | collective-permute-start | bytes 393224 | tf_op jit(solution)/shard_map/ppermute | solution.py:265
  23.8 5.8 %collective-permute-start.2 = (f32[64,256]{1,0:T(8,128)S(1)}, f32[64,256]{1,0:T(8,128)S(1)}, u32[]{:S(2)}, u32[]{:S(2)}) collective-permute-start(f32[64,256]{1,0:T(8,128)S(1)} %constant_dynamic-slice_fusion.5), channel_id=1, source_target_pairs={{0,8},{4,12},{8,0},{12,4},{1,9},{5,13},{9,1},{13,5},{2,10},{6,14},... | collective-permute-start | bytes 196616 | tf_op jit(solution)/shard_map/ppermute | solution.py:265
  25.4 12.9 %collective-permute-start.9 = (f32[64,512]{1,0:T(8,128)S(1)}, f32[64,512]{1,0:T(8,128)S(1)}, u32[]{:S(2)}, u32[]{:S(2)}) collective-permute-start(f32[64,512]{1,0:T(8,128)S(1)} %pad_maximum_fusion), channel_id=1, source_target_pairs={{0,2},{1,3},{2,0},{3,1},{4,6},{5,7},{6,4},{7,5},{8,10},{9,11},{10,... | collective-permute-start | bytes 393224 | tf_op jit(solution)/shard_map/ppermute | solution.py:265
  28.0 10.5 %collective-permute-start.10 = (f32[64,512]{1,0:T(8,128)S(1)}, f32[64,512]{1,0:T(8,128)S(1)}, u32[]{:S(2)}, u32[]{:S(2)}) collective-permute-start(f32[64,512]{1,0:T(8,128)S(1)} %pad_maximum_fusion), channel_id=1, source_target_pairs={{0,3},{1,2},{2,1},{3,0},{4,7},{5,6},{6,5},{7,4},{8,11},{9,10},{10,... | collective-permute-start | bytes 393224 | tf_op jit(solution)/shard_map/ppermute | solution.py:265
  29.4 9.2 %collective-permute-start.8 = (f32[64,512]{1,0:T(8,128)S(1)}, f32[64,512]{1,0:T(8,128)S(1)}, u32[]{:S(2)}, u32[]{:S(2)}) collective-permute-start(f32[64,512]{1,0:T(8,128)S(1)} %pad_maximum_fusion), channel_id=1, source_target_pairs={{0,1},{1,0},{2,3},{3,2},{4,5},{5,4},{6,7},{7,6},{8,9},{9,8},{10,11... | collective-permute-start | bytes 393224 | tf_op jit(solution)/shard_map/ppermute | solution.py:265
  29.6 14.5 %collective-permute-start.4 = (f32[64,256]{1,0:T(8,128)S(1)}, f32[64,256]{1,0:T(8,128)S(1)}, u32[]{:S(2)}, u32[]{:S(2)}) collective-permute-start(f32[64,256]{1,0:T(8,128)S(1)} %dynamic-slice_add_fusion.5), channel_id=1, source_target_pairs={{0,2},{1,3},{2,0},{3,1},{4,6},{5,7},{6,4},{7,5},{8,10},{9,11},{10,... | collective-permute-start | bytes 196616 | tf_op jit(solution)/shard_map/ppermute | solution.py:265
  32.5 11.7 %collective-permute-start.5 = (f32[64,256]{1,0:T(8,128)S(1)}, f32[64,256]{1,0:T(8,128)S(1)}, u32[]{:S(2)}, u32[]{:S(2)}) collective-permute-start(f32[64,256]{1,0:T(8,128)S(1)} %dynamic-slice_add_fusion.5), channel_id=1, source_target_pairs={{0,3},{1,2},{2,1},{3,0},{4,7},{5,6},{6,5},{7,4},{8,11},{9,10},{10,... | collective-permute-start | bytes 196616 | tf_op jit(solution)/shard_map/ppermute | solution.py:265
  38.2 5.9 %collective-permute-start.3 = (f32[64,256]{1,0:T(8,128)S(1)}, f32[64,256]{1,0:T(8,128)S(1)}, u32[]{:S(2)}, u32[]{:S(2)}) collective-permute-start(f32[64,256]{1,0:T(8,128)S(1)} %dynamic-slice_add_fusion.5), channel_id=1, source_target_pairs={{0,1},{1,0},{2,3},{3,2},{4,5},{5,4},{6,7},{7,6},{8,9},{9,8},{10,11... | collective-permute-start | bytes 196616 | tf_op jit(solution)/shard_map/ppermute | solution.py:265
  38.6 5.6 %collective-permute-start.11 = (f32[64,256]{1,0:T(8,128)S(1)}, f32[64,256]{1,0:T(8,128)S(1)}, u32[]{:S(2)}, u32[]{:S(2)}) collective-permute-start(f32[64,256]{1,0:T(8,128)S(1)} %slice.19), channel_id=1, source_target_pairs={{0,16},{16,0},{1,17},{17,1},{2,18},{18,2},{3,19},{19,3},{4,20},{20... | collective-permute-start | bytes 196616 | tf_op jit(solution)/shard_map/ppermute | solution.py:265
  44.4 4.0 %collective-permute-start.12 = (bf16[64,256]{1,0:T(8,128)(2,1)S(1)}, bf16[64,256]{1,0:T(8,128)(2,1)S(1)}, u32[]{:S(2)}, u32[]{:S(2)}) collective-permute-start(bf16[64,256]{1,0:T(8,128)(2,1)S(1)} %fusion.17), channel_id=1, source_target_pairs={{0,8},{4,12},{8,0},{12,4},{1,9},{5,13},{9,1},{13,5},{2,10},{6,14},... | collective-permute-start | bytes 98312 | tf_op jit(solution)/shard_map/ppermute | solution.py:265
  48.4 4.1 %collective-permute-start.13 = (bf16[128,256]{1,0:T(8,128)(2,1)S(1)}, bf16[128,256]{1,0:T(8,128)(2,1)S(1)}, u32[]{:S(2)}, u32[]{:S(2)}) collective-permute-start(bf16[128,256]{1,0:T(8,128)(2,1)S(1)} %maximum_select_fusion.7), channel_id=1, source_target_pairs={{0,4},{4,0},{8,12},{12,8},{1,5},{5,1},{9,13},{13,9},{2,6},{6,2},{1... | collective-permute-start | bytes 196616 | tf_op jit(solution)/shard_map/ppermute | solution.py:265
  48.5 10.2 %collective-permute-start.19 = (bf16[128,256]{1,0:T(8,128)(2,1)S(1)}, bf16[128,256]{1,0:T(8,128)(2,1)S(1)}, u32[]{:S(2)}, u32[]{:S(2)}) collective-permute-start(bf16[128,256]{1,0:T(8,128)(2,1)S(1)} %copy-done.1), channel_id=1, source_target_pairs={{0,1},{1,0},{2,3},{3,2},{4,5},{5,4},{6,7},{7,6},{8,9},{9,8},{10,11... | collective-permute-start | bytes 196616 | tf_op jit(solution)/shard_map/ppermute | solution.py:265
  52.6 18.4 %copy-start.4 = (bf16[128,256]{1,0:T(8,128)(2,1)S(1)}, bf16[128,256]{1,0:T(8,128)(2,1)}, u32[]{:S(2)}) copy-start(bf16[128,256]{1,0:T(8,128)(2,1)} %second.1) | copy-start | bytes 196612
  58.1 4.4 %collective-permute-start.14 = (f32[64,256]{1,0:T(8,128)S(1)}, f32[64,256]{1,0:T(8,128)S(1)}, u32[]{:S(2)}, u32[]{:S(2)}) collective-permute-start(f32[64,256]{1,0:T(8,128)S(1)} %constant_dynamic-slice_fusion.1), channel_id=1, source_target_pairs={{0,16},{16,0},{1,17},{17,1},{2,18},{18,2},{3,19},{19,3},{4,20},{20... | collective-permute-start | bytes 196616 | tf_op jit(solution)/shard_map/ppermute | solution.py:265
  58.8 11.9 %collective-permute-start.20 = (bf16[256,256]{1,0:T(8,128)(2,1)S(1)}, bf16[256,256]{1,0:T(8,128)(2,1)S(1)}, u32[]{:S(2)}, u32[]{:S(2)}) collective-permute-start(bf16[256,256]{1,0:T(8,128)(2,1)S(1)} %maximum_select_fusion.5), channel_id=1, source_target_pairs={{0,2},{1,3},{2,0},{3,1},{4,6},{5,7},{6,4},{7,5},{8,10},{9,11},{10,... | collective-permute-start | bytes 393224 | tf_op jit(solution)/shard_map/ppermute | solution.py:265
  61.0 5.1 %collective-permute-start.18 = (bf16[256,256]{1,0:T(8,128)(2,1)S(1)}, bf16[256,256]{1,0:T(8,128)(2,1)S(1)}, u32[]{:S(2)}, u32[]{:S(2)}) collective-permute-start(bf16[256,256]{1,0:T(8,128)(2,1)S(1)} %maximum_select_fusion.4.refs_2_), channel_id=1, source_target_pairs={{0,16},{16,0},{1,17},{17,1},{2,18},{18,2},{3,19},{19,3},{4,20},{20... | collective-permute-start | bytes 393224 | tf_op jit(solution)/shard_map/ppermute | solution.py:265
  62.5 10.2 %collective-permute-start.16 = (f32[64,256]{1,0:T(8,128)S(1)}, f32[64,256]{1,0:T(8,128)S(1)}, u32[]{:S(2)}, u32[]{:S(2)}) collective-permute-start(f32[64,256]{1,0:T(8,128)S(1)} %dynamic-slice_add_fusion.4), channel_id=1, source_target_pairs={{0,2},{1,3},{2,0},{3,1},{4,6},{5,7},{6,4},{7,5},{8,10},{9,11},{10,... | collective-permute-start | bytes 196616 | tf_op jit(solution)/shard_map/ppermute | solution.py:265
  65.4 7.3 %collective-permute-start.17 = (f32[64,256]{1,0:T(8,128)S(1)}, f32[64,256]{1,0:T(8,128)S(1)}, u32[]{:S(2)}, u32[]{:S(2)}) collective-permute-start(f32[64,256]{1,0:T(8,128)S(1)} %dynamic-slice_add_fusion.4), channel_id=1, source_target_pairs={{0,3},{1,2},{2,1},{3,0},{4,7},{5,6},{6,5},{7,4},{8,11},{9,10},{10,... | collective-permute-start | bytes 196616 | tf_op jit(solution)/shard_map/ppermute | solution.py:265
  66.1 6.7 %collective-permute-start.15 = (f32[64,256]{1,0:T(8,128)S(1)}, f32[64,256]{1,0:T(8,128)S(1)}, u32[]{:S(2)}, u32[]{:S(2)}) collective-permute-start(f32[64,256]{1,0:T(8,128)S(1)} %dynamic-slice_add_fusion.4), channel_id=1, source_target_pairs={{0,1},{1,0},{2,3},{3,2},{4,5},{5,4},{6,7},{7,6},{8,9},{9,8},{10,11... | collective-permute-start | bytes 196616 | tf_op jit(solution)/shard_map/ppermute | solution.py:265
  72.8 4.0 %collective-permute-start.21 = (bf16[64,256]{1,0:T(8,128)(2,1)S(1)}, bf16[64,256]{1,0:T(8,128)(2,1)S(1)}, u32[]{:S(2)}, u32[]{:S(2)}) collective-permute-start(bf16[64,256]{1,0:T(8,128)(2,1)S(1)} %divide_convert_fusion.1), channel_id=1, source_target_pairs={{0,16},{16,0},{1,17},{17,1},{2,18},{18,2},{3,19},{19,3},{4,20},{20... | collective-permute-start | bytes 98312 | tf_op jit(solution)/shard_map/ppermute | solution.py:265
  76.8 5.6 %collective-permute-start.26 = (bf16[128,256]{1,0:T(8,128)(2,1)S(1)}, bf16[128,256]{1,0:T(8,128)(2,1)S(1)}, u32[]{:S(2)}, u32[]{:S(2)}) collective-permute-start(bf16[128,256]{1,0:T(8,128)(2,1)S(1)} %maximum_select_fusion.8.refs_3_), channel_id=1, source_target_pairs={{0,8},{4,12},{8,0},{12,4},{1,9},{5,13},{9,1},{13,5},{2,10},{6,14},... | collective-permute-start | bytes 196616 | tf_op jit(solution)/shard_map/ppermute | solution.py:265
  82.3 1.3 %collective-permute-start.22 = (f32[64,256]{1,0:T(8,128)S(1)}, f32[64,256]{1,0:T(8,128)S(1)}, u32[]{:S(2)}, u32[]{:S(2)}) collective-permute-start(f32[64,256]{1,0:T(8,128)S(1)} %constant_dynamic-slice_fusion), channel_id=1, source_target_pairs={{0,4},{4,0},{8,12},{12,8},{1,5},{5,1},{9,13},{13,9},{2,6},{6,2},{1... | collective-permute-start | bytes 196616 | tf_op jit(solution)/shard_map/ppermute | solution.py:265
  82.4 4.8 %collective-permute-start.27 = (bf16[256,256]{1,0:T(8,128)(2,1)S(1)}, bf16[256,256]{1,0:T(8,128)(2,1)S(1)}, u32[]{:S(2)}, u32[]{:S(2)}) collective-permute-start(bf16[256,256]{1,0:T(8,128)(2,1)S(1)} %maximum_select_fusion.6), channel_id=1, source_target_pairs={{0,4},{4,0},{8,12},{12,8},{1,5},{5,1},{9,13},{13,9},{2,6},{6,2},{1... | collective-permute-start | bytes 393224 | tf_op jit(solution)/shard_map/ppermute | solution.py:265
  83.6 4.3 %collective-permute-start.24 = (f32[64,256]{1,0:T(8,128)S(1)}, f32[64,256]{1,0:T(8,128)S(1)}, u32[]{:S(2)}, u32[]{:S(2)}) collective-permute-start(f32[64,256]{1,0:T(8,128)S(1)} %dynamic-slice_add_fusion.3), channel_id=1, source_target_pairs={{0,16},{4,20},{8,24},{12,28},{16,0},{20,4},{24,8},{28,12},{1,17},{... | collective-permute-start | bytes 196616 | tf_op jit(solution)/shard_map/ppermute | solution.py:265
  85.2 5.2 %collective-permute-start.25 = (f32[64,256]{1,0:T(8,128)S(1)}, f32[64,256]{1,0:T(8,128)S(1)}, u32[]{:S(2)}, u32[]{:S(2)}) collective-permute-start(f32[64,256]{1,0:T(8,128)S(1)} %dynamic-slice_add_fusion.3), channel_id=1, source_target_pairs={{0,24},{4,28},{8,16},{12,20},{16,8},{20,12},{24,0},{28,4},{1,25},{... | collective-permute-start | bytes 196616 | tf_op jit(solution)/shard_map/ppermute | solution.py:265
  86.7 4.8 %collective-permute-start.23 = (f32[64,256]{1,0:T(8,128)S(1)}, f32[64,256]{1,0:T(8,128)S(1)}, u32[]{:S(2)}, u32[]{:S(2)}) collective-permute-start(f32[64,256]{1,0:T(8,128)S(1)} %dynamic-slice_add_fusion.3), channel_id=1, source_target_pairs={{0,8},{4,12},{8,0},{12,4},{16,24},{20,28},{24,16},{28,20},{1,9},{5... | collective-permute-start | bytes 196616 | tf_op jit(solution)/shard_map/ppermute | solution.py:265
  91.6 1.3 %collective-permute-start.28 = (bf16[64,256]{1,0:T(8,128)(2,1)S(1)}, bf16[64,256]{1,0:T(8,128)(2,1)S(1)}, u32[]{:S(2)}, u32[]{:S(2)}) collective-permute-start(bf16[64,256]{1,0:T(8,128)(2,1)S(1)} %divide_convert_fusion), channel_id=1, source_target_pairs={{0,4},{4,0},{8,12},{12,8},{1,5},{5,1},{9,13},{13,9},{2,6},{6,2},{1... | collective-permute-start | bytes 98312 | tf_op jit(solution)/shard_map/ppermute | solution.py:265
  (2 other events, 6.8 us)

commit v3 on v2

--- a/solution.py
+++ b/solution.py
@@ -42,9 +42,13 @@
     return lambda index: copy(index).wait()
 
 
-def gram_kernel(column, second, time, grams, gram_time, turned, second_out, time_out, held, sem):
+def local_kernel(
+    column, second, time, matrix, grams, gram_time, coupled, second_out, time_out, *scratch
+):
     f32 = jnp.float32
-    wait = bring((column, second, time), (held, second_out, time_out), sem)
+    held, held_matrix, turned, sem = scratch
+    targets = (held, second_out, time_out, held_matrix)
+    wait = bring((column, second, time, matrix), targets, sem)
     rank = column.shape[1]
     wait(0)
     turned[...] = held[...].T
@@ -53,48 +57,36 @@
     grams[:, rank:] = jnp.dot(second_out[...].T, second_out[...], preferred_element_type=f32)
     wait(2)
     gram_time[...] = jnp.dot(time_out[...].T, time_out[...], preferred_element_type=f32)
-
-
-def local_grams(column, second, time):
+    wait(3)
+    coupled[...] = lax.dot_general(
+        turned[...], held_matrix[...], (((1,), (1,)), ((), ())), preferred_element_type=f32
+    )
+
+
+def local_products(column, second, time, matrix):
     width, rank = column.shape
+    rows = matrix.shape[0]
     f32 = jnp.float32
     return kernel_call(
-        gram_kernel,
-        2 * width * rank * rank,
-        2 * width * rank,
+        local_kernel,
+        2 * width * rank * (rank + rows),
+        2 * width * (rank + rows),
         out_shape=(
             jax.ShapeDtypeStruct((rank, 2 * rank), f32),
             jax.ShapeDtypeStruct((rank, rank), f32),
-            jax.ShapeDtypeStruct((rank, width), column.dtype),
+            jax.ShapeDtypeStruct((rank, rows), f32),
             jax.ShapeDtypeStruct(second.shape, second.dtype),
             jax.ShapeDtypeStruct(time.shape, time.dtype),
         ),
-        in_specs=[ANY] * 3,
+        in_specs=[ANY] * 4,
         out_specs=(VMEM,) * 5,
         scratch_shapes=[
             pltpu.VMEM(column.shape, column.dtype),
-            pltpu.SemaphoreType.DMA((3,)),
+            pltpu.VMEM(matrix.shape, matrix.dtype),
+            pltpu.VMEM((rank, width), column.dtype),
+            pltpu.SemaphoreType.DMA((4,)),
         ],
-    )(*(in_hbm(a) for a in (column, second, time)))
-
-
-def coupled_kernel(turned, matrix, coupled):
-    coupled[...] = lax.dot_general(
-        turned[...], matrix[...], (((1,), (1,)), ((), ())), preferred_element_type=jnp.float32
-    )
-
-
-def local_coupled(turned, matrix):
-    rank, width = turned.shape
-    rows = matrix.shape[0]
-    return kernel_call(
-        coupled_kernel,
-        2 * width * rank * rows,
-        2 * width * (rows + rank),
-        out_shape=jax.ShapeDtypeStruct((rank, rows), jnp.float32),
-        in_specs=[VMEM] * 2,
-        out_specs=VMEM,
-    )(turned, matrix)
+    )(*(in_hbm(a) for a in (column, second, time, matrix)))
 
 
 def slab_kernel(first, chunk, steps, tensor, second, time, *refs):
@@ -302,6 +294,27 @@
     return tree_sum(spread(values, axis, size, step))
 
 
+def share_sum(values, axis, size):
+    rows = values.shape[0] // size
+    own = lax.axis_index(axis)
+
+    def share(index):
+        return lax.dynamic_slice_in_dim(values, index * rows, rows, 0)
+
+    return tree_sum(
+        [share(own)] + [swap(share(own ^ d), axis, size, d) for d in range(1, size)]
+    )
+
+
+def collect(values, axis, size):
+    pieces = spread(values, axis, size)
+    for mask in masks_of(size):
+        pieces = [
+            in_order(pieces[i], pieces[i + 1], axis, mask) for i in range(0, len(pieces), 2)
+        ]
+    return pieces[0]
+
+
 def full_dot(left, right, dims):
     return lax.dot_general(
         left, right, (dims, ((), ())), precision=lax.Precision.HIGHEST,
@@ -315,27 +328,27 @@
     f32 = jnp.float32
     tile_i, tile_j, tile_k = tensor.shape
     rank = first_factor.shape[1]
-    share = rank // size_j
-    part = 0
-    for mask in masks_of(size_j):
-        part = 2 * part + (lax.axis_index("ja") & mask) // mask
-
-    grams, gram_time, column_turned, second_near, time_near = local_grams(
-        column_factor, second_factor, time_factor
-    )
-    for mask in masks_of(size_j):
-        grams = halve(grams, "ja", size_j, mask)
-    gram_second = grams[:, rank:]
-    time_rows = lax.dynamic_slice_in_dim(gram_time, part * share, share, 0)
-    grams = jnp.concatenate([grams[:, :rank], time_rows], 1)
-    grams = all_sum(grams, "ka", size_k)
-    gram_column, time_rows = grams[:, :rank], grams[:, rank:]
+    half_rank = rank // 2
+    share = half_rank // size_k
+    core = lax.axis_index("ja") % 2
+    along = lax.axis_index("ka") * share
+    part = core * half_rank + along
+
+    grams, gram_time, coupled, second_near, time_near = local_products(
+        column_factor, second_factor, time_factor, matrix
+    )
+    grams = halve(grams, "ja", size_j, 1)
+    gram_second = lax.dynamic_slice_in_dim(grams[:, rank:], along, share, 0)
+    time_rows = lax.dynamic_slice_in_dim(gram_time, core * half_rank, half_rank, 0)
+    grams = share_sum(jnp.concatenate([grams[:, :rank], time_rows], 1), "ka", size_k)
+    time_rows = grams[:, rank:]
+    grams = all_sum(jnp.concatenate([grams[:, :rank], gram_second], 1), "ja", size_j, 2)
+    gram_column, gram_second = grams[:, :rank], grams[:, rank:]
     gram_column = all_sum(gram_column, "ia", size_i)
     gram_total = gram_second * time_rows + gram_column
     first_wide = first_factor.astype(f32)
     denominator = full_dot(gram_total, first_wide, ((1,), (1,)))
 
-    coupled = local_coupled(column_turned, matrix)
     for mask in reversed(masks_of(size_i)):
         coupled = halve(coupled, "ia", size_i, mask, 1)
     half = tile_j // 2
@@ -343,13 +356,13 @@
     slab, high = slab_and_turn(tensor, second_near, time_near, half, half, (slab,))
     turned = (low, high)
     numerator = slab + coupled
-    for mask in masks_of(size_j):
-        numerator = halve(numerator, "ja", size_j, mask)
-    numerator = all_sum(numerator, "ka", size_k)
-    own = lax.dynamic_slice_in_dim(first_wide.T, part * share, share, 0)
+    numerator = halve(numerator, "ja", size_j, 1)
+    numerator = share_sum(numerator, "ka", size_k)
+    numerator = all_sum(numerator, "ja", size_j, 2)
+    own = lax.dynamic_slice_in_dim(first_wide.T, part, share, 0)
     first_new = (own * numerator / denominator).astype(jnp.bfloat16)
-    for mask in reversed(masks_of(size_j)):
-        first_new = double(first_new, "ja", size_j, mask)
+    first_new = collect(first_new, "ka", size_k)
+    first_new = double(first_new, "ja", size_j, 1)
 
     firsts = spread(first_new, "ia", size_i)
     gram_first = tree_sum([row_product(piece) for piece in firsts])
@@ -366,15 +379,13 @@
             jax.ShapeDtypeStruct((tile_i, rank), jnp.bfloat16),
         ),
     )
-    for mask in reversed(masks_of(size_i)):
-        plane_sum = halve(plane_sum, "ia", size_i, mask)
-    plane_sum = all_sum(plane_sum, "ka", size_k)
-    rows = tile_j // size_i
-    own = lax.dynamic_slice_in_dim(second_factor, lax.axis_index("ia") * rows, rows, 0).astype(f32)
+    plane_sum = share_sum(plane_sum, "ka", size_k)
+    plane_sum = all_sum(plane_sum, "ia", size_i)
+    rows = tile_j // size_k
+    own = lax.dynamic_slice_in_dim(second_factor, lax.axis_index("ka") * rows, rows, 0).astype(f32)
     denominator = full_dot(own, gram_first * gram_time, ((1,), (0,)))
     second_new = (own * plane_sum / denominator).astype(jnp.bfloat16)
-    for mask in masks_of(size_i):
-        second_new = double(second_new, "ia", size_i, mask)
+    second_new = collect(second_new, "ka", size_k)
 
     seconds = second_new
     for mask in reversed(masks_of(size_j)):

time: 93.9 us -> 96.1 us (1.023)
  waiting for transfers between devices: 30.3 us -> 33.8 us
  local copies, waits for them, and re-layouts: 1.59 us -> 0.35 us
    ppermute x29 -> x33, waiting for transfers between devices: 30.3 us -> 33.8 us  [swap(): return lax.ppermute(values, axis, [(i, i ^ mask) for i in range(size)])]
    unnamed x11 -> x9, local copies, waits for them, and re-layouts: 1.34 us -> 0.1 us
    ppermute x29 -> x33, starting transfers between devices: 34.6 us -> 34.5 us  [swap(): return lax.ppermute(values, axis, [(i, i ^ mask) for i in range(size)])]
    pallas_call x2 -> x1, Pallas kernels: 2.42 us -> 2.44 us  [local_products(): kernel_call(local_kernel, 2 * width * rank * (rank + rows), 2 * width * (...]
  transfers between devices with their start and end apart: 29 -> 33, of which waited for: 12 -> 19; matrix products, arithmetic and copies ran while one was open for 2% -> 2% of each run, Pallas kernels for 23% -> 17%
where the time goes in v3:
time: 96.1 us; the launch traced here: 95.8 us
  starting transfers between devices  34.5 us (36%)
  waiting for transfers between devices  33.8 us (35%)
  Pallas kernels  23.2 us (24%)
  matrix products  1.72 us (2%)
  between operations  1.17 us (1%)
  other arithmetic  1.06 us (1%)
    ppermute x33, starting transfers between devices, swap(): return lax.ppermute(values, axis, [(i, i ^ mask) for i in range(size)])  34.5 us
    ppermute x33, waiting for transfers between devices, swap(): return lax.ppermute(values, axis, [(i, i ^ mask) for i in range(size)])  33.8 us
    pallas_call x2, Pallas kernels, weighted_call(): kernel_call(on_parts, 2 * tile_i * len(parts) * count * tile_k * rank, 2...  10.5 us
    pallas_call x2, Pallas kernels, slab_and_turn(): kernel_call(functools.partial(slab_kernel, first, chunk, steps), 2 * tile...  10.3 us
    pallas_call x1, Pallas kernels, local_products(): kernel_call(local_kernel, 2 * width * rank * (rank + rows), 2 * width * (...  2.44 us
  transfers between devices with their start and end apart: 33, of which 19 were waited for; matrix products, arithmetic and copies ran while one was open for 2% of the time, Pallas kernels for 17%

profile of v3, /device:TPU:0, one launch (start us, length us, event | category | flops | bytes accessed | tf_op | source)
XLA Modules:
  0.0 95.8 jit_solution(2398216377152651925)
XLA Ops:
  0.7 2.4 %shard_map.85 = (f32[256,512]{1,0:T(8,128)S(1)}, f32[256,256]{1,0:T(8,128)S(1)}, f32[256,512]{1,0:T(8,128)S(1)}, bf16[128,256]{1,0:T(8,128)(2,1)S(1)}, bf16[128,256]{1,0:T(8,128)(2,1)S(1)}) custom-call(bf16[1024,256]{1,0:T(8,128)(2,1)} %column.1, bf16[128,256]{1,0:T(8,128)(2,1)} %second.1, bf16[128,256]{1,0:T(8,128)(2,1)} %refs_3_.1, bf16[512,1024]{1,0:T(8,128)(2,1)} %matrix.1), custom_call_target="tpu_custom_call" | custom-call | flops 402653184 | bytes 1572864 | tf_op jit(solution)/shard_map/pallas_call | solution.py:70
  3.7 2.6 %collective-permute-start = (f32[256,256]{1,0:T(8,128)S(1)}, f32[256,256]{1,0:T(8,128)S(1)}, u32[]{:S(2)}, u32[]{:S(2)}) collective-permute-start(f32[256,256]{1,0:T(8,128)S(1)} %constant_dynamic-slice_fusion.11), channel_id=1, source_target_pairs={{0,16},{16,0},{1,17},{17,1},{2,18},{18,2},{3,19},{19,3},{4,20},{20... | collective-permute-start | bytes 786440 | tf_op jit(solution)/shard_map/ppermute | solution.py:257
  6.3 5.1 %shard_map.86 = (f32[256,256]{1,0:T(8,128)S(1)}, bf16[64,128,256]{2,1,0:T(8,128)(2,1)}) custom-call(bf16[256,128,128]{2,1,0:T(8,128)(2,1)} %tensor.3, bf16[128,256]{1,0:T(8,128)(2,1)S(1)} %get-tuple-element.14.second, bf16[128,256]{1,0:T(8,128)(2,1)S(1)} %get-tuple-element.15.time), custom_call_target="tpu_custom_call" | custom-call | flops 1073741824 | bytes 8388608 | tf_op jit(solution)/shard_map/pallas_call | solution.py:144
  11.5 5.2 %shard_map.87 = (f32[256,256]{1,0:T(8,128)S(1)}, bf16[64,128,256]{2,1,0:T(8,128)(2,1)}) custom-call(bf16[256,128,128]{2,1,0:T(8,128)(2,1)} %tensor.3, bf16[128,256]{1,0:T(8,128)(2,1)S(1)} %get-tuple-element.14.second, bf16[128,256]{1,0:T(8,128)(2,1)S(1)} %get-tuple-element.15.time, f32[256,256]{1,0:T(8,128)S(1)} %get-tuple-element.17.refs_0_), custom_call_target="tpu_custom_call" | custom-call | flops 1073741824 | bytes 8388608 | tf_op jit(solution)/shard_map/pallas_call | solution.py:144
  16.8 3.7 %collective-permute-start.9 = (f32[32,512]{1,0:T(8,128)S(1)}, f32[32,512]{1,0:T(8,128)S(1)}, u32[]{:S(2)}, u32[]{:S(2)}) collective-permute-start(f32[32,512]{1,0:T(8,128)S(1)} %get-tuple-element.27), channel_id=1, source_target_pairs={{0,3},{1,2},{2,1},{3,0},{4,7},{5,6},{6,5},{7,4},{8,11},{9,10},{10,... | collective-permute-start | bytes 196616 | tf_op jit(solution)/shard_map/ppermute | solution.py:257
  21.4 2.2 %collective-permute-done.9 = f32[32,512]{1,0:T(8,128)S(1)} collective-permute-done((f32[32,512]{1,0:T(8,128)S(1)}, f32[32,512]{1,0:T(8,128)S(1)}, u32[]{:S(2)}, u32[]{:S(2)}) %collective-permute-start.9) | collective-permute-done | bytes 65568 | tf_op jit(solution)/shard_map/ppermute | solution.py:257
  23.6 2.0 %collective-permute-done.7 = f32[32,512]{1,0:T(8,128)S(1)} collective-permute-done((f32[32,512]{1,0:T(8,128)S(1)}, f32[32,512]{1,0:T(8,128)S(1)}, u32[]{:S(2)}, u32[]{:S(2)}) %collective-permute-start.7) | collective-permute-done | bytes 65568 | tf_op jit(solution)/shard_map/ppermute | solution.py:257
  26.4 1.6 %collective-permute-start.10 = (f32[32,512]{1,0:T(8,128)S(1)}, f32[32,512]{1,0:T(8,128)S(1)}, u32[]{:S(2)}, u32[]{:S(2)}) collective-permute-start(f32[32,512]{1,0:T(8,128)S(1)} %pad_maximum_fusion), channel_id=1, source_target_pairs={{0,8},{4,12},{8,0},{12,4},{1,9},{5,13},{9,1},{13,5},{2,10},{6,14},... | collective-permute-start | bytes 196616 | tf_op jit(solution)/shard_map/ppermute | solution.py:257
  28.0 1.4 %collective-permute-start.2 = (f32[32,256]{1,0:T(8,128)S(1)}, f32[32,256]{1,0:T(8,128)S(1)}, u32[]{:S(2)}, u32[]{:S(2)}) collective-permute-start(f32[32,256]{1,0:T(8,128)S(1)} %get-tuple-element.33), channel_id=1, source_target_pairs={{0,1},{1,0},{2,3},{3,2},{4,5},{5,4},{6,7},{7,6},{8,9},{9,8},{10,11... | collective-permute-start | bytes 98312 | tf_op jit(solution)/shard_map/ppermute | solution.py:257
  29.4 2.2 %collective-permute-start.4 = (f32[32,256]{1,0:T(8,128)S(1)}, f32[32,256]{1,0:T(8,128)S(1)}, u32[]{:S(2)}, u32[]{:S(2)}) collective-permute-start(f32[32,256]{1,0:T(8,128)S(1)} %get-tuple-element.34), channel_id=1, source_target_pairs={{0,3},{1,2},{2,1},{3,0},{4,7},{5,6},{6,5},{7,4},{8,11},{9,10},{10,... | collective-permute-start | bytes 98312 | tf_op jit(solution)/shard_map/ppermute | solution.py:257
  32.4 2.8 %collective-permute-done.4 = f32[32,256]{1,0:T(8,128)S(1)} collective-permute-done((f32[32,256]{1,0:T(8,128)S(1)}, f32[32,256]{1,0:T(8,128)S(1)}, u32[]{:S(2)}, u32[]{:S(2)}) %collective-permute-start.4) | collective-permute-done | bytes 32800 | tf_op jit(solution)/shard_map/ppermute | solution.py:257
  35.1 1.3 %collective-permute-done.3 = f32[32,256]{1,0:T(8,128)S(1)} collective-permute-done((f32[32,256]{1,0:T(8,128)S(1)}, f32[32,256]{1,0:T(8,128)S(1)}, u32[]{:S(2)}, u32[]{:S(2)}) %collective-permute-start.3) | collective-permute-done | bytes 32800 | tf_op jit(solution)/shard_map/ppermute | solution.py:257
  37.2 3.2 %collective-permute-done.5 = f32[32,256]{1,0:T(8,128)S(1)} collective-permute-done((f32[32,256]{1,0:T(8,128)S(1)}, f32[32,256]{1,0:T(8,128)S(1)}, u32[]{:S(2)}, u32[]{:S(2)}) %collective-permute-start.5) | collective-permute-done | bytes 32800 | tf_op jit(solution)/shard_map/ppermute | solution.py:257
  40.8 2.2 %collective-permute-start.13 = (bf16[32,256]{1,0:T(8,128)(2,1)S(1)}, bf16[32,256]{1,0:T(8,128)(2,1)S(1)}, u32[]{:S(2)}, u32[]{:S(2)}) collective-permute-start(bf16[32,256]{1,0:T(8,128)(2,1)S(1)} %fusion.23), channel_id=1, source_target_pairs={{0,2},{1,3},{2,0},{3,1},{4,6},{5,7},{6,4},{7,5},{8,10},{9,11},{10,... | collective-permute-start | bytes 49160 | tf_op jit(solution)/shard_map/ppermute | solution.py:257
  42.9 2.2 %collective-permute-start.14 = (bf16[32,256]{1,0:T(8,128)(2,1)S(1)}, bf16[32,256]{1,0:T(8,128)(2,1)S(1)}, u32[]{:S(2)}, u32[]{:S(2)}) collective-permute-start(bf16[32,256]{1,0:T(8,128)(2,1)S(1)} %fusion.23), channel_id=1, source_target_pairs={{0,3},{1,2},{2,1},{3,0},{4,7},{5,6},{6,5},{7,4},{8,11},{9,10},{10,... | collective-permute-start | bytes 49160 | tf_op jit(solution)/shard_map/ppermute | solution.py:257
  45.5 3.0 %collective-permute-done.14 = bf16[32,256]{1,0:T(8,128)(2,1)S(1)} collective-permute-done((bf16[32,256]{1,0:T(8,128)(2,1)S(1)}, bf16[32,256]{1,0:T(8,128)(2,1)S(1)}, u32[]{:S(2)}, u32[]{:S(2)}) %collective-permute-start.14) | collective-permute-done | bytes 16416 | tf_op jit(solution)/shard_map/ppermute | solution.py:257
  48.7 1.1 %collective-permute-done.15 = bf16[128,256]{1,0:T(8,128)(2,1)S(1)} collective-permute-done((bf16[128,256]{1,0:T(8,128)(2,1)S(1)}, bf16[128,256]{1,0:T(8,128)(2,1)S(1)}, u32[]{:S(2)}, u32[]{:S(2)}) %collective-permute-start.15) | collective-permute-done | bytes 65568 | tf_op jit(solution)/shard_map/ppermute | solution.py:257
  49.9 5.5 %shard_map.88 = (f32[128,256]{1,0:T(8,128)S(1)}, bf16[256,256]{1,0:T(8,128)(2,1)}) custom-call(bf16[64,128,256]{2,1,0:T(8,128)(2,1)} %get-tuple-element.16.refs_0_, bf16[64,128,256]{2,1,0:T(8,128)(2,1)} %get-tuple-element.18.refs_1_, bf16[256,256]{1,0:T(8,128)(2,1)S(1)} %maximum_select_fusion.4.refs_2_, bf16[128,256]{1,0:T(8,128)(2,1)S(1)} %copy-done.1), custom_call_target="tpu_custom_call" | custom-call | flops 2147483648 | bytes 8388608 | tf_op jit(solution)/shard_map/pallas_call | solution.py:229
  56.4 2.2 %collective-permute-start.18 = (f32[32,256]{1,0:T(8,128)S(1)}, f32[32,256]{1,0:T(8,128)S(1)}, u32[]{:S(2)}, u32[]{:S(2)}) collective-permute-start(f32[32,256]{1,0:T(8,128)S(1)} %get-tuple-element.31), channel_id=1, source_target_pairs={{0,3},{1,2},{2,1},{3,0},{4,7},{5,6},{6,5},{7,4},{8,11},{9,10},{10,... | collective-permute-start | bytes 98312 | tf_op jit(solution)/shard_map/ppermute | solution.py:257
  59.0 2.5 %collective-permute-start.22 = (bf16[256,256]{1,0:T(8,128)(2,1)S(1)}, bf16[256,256]{1,0:T(8,128)(2,1)S(1)}, u32[]{:S(2)}, u32[]{:S(2)}) collective-permute-start(bf16[256,256]{1,0:T(8,128)(2,1)S(1)} %maximum_select_fusion.5), channel_id=1, source_target_pairs={{0,2},{1,3},{2,0},{3,1},{4,6},{5,7},{6,4},{7,5},{8,10},{9,11},{10,... | collective-permute-start | bytes 393224 | tf_op jit(solution)/shard_map/ppermute | solution.py:257
  62.1 4.6 %collective-permute-done.17 = f32[32,256]{1,0:T(8,128)S(1)} collective-permute-done((f32[32,256]{1,0:T(8,128)S(1)}, f32[32,256]{1,0:T(8,128)S(1)}, u32[]{:S(2)}, u32[]{:S(2)}) %collective-permute-start.17) | collective-permute-done | bytes 32800 | tf_op jit(solution)/shard_map/ppermute | solution.py:257
  67.7 1.0 %collective-permute-done.22 = bf16[256,256]{1,0:T(8,128)(2,1)S(1)} collective-permute-done((bf16[256,256]{1,0:T(8,128)(2,1)S(1)}, bf16[256,256]{1,0:T(8,128)(2,1)S(1)}, u32[]{:S(2)}, u32[]{:S(2)}) %collective-permute-start.22) | collective-permute-done | bytes 131104 | tf_op jit(solution)/shard_map/ppermute | solution.py:257
  69.3 1.4 %collective-permute-done.19 = f32[32,256]{1,0:T(8,128)S(1)} collective-permute-done((f32[32,256]{1,0:T(8,128)S(1)}, f32[32,256]{1,0:T(8,128)S(1)}, u32[]{:S(2)}, u32[]{:S(2)}) %collective-permute-start.19) | collective-permute-done | bytes 32800 | tf_op jit(solution)/shard_map/ppermute | solution.py:257
  70.8 1.2 %collective-permute-start.24 = (bf16[32,256]{1,0:T(8,128)(2,1)S(1)}, bf16[32,256]{1,0:T(8,128)(2,1)S(1)}, u32[]{:S(2)}, u32[]{:S(2)}) collective-permute-start(bf16[32,256]{1,0:T(8,128)(2,1)S(1)} %divide_convert_fusion.1), channel_id=1, source_target_pairs={{0,2},{1,3},{2,0},{3,1},{4,6},{5,7},{6,4},{7,5},{8,10},{9,11},{10,... | collective-permute-start | bytes 49160 | tf_op jit(solution)/shard_map/ppermute | solution.py:257
  72.0 3.1 %collective-permute-start.25 = (bf16[32,256]{1,0:T(8,128)(2,1)S(1)}, bf16[32,256]{1,0:T(8,128)(2,1)S(1)}, u32[]{:S(2)}, u32[]{:S(2)}) collective-permute-start(bf16[32,256]{1,0:T(8,128)(2,1)S(1)} %divide_convert_fusion.1), channel_id=1, source_target_pairs={{0,3},{1,2},{2,1},{3,0},{4,7},{5,6},{6,5},{7,4},{8,11},{9,10},{10,... | collective-permute-start | bytes 49160 | tf_op jit(solution)/shard_map/ppermute | solution.py:257
  75.5 2.0 %collective-permute-done.25 = bf16[32,256]{1,0:T(8,128)(2,1)S(1)} collective-permute-done((bf16[32,256]{1,0:T(8,128)(2,1)S(1)}, bf16[32,256]{1,0:T(8,128)(2,1)S(1)}, u32[]{:S(2)}, u32[]{:S(2)}) %collective-permute-start.25) | collective-permute-done | bytes 16416 | tf_op jit(solution)/shard_map/ppermute | solution.py:257
  77.6 4.9 %shard_map.89 = f32[128,256]{1,0:T(8,128)S(1)} custom-call(bf16[64,128,256]{2,1,0:T(8,128)(2,1)} %get-tuple-element.16.refs_0_, bf16[64,128,256]{2,1,0:T(8,128)(2,1)} %get-tuple-element.18.refs_1_, bf16[256,256]{1,0:T(8,128)(2,1)S(1)} %maximum_select_fusion.4.refs_2_, bf16[128,256]{1,0:T(8,128)(2,1)S(1)} %maximum_select_fusion.8.refs_3_), custom_call_target="tpu_custom_call" | custom-call | flops 2147483648 | bytes 8388608 | tf_op jit(solution)/shard_map/pallas_call | solution.py:229
  83.1 3.7 %collective-permute-done.30 = bf16[128,256]{1,0:T(8,128)(2,1)S(1)} collective-permute-done((bf16[128,256]{1,0:T(8,128)(2,1)S(1)}, bf16[128,256]{1,0:T(8,128)(2,1)S(1)}, u32[]{:S(2)}, u32[]{:S(2)}) %collective-permute-start.30) | collective-permute-done | bytes 65568 | tf_op jit(solution)/shard_map/ppermute | solution.py:257
  87.5 1.5 %collective-permute-start.28 = (f32[64,256]{1,0:T(8,128)S(1)}, f32[64,256]{1,0:T(8,128)S(1)}, u32[]{:S(2)}, u32[]{:S(2)}) collective-permute-start(f32[64,256]{1,0:T(8,128)S(1)} %dynamic-slice_add_fusion.2), channel_id=1, source_target_pairs={{0,16},{4,20},{8,24},{12,28},{16,0},{20,4},{24,8},{28,12},{1,17},{... | collective-permute-start | bytes 196616 | tf_op jit(solution)/shard_map/ppermute | solution.py:257
  89.1 1.5 %collective-permute-start.27 = (f32[64,256]{1,0:T(8,128)S(1)}, f32[64,256]{1,0:T(8,128)S(1)}, u32[]{:S(2)}, u32[]{:S(2)}) collective-permute-start(f32[64,256]{1,0:T(8,128)S(1)} %dynamic-slice_add_fusion.2), channel_id=1, source_target_pairs={{0,8},{4,12},{8,0},{12,4},{16,24},{20,28},{24,16},{28,20},{1,9},{5... | collective-permute-start | bytes 196616 | tf_op jit(solution)/shard_map/ppermute | solution.py:257
  91.1 1.8 %collective-permute-done.29 = f32[64,256]{1,0:T(8,128)S(1)} collective-permute-done((f32[64,256]{1,0:T(8,128)S(1)}, f32[64,256]{1,0:T(8,128)S(1)}, u32[]{:S(2)}, u32[]{:S(2)}) %collective-permute-start.29) | collective-permute-done | bytes 65568 | tf_op jit(solution)/shard_map/ppermute | solution.py:257
  94.0 1.2 %collective-permute-done.32 = bf16[64,256]{1,0:T(8,128)(2,1)S(1)} collective-permute-done((bf16[64,256]{1,0:T(8,128)(2,1)S(1)}, bf16[64,256]{1,0:T(8,128)(2,1)S(1)}, u32[]{:S(2)}, u32[]{:S(2)}) %collective-permute-start.32) | collective-permute-done | bytes 32800 | tf_op jit(solution)/shard_map/ppermute | solution.py:257
  (89 shorter events, 12.2 us)
Async XLA Ops:
  3.1 13.5 %collective-permute-start.6 = (f32[128,512]{1,0:T(8,128)S(1)}, f32[128,512]{1,0:T(8,128)S(1)}, u32[]{:S(2)}, u32[]{:S(2)}) collective-permute-start(f32[128,512]{1,0:T(8,128)S(1)} %constant_dynamic-slice_fusion.6), channel_id=1, source_target_pairs={{0,4},{4,0},{8,12},{12,8},{1,5},{5,1},{9,13},{13,9},{2,6},{6,2},{1... | collective-permute-start | bytes 786440 | tf_op jit(solution)/shard_map/ppermute | solution.py:257
  3.7 17.5 %collective-permute-start = (f32[256,256]{1,0:T(8,128)S(1)}, f32[256,256]{1,0:T(8,128)S(1)}, u32[]{:S(2)}, u32[]{:S(2)}) collective-permute-start(f32[256,256]{1,0:T(8,128)S(1)} %constant_dynamic-slice_fusion.11), channel_id=1, source_target_pairs={{0,16},{16,0},{1,17},{17,1},{2,18},{18,2},{3,19},{19,3},{4,20},{20... | collective-permute-start | bytes 786440 | tf_op jit(solution)/shard_map/ppermute | solution.py:257
  16.8 6.8 %collective-permute-start.9 = (f32[32,512]{1,0:T(8,128)S(1)}, f32[32,512]{1,0:T(8,128)S(1)}, u32[]{:S(2)}, u32[]{:S(2)}) collective-permute-start(f32[32,512]{1,0:T(8,128)S(1)} %get-tuple-element.27), channel_id=1, source_target_pairs={{0,3},{1,2},{2,1},{3,0},{4,7},{5,6},{6,5},{7,4},{8,11},{9,10},{10,... | collective-permute-start | bytes 196616 | tf_op jit(solution)/shard_map/ppermute | solution.py:257
  20.5 5.2 %collective-permute-start.7 = (f32[32,512]{1,0:T(8,128)S(1)}, f32[32,512]{1,0:T(8,128)S(1)}, u32[]{:S(2)}, u32[]{:S(2)}) collective-permute-start(f32[32,512]{1,0:T(8,128)S(1)} %get-tuple-element.28), channel_id=1, source_target_pairs={{0,1},{1,0},{2,3},{3,2},{4,5},{5,4},{6,7},{7,6},{8,9},{9,8},{10,11... | collective-permute-start | bytes 196616 | tf_op jit(solution)/shard_map/ppermute | solution.py:257
  20.5 5.9 %collective-permute-start.8 = (f32[32,512]{1,0:T(8,128)S(1)}, f32[32,512]{1,0:T(8,128)S(1)}, u32[]{:S(2)}, u32[]{:S(2)}) collective-permute-start(f32[32,512]{1,0:T(8,128)S(1)} %get-tuple-element.29), channel_id=1, source_target_pairs={{0,2},{1,3},{2,0},{3,1},{4,6},{5,7},{6,4},{7,5},{8,10},{9,11},{10,... | collective-permute-start | bytes 196616 | tf_op jit(solution)/shard_map/ppermute | solution.py:257
  21.3 6.6 %collective-permute-start.1 = (f32[128,256]{1,0:T(8,128)S(1)}, f32[128,256]{1,0:T(8,128)S(1)}, u32[]{:S(2)}, u32[]{:S(2)}) collective-permute-start(f32[128,256]{1,0:T(8,128)S(1)} %constant_dynamic-slice_fusion.10), channel_id=1, source_target_pairs={{0,4},{4,0},{8,12},{12,8},{1,5},{5,1},{9,13},{13,9},{2,6},{6,2},{1... | collective-permute-start | bytes 393224 | tf_op jit(solution)/shard_map/ppermute | solution.py:257
  26.4 5.2 %collective-permute-start.10 = (f32[32,512]{1,0:T(8,128)S(1)}, f32[32,512]{1,0:T(8,128)S(1)}, u32[]{:S(2)}, u32[]{:S(2)}) collective-permute-start(f32[32,512]{1,0:T(8,128)S(1)} %pad_maximum_fusion), channel_id=1, source_target_pairs={{0,8},{4,12},{8,0},{12,4},{1,9},{5,13},{9,1},{13,5},{2,10},{6,14},... | collective-permute-start | bytes 196616 | tf_op jit(solution)/shard_map/ppermute | solution.py:257
  28.0 4.3 %collective-permute-start.2 = (f32[32,256]{1,0:T(8,128)S(1)}, f32[32,256]{1,0:T(8,128)S(1)}, u32[]{:S(2)}, u32[]{:S(2)}) collective-permute-start(f32[32,256]{1,0:T(8,128)S(1)} %get-tuple-element.33), channel_id=1, source_target_pairs={{0,1},{1,0},{2,3},{3,2},{4,5},{5,4},{6,7},{7,6},{8,9},{9,8},{10,11... | collective-permute-start | bytes 98312 | tf_op jit(solution)/shard_map/ppermute | solution.py:257
  29.4 5.7 %collective-permute-start.4 = (f32[32,256]{1,0:T(8,128)S(1)}, f32[32,256]{1,0:T(8,128)S(1)}, u32[]{:S(2)}, u32[]{:S(2)}) collective-permute-start(f32[32,256]{1,0:T(8,128)S(1)} %get-tuple-element.34), channel_id=1, source_target_pairs={{0,3},{1,2},{2,1},{3,0},{4,7},{5,6},{6,5},{7,4},{8,11},{9,10},{10,... | collective-permute-start | bytes 98312 | tf_op jit(solution)/shard_map/ppermute | solution.py:257
  31.6 4.8 %collective-permute-start.3 = (f32[32,256]{1,0:T(8,128)S(1)}, f32[32,256]{1,0:T(8,128)S(1)}, u32[]{:S(2)}, u32[]{:S(2)}) collective-permute-start(f32[32,256]{1,0:T(8,128)S(1)} %get-tuple-element.35), channel_id=1, source_target_pairs={{0,2},{1,3},{2,0},{3,1},{4,6},{5,7},{6,4},{7,5},{8,10},{9,11},{10,... | collective-permute-start | bytes 98312 | tf_op jit(solution)/shard_map/ppermute | solution.py:257
  31.6 5.6 %collective-permute-start.11 = (f32[32,256]{1,0:T(8,128)S(1)}, f32[32,256]{1,0:T(8,128)S(1)}, u32[]{:S(2)}, u32[]{:S(2)}) collective-permute-start(f32[32,256]{1,0:T(8,128)S(1)} %slice.29), channel_id=1, source_target_pairs={{0,16},{16,0},{1,17},{17,1},{2,18},{18,2},{3,19},{19,3},{4,20},{20... | collective-permute-start | bytes 98312 | tf_op jit(solution)/shard_map/ppermute | solution.py:257
  36.4 4.0 %collective-permute-start.5 = (f32[32,256]{1,0:T(8,128)S(1)}, f32[32,256]{1,0:T(8,128)S(1)}, u32[]{:S(2)}, u32[]{:S(2)}) collective-permute-start(f32[32,256]{1,0:T(8,128)S(1)} %add_add_fusion.2), channel_id=1, source_target_pairs={{0,8},{4,12},{8,0},{12,4},{1,9},{5,13},{9,1},{13,5},{2,10},{6,14},... | collective-permute-start | bytes 98312 | tf_op jit(solution)/shard_map/ppermute | solution.py:257
  40.7 4.5 %collective-permute-start.12 = (bf16[32,256]{1,0:T(8,128)(2,1)S(1)}, bf16[32,256]{1,0:T(8,128)(2,1)S(1)}, u32[]{:S(2)}, u32[]{:S(2)}) collective-permute-start(bf16[32,256]{1,0:T(8,128)(2,1)S(1)} %fusion.23), channel_id=1, source_target_pairs={{0,1},{1,0},{2,3},{3,2},{4,5},{5,4},{6,7},{7,6},{8,9},{9,8},{10,11... | collective-permute-start | bytes 49160 | tf_op jit(solution)/shard_map/ppermute | solution.py:257
  40.8 4.7 %collective-permute-start.13 = (bf16[32,256]{1,0:T(8,128)(2,1)S(1)}, bf16[32,256]{1,0:T(8,128)(2,1)S(1)}, u32[]{:S(2)}, u32[]{:S(2)}) collective-permute-start(bf16[32,256]{1,0:T(8,128)(2,1)S(1)} %fusion.23), channel_id=1, source_target_pairs={{0,2},{1,3},{2,0},{3,1},{4,6},{5,7},{6,4},{7,5},{8,10},{9,11},{10,... | collective-permute-start | bytes 49160 | tf_op jit(solution)/shard_map/ppermute | solution.py:257
  42.9 5.5 %collective-permute-start.14 = (bf16[32,256]{1,0:T(8,128)(2,1)S(1)}, bf16[32,256]{1,0:T(8,128)(2,1)S(1)}, u32[]{:S(2)}, u32[]{:S(2)}) collective-permute-start(bf16[32,256]{1,0:T(8,128)(2,1)S(1)} %fusion.23), channel_id=1, source_target_pairs={{0,3},{1,2},{2,1},{3,0},{4,7},{5,6},{6,5},{7,4},{8,11},{9,10},{10,... | collective-permute-start | bytes 49160 | tf_op jit(solution)/shard_map/ppermute | solution.py:257
  48.5 1.3 %collective-permute-start.15 = (bf16[128,256]{1,0:T(8,128)(2,1)S(1)}, bf16[128,256]{1,0:T(8,128)(2,1)S(1)}, u32[]{:S(2)}, u32[]{:S(2)}) collective-permute-start(bf16[128,256]{1,0:T(8,128)(2,1)S(1)} %maximum_select_fusion.7), channel_id=1, source_target_pairs={{0,4},{4,0},{8,12},{12,8},{1,5},{5,1},{9,13},{13,9},{2,6},{6,2},{1... | collective-permute-start | bytes 196616 | tf_op jit(solution)/shard_map/ppermute | solution.py:257
  48.6 10.4 %collective-permute-start.21 = (bf16[128,256]{1,0:T(8,128)(2,1)S(1)}, bf16[128,256]{1,0:T(8,128)(2,1)S(1)}, u32[]{:S(2)}, u32[]{:S(2)}) collective-permute-start(bf16[128,256]{1,0:T(8,128)(2,1)S(1)} %copy-done.1), channel_id=1, source_target_pairs={{0,1},{1,0},{2,3},{3,2},{4,5},{5,4},{6,7},{7,6},{8,9},{9,8},{10,11... | collective-permute-start | bytes 196616 | tf_op jit(solution)/shard_map/ppermute | solution.py:257
  55.4 6.7 %collective-permute-start.16 = (f32[32,256]{1,0:T(8,128)S(1)}, f32[32,256]{1,0:T(8,128)S(1)}, u32[]{:S(2)}, u32[]{:S(2)}) collective-permute-start(f32[32,256]{1,0:T(8,128)S(1)} %get-tuple-element.30), channel_id=1, source_target_pairs={{0,1},{1,0},{2,3},{3,2},{4,5},{5,4},{6,7},{7,6},{8,9},{9,8},{10,11... | collective-permute-start | bytes 98312 | tf_op jit(solution)/shard_map/ppermute | solution.py:257
  56.4 5.7 %collective-permute-start.18 = (f32[32,256]{1,0:T(8,128)S(1)}, f32[32,256]{1,0:T(8,128)S(1)}, u32[]{:S(2)}, u32[]{:S(2)}) collective-permute-start(f32[32,256]{1,0:T(8,128)S(1)} %get-tuple-element.31), channel_id=1, source_target_pairs={{0,3},{1,2},{2,1},{3,0},{4,7},{5,6},{6,5},{7,4},{8,11},{9,10},{10,... | collective-permute-start | bytes 98312 | tf_op jit(solution)/shard_map/ppermute | solution.py:257
  58.6 8.1 %collective-permute-start.17 = (f32[32,256]{1,0:T(8,128)S(1)}, f32[32,256]{1,0:T(8,128)S(1)}, u32[]{:S(2)}, u32[]{:S(2)}) collective-permute-start(f32[32,256]{1,0:T(8,128)S(1)} %get-tuple-element.32), channel_id=1, source_target_pairs={{0,2},{1,3},{2,0},{3,1},{4,6},{5,7},{6,4},{7,5},{8,10},{9,11},{10,... | collective-permute-start | bytes 98312 | tf_op jit(solution)/shard_map/ppermute | solution.py:257
  59.0 9.7 %collective-permute-start.22 = (bf16[256,256]{1,0:T(8,128)(2,1)S(1)}, bf16[256,256]{1,0:T(8,128)(2,1)S(1)}, u32[]{:S(2)}, u32[]{:S(2)}) collective-permute-start(bf16[256,256]{1,0:T(8,128)(2,1)S(1)} %maximum_select_fusion.5), channel_id=1, source_target_pairs={{0,2},{1,3},{2,0},{3,1},{4,6},{5,7},{6,4},{7,5},{8,10},{9,11},{10,... | collective-permute-start | bytes 393224 | tf_op jit(solution)/shard_map/ppermute | solution.py:257
  61.6 5.7 %collective-permute-start.20 = (bf16[256,256]{1,0:T(8,128)(2,1)S(1)}, bf16[256,256]{1,0:T(8,128)(2,1)S(1)}, u32[]{:S(2)}, u32[]{:S(2)}) collective-permute-start(bf16[256,256]{1,0:T(8,128)(2,1)S(1)} %maximum_select_fusion.4.refs_2_), channel_id=1, source_target_pairs={{0,16},{16,0},{1,17},{17,1},{2,18},{18,2},{3,19},{19,3},{4,20},{20... | collective-permute-start | bytes 393224 | tf_op jit(solution)/shard_map/ppermute | solution.py:257
  66.7 4.0 %collective-permute-start.19 = (f32[32,256]{1,0:T(8,128)S(1)}, f32[32,256]{1,0:T(8,128)S(1)}, u32[]{:S(2)}, u32[]{:S(2)}) collective-permute-start(f32[32,256]{1,0:T(8,128)S(1)} %add_add_fusion.1), channel_id=1, source_target_pairs={{0,16},{16,0},{1,17},{17,1},{2,18},{18,2},{3,19},{19,3},{4,20},{20... | collective-permute-start | bytes 98312 | tf_op jit(solution)/shard_map/ppermute | solution.py:257
  70.7 4.5 %collective-permute-start.23 = (bf16[32,256]{1,0:T(8,128)(2,1)S(1)}, bf16[32,256]{1,0:T(8,128)(2,1)S(1)}, u32[]{:S(2)}, u32[]{:S(2)}) collective-permute-start(bf16[32,256]{1,0:T(8,128)(2,1)S(1)} %divide_convert_fusion.1), channel_id=1, source_target_pairs={{0,1},{1,0},{2,3},{3,2},{4,5},{5,4},{6,7},{7,6},{8,9},{9,8},{10,11... | collective-permute-start | bytes 49160 | tf_op jit(solution)/shard_map/ppermute | solution.py:257
  70.8 4.7 %collective-permute-start.24 = (bf16[32,256]{1,0:T(8,128)(2,1)S(1)}, bf16[32,256]{1,0:T(8,128)(2,1)S(1)}, u32[]{:S(2)}, u32[]{:S(2)}) collective-permute-start(bf16[32,256]{1,0:T(8,128)(2,1)S(1)} %divide_convert_fusion.1), channel_id=1, source_target_pairs={{0,2},{1,3},{2,0},{3,1},{4,6},{5,7},{6,4},{7,5},{8,10},{9,11},{10,... | collective-permute-start | bytes 49160 | tf_op jit(solution)/shard_map/ppermute | solution.py:257
  72.0 5.5 %collective-permute-start.25 = (bf16[32,256]{1,0:T(8,128)(2,1)S(1)}, bf16[32,256]{1,0:T(8,128)(2,1)S(1)}, u32[]{:S(2)}, u32[]{:S(2)}) collective-permute-start(bf16[32,256]{1,0:T(8,128)(2,1)S(1)} %divide_convert_fusion.1), channel_id=1, source_target_pairs={{0,3},{1,2},{2,1},{3,0},{4,7},{5,6},{6,5},{7,4},{8,11},{9,10},{10,... | collective-permute-start | bytes 49160 | tf_op jit(solution)/shard_map/ppermute | solution.py:257
  82.5 4.3 %collective-permute-start.30 = (bf16[128,256]{1,0:T(8,128)(2,1)S(1)}, bf16[128,256]{1,0:T(8,128)(2,1)S(1)}, u32[]{:S(2)}, u32[]{:S(2)}) collective-permute-start(bf16[128,256]{1,0:T(8,128)(2,1)S(1)} %maximum_select_fusion.8.refs_3_), channel_id=1, source_target_pairs={{0,8},{4,12},{8,0},{12,4},{1,9},{5,13},{9,1},{13,5},{2,10},{6,14},... | collective-permute-start | bytes 196616 | tf_op jit(solution)/shard_map/ppermute | solution.py:257
  83.1 3.9 %collective-permute-start.26 = (f32[64,256]{1,0:T(8,128)S(1)}, f32[64,256]{1,0:T(8,128)S(1)}, u32[]{:S(2)}, u32[]{:S(2)}) collective-permute-start(f32[64,256]{1,0:T(8,128)S(1)} %constant_dynamic-slice_fusion), channel_id=1, source_target_pairs={{0,4},{4,0},{8,12},{12,8},{1,5},{5,1},{9,13},{13,9},{2,6},{6,2},{1... | collective-permute-start | bytes 196616 | tf_op jit(solution)/shard_map/ppermute | solution.py:257
  86.9 3.7 %collective-permute-start.31 = (bf16[256,256]{1,0:T(8,128)(2,1)S(1)}, bf16[256,256]{1,0:T(8,128)(2,1)S(1)}, u32[]{:S(2)}, u32[]{:S(2)}) collective-permute-start(bf16[256,256]{1,0:T(8,128)(2,1)S(1)} %maximum_select_fusion.6), channel_id=1, source_target_pairs={{0,4},{4,0},{8,12},{12,8},{1,5},{5,1},{9,13},{13,9},{2,6},{6,2},{1... | collective-permute-start | bytes 393224 | tf_op jit(solution)/shard_map/ppermute | solution.py:257
  87.0 5.9 %collective-permute-start.29 = (f32[64,256]{1,0:T(8,128)S(1)}, f32[64,256]{1,0:T(8,128)S(1)}, u32[]{:S(2)}, u32[]{:S(2)}) collective-permute-start(f32[64,256]{1,0:T(8,128)S(1)} %dynamic-slice_add_fusion.2), channel_id=1, source_target_pairs={{0,24},{4,28},{8,16},{12,20},{16,8},{20,12},{24,0},{28,4},{1,25},{... | collective-permute-start | bytes 196616 | tf_op jit(solution)/shard_map/ppermute | solution.py:257
  87.5 5.4 %collective-permute-start.28 = (f32[64,256]{1,0:T(8,128)S(1)}, f32[64,256]{1,0:T(8,128)S(1)}, u32[]{:S(2)}, u32[]{:S(2)}) collective-permute-start(f32[64,256]{1,0:T(8,128)S(1)} %dynamic-slice_add_fusion.2), channel_id=1, source_target_pairs={{0,16},{4,20},{8,24},{12,28},{16,0},{20,4},{24,8},{28,12},{1,17},{... | collective-permute-start | bytes 196616 | tf_op jit(solution)/shard_map/ppermute | solution.py:257
  89.1 4.8 %collective-permute-start.27 = (f32[64,256]{1,0:T(8,128)S(1)}, f32[64,256]{1,0:T(8,128)S(1)}, u32[]{:S(2)}, u32[]{:S(2)}) collective-permute-start(f32[64,256]{1,0:T(8,128)S(1)} %dynamic-slice_add_fusion.2), channel_id=1, source_target_pairs={{0,8},{4,12},{8,0},{12,4},{16,24},{20,28},{24,16},{28,20},{1,9},{5... | collective-permute-start | bytes 196616 | tf_op jit(solution)/shard_map/ppermute | solution.py:257
  (5 other events, 98.0 us)

commit v4 on v2

--- a/solution.py
+++ b/solution.py
@@ -42,9 +42,13 @@
     return lambda index: copy(index).wait()
 
 
-def gram_kernel(column, second, time, grams, gram_time, turned, second_out, time_out, held, sem):
+def local_kernel(
+    column, second, time, matrix, grams, gram_time, coupled, second_out, time_out, *scratch
+):
     f32 = jnp.float32
-    wait = bring((column, second, time), (held, second_out, time_out), sem)
+    held, held_matrix, turned, sem = scratch
+    targets = (held, second_out, time_out, held_matrix)
+    wait = bring((column, second, time, matrix), targets, sem)
     rank = column.shape[1]
     wait(0)
     turned[...] = held[...].T
@@ -53,48 +57,36 @@
     grams[:, rank:] = jnp.dot(second_out[...].T, second_out[...], preferred_element_type=f32)
     wait(2)
     gram_time[...] = jnp.dot(time_out[...].T, time_out[...], preferred_element_type=f32)
-
-
-def local_grams(column, second, time):
+    wait(3)
+    coupled[...] = lax.dot_general(
+        turned[...], held_matrix[...], (((1,), (1,)), ((), ())), preferred_element_type=f32
+    )
+
+
+def local_products(column, second, time, matrix):
     width, rank = column.shape
+    rows = matrix.shape[0]
     f32 = jnp.float32
     return kernel_call(
-        gram_kernel,
-        2 * width * rank * rank,
-        2 * width * rank,
+        local_kernel,
+        2 * width * rank * (rank + rows),
+        2 * width * (rank + rows),
         out_shape=(
             jax.ShapeDtypeStruct((rank, 2 * rank), f32),
             jax.ShapeDtypeStruct((rank, rank), f32),
-            jax.ShapeDtypeStruct((rank, width), column.dtype),
+            jax.ShapeDtypeStruct((rank, rows), f32),
             jax.ShapeDtypeStruct(second.shape, second.dtype),
             jax.ShapeDtypeStruct(time.shape, time.dtype),
         ),
-        in_specs=[ANY] * 3,
+        in_specs=[ANY] * 4,
         out_specs=(VMEM,) * 5,
         scratch_shapes=[
             pltpu.VMEM(column.shape, column.dtype),
-            pltpu.SemaphoreType.DMA((3,)),
+            pltpu.VMEM(matrix.shape, matrix.dtype),
+            pltpu.VMEM((rank, width), column.dtype),
+            pltpu.SemaphoreType.DMA((4,)),
         ],
-    )(*(in_hbm(a) for a in (column, second, time)))
-
-
-def coupled_kernel(turned, matrix, coupled):
-    coupled[...] = lax.dot_general(
-        turned[...], matrix[...], (((1,), (1,)), ((), ())), preferred_element_type=jnp.float32
-    )
-
-
-def local_coupled(turned, matrix):
-    rank, width = turned.shape
-    rows = matrix.shape[0]
-    return kernel_call(
-        coupled_kernel,
-        2 * width * rank * rows,
-        2 * width * (rows + rank),
-        out_shape=jax.ShapeDtypeStruct((rank, rows), jnp.float32),
-        in_specs=[VMEM] * 2,
-        out_specs=VMEM,
-    )(turned, matrix)
+    )(*(in_hbm(a) for a in (column, second, time, matrix)))
 
 
 def slab_kernel(first, chunk, steps, tensor, second, time, *refs):
@@ -183,25 +175,65 @@
     return fetch, steps
 
 
-def plane_kernel(chunk, parts, first_turned, time, total, first, read, read_sem):
-    fetch, steps = fetcher(parts, read, read_sem, chunk)
+def plane_kernel(chunk, parts, which, first_turned, time, total, *refs):
+    *first_out, first, read, read_sem = refs
+    steps = parts[0].shape[0] // chunk
+
+    def fetch(part, step):
+        source = parts[part].at[pl.ds(step * chunk, chunk)]
+        return pltpu.make_async_copy(source, read.at[step], read_sem.at[step])
+
+    for part in range(len(parts)):
+
+        @pl.when(which[0] == part)
+        def _():
+            for step in range(steps):
+                fetch(part, step).start()
+
     first[...] = first_turned[...].T
     shared = first[...]
-    for part in range(len(parts)):
-
-        def body(step, carry):
-            fetch(part, step).wait()
-            slot = part * steps + step
-            sums = []
-            for j in range(chunk):
-                weighted = jnp.dot(read[slot, j], shared, preferred_element_type=jnp.float32)
-                scaled = weighted * time[...].astype(jnp.float32)
-                sums.append(jnp.sum(scaled, axis=0, keepdims=True))
-            row = pl.multiple_of(slot * chunk, chunk)
-            total[pl.ds(row, chunk), :] = jnp.concatenate(sums, 0)
-            return carry
-
-        lax.fori_loop(0, steps, body, 0)
+
+    def body(step, carry):
+        fetch(0, step).wait()
+        sums = []
+        for j in range(chunk):
+            weighted = jnp.dot(read[step, j], shared, preferred_element_type=jnp.float32)
+            scaled = weighted * time[...].astype(jnp.float32)
+            sums.append(jnp.sum(scaled, axis=0, keepdims=True))
+        row = pl.multiple_of(step * chunk, chunk)
+        total[pl.ds(row, chunk), :] = jnp.concatenate(sums, 0)
+        return carry
+
+    lax.fori_loop(0, steps, body, 0)
+    if first_out:
+        first_out[0][...] = first[...]
+
+
+def plane_sums(parts, which, first_turned, time, with_first):
+    count, tile_k, tile_i = parts[0].shape
+    rank = first_turned.shape[0]
+    chunk = chunk_of(count, 16)
+    steps = count // chunk
+
+    def on_parts(*refs):
+        plane_kernel(chunk, refs[: len(parts)], *refs[len(parts) :])
+
+    outs = (jax.ShapeDtypeStruct((count, rank), jnp.float32),)
+    if with_first:
+        outs += (jax.ShapeDtypeStruct((tile_i, rank), first_turned.dtype),)
+    return kernel_call(
+        on_parts,
+        2 * tile_i * count * tile_k * rank,
+        2 * tile_i * count * tile_k,
+        out_shape=outs,
+        in_specs=[ANY] * len(parts) + [pl.BlockSpec(memory_space=pltpu.SMEM), VMEM, VMEM],
+        out_specs=(VMEM,) * len(outs),
+        scratch_shapes=[
+            pltpu.VMEM((tile_i, rank), first_turned.dtype),
+            pltpu.VMEM((steps, chunk, tile_k, tile_i), parts[0].dtype),
+            pltpu.SemaphoreType.DMA((steps,)),
+        ],
+    )(*(in_hbm(a) for a in parts), which.reshape(1).astype(jnp.int32), first_turned, time)
 
 
 def time_kernel(chunk, parts, first_turned, second, total, read, read_sem, wide, first):
@@ -320,8 +352,8 @@
     for mask in masks_of(size_j):
         part = 2 * part + (lax.axis_index("ja") & mask) // mask
 
-    grams, gram_time, column_turned, second_near, time_near = local_grams(
-        column_factor, second_factor, time_factor
+    grams, gram_time, coupled, second_near, time_near = local_products(
+        column_factor, second_factor, time_factor, matrix
     )
     for mask in masks_of(size_j):
         grams = halve(grams, "ja", size_j, mask)
@@ -335,7 +367,6 @@
     first_wide = first_factor.astype(f32)
     denominator = full_dot(gram_total, first_wide, ((1,), (1,)))
 
-    coupled = local_coupled(column_turned, matrix)
     for mask in reversed(masks_of(size_i)):
         coupled = halve(coupled, "ia", size_i, mask, 1)
     half = tile_j // 2
@@ -348,8 +379,10 @@
     numerator = all_sum(numerator, "ka", size_k)
     own = lax.dynamic_slice_in_dim(first_wide.T, part * share, share, 0)
     first_new = (own * numerator / denominator).astype(jnp.bfloat16)
+    pieces = spread(first_new, "ja", size_j)
     for mask in reversed(masks_of(size_j)):
-        first_new = double(first_new, "ja", size_j, mask)
+        pieces = [in_order(pieces[d], pieces[d + mask], "ja", mask) for d in range(mask)]
+    first_new = pieces[0]
 
     firsts = spread(first_new, "ia", size_i)
     gram_first = tree_sum([row_product(piece) for piece in firsts])
@@ -357,16 +390,13 @@
     for mask in masks_of(size_k):
         times = double(times, "ka", size_k, mask)
     gram_time = cross_product(times)
-    plane_sum, first_out = weighted_call(
-        plane_kernel,
-        turned,
-        (first_new, time_factor),
-        (
-            jax.ShapeDtypeStruct((tile_j, rank), f32),
-            jax.ShapeDtypeStruct((tile_i, rank), jnp.bfloat16),
-        ),
-    )
-    for mask in reversed(masks_of(size_i)):
+    upper, *lower = reversed(masks_of(size_i))
+    bit = (lax.axis_index("ia") & upper) // upper
+    (sent,) = plane_sums(turned, 1 - bit, first_new, time_factor, False)
+    came = swap(sent, "ia", size_i, upper)
+    kept, first_out = plane_sums(turned, bit, first_new, time_factor, True)
+    plane_sum = kept + came
+    for mask in lower:
         plane_sum = halve(plane_sum, "ia", size_i, mask)
     plane_sum = all_sum(plane_sum, "ka", size_k)
     rows = tile_j // size_i

time: 93.9 us -> 92.5 us (0.985)
  waiting for transfers between devices: 30.3 us -> 26.4 us
  starting transfers between devices: 34.6 us -> 37 us
  Pallas kernels: 23.2 us -> 24.6 us
  local copies, waits for them, and re-layouts: 1.59 us -> 0.35 us
    pallas_call x2 -> x3, Pallas kernels: 2.42 us -> 9.34 us  [the longest x2 6.94 us: plane_sums(): kernel_call(on_parts, 2 * tile_i * count * tile_k * rank, 2 * tile_i * co...]
    pallas_call x2 -> x1, Pallas kernels: 10.4 us -> 4.93 us  [weighted_call(): kernel_call(on_parts, 2 * tile_i * len(parts) * count * tile_k * rank, 2...]
    ppermute x29 -> x30, waiting for transfers between devices: 30.3 us -> 26.4 us  [swap(): return lax.ppermute(values, axis, [(i, i ^ mask) for i in range(size)])]
    ppermute x29 -> x30, starting transfers between devices: 34.6 us -> 37 us  [swap(): return lax.ppermute(values, axis, [(i, i ^ mask) for i in range(size)])]
    unnamed x11 -> x9, local copies, waits for them, and re-layouts: 1.34 us -> 0.12 us
  transfers between devices with their start and end apart: 29 -> 30, of which waited for: 12 -> 15; matrix products, arithmetic and copies ran while one was open for 2% -> 3% of each run, Pallas kernels for 23% -> 27%
where the time goes in v4:
time: 92.5 us; the launch traced here: 92.2 us
  starting transfers between devices  37 us (40%)
  waiting for transfers between devices  26.4 us (29%)
  Pallas kernels  24.6 us (27%)
  matrix products  1.75 us (2%)
  between operations  1.11 us (1%)
  other arithmetic  1.05 us (1%)
    ppermute x30, starting transfers between devices, swap(): return lax.ppermute(values, axis, [(i, i ^ mask) for i in range(size)])  37 us
    ppermute x30, waiting for transfers between devices, swap(): return lax.ppermute(values, axis, [(i, i ^ mask) for i in range(size)])  26.4 us
    pallas_call x2, Pallas kernels, slab_and_turn(): kernel_call(functools.partial(slab_kernel, first, chunk, steps), 2 * tile...  10.3 us
    pallas_call x2, Pallas kernels, plane_sums(): kernel_call(on_parts, 2 * tile_i * count * tile_k * rank, 2 * tile_i * co...  6.94 us
    pallas_call x1, Pallas kernels, weighted_call(): kernel_call(on_parts, 2 * tile_i * len(parts) * count * tile_k * rank, 2...  4.93 us
    pallas_call x1, Pallas kernels, local_products(): kernel_call(local_kernel, 2 * width * rank * (rank + rows), 2 * width * (...  2.4 us
  transfers between devices with their start and end apart: 30, of which 15 were waited for; matrix products, arithmetic and copies ran while one was open for 3% of the time, Pallas kernels for 27%

profile of v4, /device:TPU:0, one launch (start us, length us, event | category | flops | bytes accessed | tf_op | source)
XLA Modules:
  0.0 92.2 jit_solution(15672752132648965558)
XLA Ops:
  0.6 3.1 %collective-permute-start.20 = (bf16[128,256]{1,0:T(8,128)(2,1)}, bf16[128,256]{1,0:T(8,128)(2,1)S(1)}, u32[]{:S(2)}, u32[]{:S(2)}) collective-permute-start(bf16[128,256]{1,0:T(8,128)(2,1)} %refs_4_.3), channel_id=1, source_target_pairs={{0,1},{1,0},{2,3},{3,2},{4,5},{5,4},{6,7},{7,6},{8,9},{9,8},{10,11... | collective-permute-start | bytes 196616 | tf_op jit(solution)/shard_map/ppermute | solution.py:297
  3.8 2.4 %shard_map.85 = (f32[256,512]{1,0:T(8,128)S(1)}, f32[256,256]{1,0:T(8,128)S(1)}, f32[256,512]{1,0:T(8,128)S(1)}, bf16[128,256]{1,0:T(8,128)(2,1)S(1)}, bf16[128,256]{1,0:T(8,128)(2,1)S(1)}) custom-call(bf16[1024,256]{1,0:T(8,128)(2,1)} %column.1, bf16[128,256]{1,0:T(8,128)(2,1)} %second.1, bf16[128,256]{1,0:T(8,128)(2,1)} %refs_4_.3, bf16[512,1024]{1,0:T(8,128)(2,1)} %matrix.1), custom_call_target="tpu_custom_call" | custom-call | flops 402653184 | bytes 1572864 | tf_op jit(solution)/shard_map/pallas_call | solution.py:70
  6.3 1.6 %collective-permute-start = (f32[256,256]{1,0:T(8,128)S(1)}, f32[256,256]{1,0:T(8,128)S(1)}, u32[]{:S(2)}, u32[]{:S(2)}) collective-permute-start(f32[256,256]{1,0:T(8,128)S(1)} %constant_dynamic-slice_fusion.6), channel_id=1, source_target_pairs={{0,16},{16,0},{1,17},{17,1},{2,18},{18,2},{3,19},{19,3},{4,20},{20... | collective-permute-start | bytes 786440 | tf_op jit(solution)/shard_map/ppermute | solution.py:297
  7.9 5.1 %shard_map.86 = (f32[256,256]{1,0:T(8,128)S(1)}, bf16[64,128,256]{2,1,0:T(8,128)(2,1)}) custom-call(bf16[256,128,128]{2,1,0:T(8,128)(2,1)} %tensor.3, bf16[128,256]{1,0:T(8,128)(2,1)S(1)} %get-tuple-element.14.second, bf16[128,256]{1,0:T(8,128)(2,1)S(1)} %get-tuple-element.15.time), custom_call_target="tpu_custom_call" | custom-call | flops 1073741824 | bytes 8388608 | tf_op jit(solution)/shard_map/pallas_call | solution.py:144
  13.1 5.2 %shard_map.87 = (f32[256,256]{1,0:T(8,128)S(1)}, bf16[64,128,256]{2,1,0:T(8,128)(2,1)}) custom-call(bf16[256,128,128]{2,1,0:T(8,128)(2,1)} %tensor.3, bf16[128,256]{1,0:T(8,128)(2,1)S(1)} %get-tuple-element.14.second, bf16[128,256]{1,0:T(8,128)(2,1)S(1)} %get-tuple-element.15.time, f32[256,256]{1,0:T(8,128)S(1)} %get-tuple-element.17.refs_0_), custom_call_target="tpu_custom_call" | custom-call | flops 1073741824 | bytes 8388608 | tf_op jit(solution)/shard_map/pallas_call | solution.py:144
  18.4 1.6 %collective-permute-start.7 = (f32[64,512]{1,0:T(8,128)S(1)}, f32[64,512]{1,0:T(8,128)S(1)}, u32[]{:S(2)}, u32[]{:S(2)}) collective-permute-start(f32[64,512]{1,0:T(8,128)S(1)} %constant_dynamic-slice_fusion.2), channel_id=1, source_target_pairs={{0,8},{4,12},{8,0},{12,4},{1,9},{5,13},{9,1},{13,5},{2,10},{6,14},... | collective-permute-start | bytes 393224 | tf_op jit(solution)/shard_map/ppermute | solution.py:297
  20.1 3.9 %collective-permute-done.7 = f32[64,512]{1,0:T(8,128)S(1)} collective-permute-done((f32[64,512]{1,0:T(8,128)S(1)}, f32[64,512]{1,0:T(8,128)S(1)}, u32[]{:S(2)}, u32[]{:S(2)}) %collective-permute-start.7) | collective-permute-done | bytes 131104 | tf_op jit(solution)/shard_map/ppermute | solution.py:297
  24.1 1.6 %collective-permute-start.2 = (f32[64,256]{1,0:T(8,128)S(1)}, f32[64,256]{1,0:T(8,128)S(1)}, u32[]{:S(2)}, u32[]{:S(2)}) collective-permute-start(f32[64,256]{1,0:T(8,128)S(1)} %constant_dynamic-slice_fusion.4), channel_id=1, source_target_pairs={{0,8},{4,12},{8,0},{12,4},{1,9},{5,13},{9,1},{13,5},{2,10},{6,14},... | collective-permute-start | bytes 196616 | tf_op jit(solution)/shard_map/ppermute | solution.py:297
  25.7 2.7 %collective-permute-start.9 = (f32[64,512]{1,0:T(8,128)S(1)}, f32[64,512]{1,0:T(8,128)S(1)}, u32[]{:S(2)}, u32[]{:S(2)}) collective-permute-start(f32[64,512]{1,0:T(8,128)S(1)} %pad_maximum_fusion), channel_id=1, source_target_pairs={{0,2},{1,3},{2,0},{3,1},{4,6},{5,7},{6,4},{7,5},{8,10},{9,11},{10,... | collective-permute-start | bytes 393224 | tf_op jit(solution)/shard_map/ppermute | solution.py:297
  29.3 3.6 %collective-permute-start.4 = (f32[64,256]{1,0:T(8,128)S(1)}, f32[64,256]{1,0:T(8,128)S(1)}, u32[]{:S(2)}, u32[]{:S(2)}) collective-permute-start(f32[64,256]{1,0:T(8,128)S(1)} %dynamic-slice_add_fusion.4), channel_id=1, source_target_pairs={{0,2},{1,3},{2,0},{3,1},{4,6},{5,7},{6,4},{7,5},{8,10},{9,11},{10,... | collective-permute-start | bytes 196616 | tf_op jit(solution)/shard_map/ppermute | solution.py:297
  32.9 5.1 %collective-permute-done.9 = f32[64,512]{1,0:T(8,128)S(1)} collective-permute-done((f32[64,512]{1,0:T(8,128)S(1)}, f32[64,512]{1,0:T(8,128)S(1)}, u32[]{:S(2)}, u32[]{:S(2)}) %collective-permute-start.9) | collective-permute-done | bytes 131104 | tf_op jit(solution)/shard_map/ppermute | solution.py:297
  37.9 3.2 %collective-permute-start.5 = (f32[64,256]{1,0:T(8,128)S(1)}, f32[64,256]{1,0:T(8,128)S(1)}, u32[]{:S(2)}, u32[]{:S(2)}) collective-permute-start(f32[64,256]{1,0:T(8,128)S(1)} %dynamic-slice_add_fusion.4), channel_id=1, source_target_pairs={{0,3},{1,2},{2,1},{3,0},{4,7},{5,6},{6,5},{7,4},{8,11},{9,10},{10,... | collective-permute-start | bytes 196616 | tf_op jit(solution)/shard_map/ppermute | solution.py:297
  41.1 1.4 %collective-permute-start.3 = (f32[64,256]{1,0:T(8,128)S(1)}, f32[64,256]{1,0:T(8,128)S(1)}, u32[]{:S(2)}, u32[]{:S(2)}) collective-permute-start(f32[64,256]{1,0:T(8,128)S(1)} %dynamic-slice_add_fusion.4), channel_id=1, source_target_pairs={{0,1},{1,0},{2,3},{3,2},{4,5},{5,4},{6,7},{7,6},{8,9},{9,8},{10,11... | collective-permute-start | bytes 196616 | tf_op jit(solution)/shard_map/ppermute | solution.py:297
  44.2 1.1 %collective-permute-done.3 = f32[64,256]{1,0:T(8,128)S(1)} collective-permute-done((f32[64,256]{1,0:T(8,128)S(1)}, f32[64,256]{1,0:T(8,128)S(1)}, u32[]{:S(2)}, u32[]{:S(2)}) %collective-permute-start.3) | collective-permute-done | bytes 65568 | tf_op jit(solution)/shard_map/ppermute | solution.py:297
  45.4 1.5 %collective-permute-done.11 = f32[64,256]{1,0:T(8,128)S(1)} collective-permute-done((f32[64,256]{1,0:T(8,128)S(1)}, f32[64,256]{1,0:T(8,128)S(1)}, u32[]{:S(2)}, u32[]{:S(2)}) %collective-permute-start.11) | collective-permute-done | bytes 65568 | tf_op jit(solution)/shard_map/ppermute | solution.py:297
  47.8 2.0 %collective-permute-start.21 = (bf16[256,256]{1,0:T(8,128)(2,1)S(1)}, bf16[256,256]{1,0:T(8,128)(2,1)S(1)}, u32[]{:S(2)}, u32[]{:S(2)}) collective-permute-start(bf16[256,256]{1,0:T(8,128)(2,1)S(1)} %maximum_select_fusion.5), channel_id=1, source_target_pairs={{0,2},{1,3},{2,0},{3,1},{4,6},{5,7},{6,4},{7,5},{8,10},{9,11},{10,... | collective-permute-start | bytes 393224 | tf_op jit(solution)/shard_map/ppermute | solution.py:297
  49.8 1.6 %collective-permute-start.13 = (bf16[64,256]{1,0:T(8,128)(2,1)S(1)}, bf16[64,256]{1,0:T(8,128)(2,1)S(1)}, u32[]{:S(2)}, u32[]{:S(2)}) collective-permute-start(bf16[64,256]{1,0:T(8,128)(2,1)S(1)} %fusion.17), channel_id=1, source_target_pairs={{0,4},{4,0},{8,12},{12,8},{1,5},{5,1},{9,13},{13,9},{2,6},{6,2},{1... | collective-permute-start | bytes 98312 | tf_op jit(solution)/shard_map/ppermute | solution.py:297
  51.4 2.0 %collective-permute-done.14 = bf16[64,256]{1,0:T(8,128)(2,1)S(1)} collective-permute-done((bf16[64,256]{1,0:T(8,128)(2,1)S(1)}, bf16[64,256]{1,0:T(8,128)(2,1)S(1)}, u32[]{:S(2)}, u32[]{:S(2)}) %collective-permute-start.14) | collective-permute-done | bytes 32800 | tf_op jit(solution)/shard_map/ppermute | solution.py:297
  54.2 3.1 %shard_map.89 = f32[64,256]{1,0:T(8,128)S(1)} custom-call(bf16[64,128,256]{2,1,0:T(8,128)(2,1)} %get-tuple-element.16.refs_0_, bf16[64,128,256]{2,1,0:T(8,128)(2,1)} %get-tuple-element.18.refs_1_, s32[1]{0:T(128)} %bitcast.2.refs_2_, bf16[256,256]{1,0:T(8,128)(2,1)S(1)} %maximum_select_fusion.4.refs_3_.refs_2_, bf16[128,256]{1,0:T(8,128)(2,1)S(1)} %copy-done.1), custom_call_target="tpu_custom_call" | custom-call | flops 1073741824 | bytes 4194304 | tf_op jit(solution)/shard_map/pallas_call | solution.py:224
  57.4 1.6 %collective-permute-start.15 = (f32[64,256]{1,0:T(8,128)S(1)}, f32[64,256]{1,0:T(8,128)S(1)}, u32[]{:S(2)}, u32[]{:S(2)}) collective-permute-start(f32[64,256]{1,0:T(8,128)S(1)} %shard_map.89), channel_id=1, source_target_pairs={{0,16},{16,0},{1,17},{17,1},{2,18},{18,2},{3,19},{19,3},{4,20},{20... | collective-permute-start | bytes 196616 | tf_op jit(solution)/shard_map/ppermute | solution.py:297
  58.9 3.8 %shard_map.88 = (f32[64,256]{1,0:T(8,128)S(1)}, bf16[256,256]{1,0:T(8,128)(2,1)}) custom-call(bf16[64,128,256]{2,1,0:T(8,128)(2,1)} %get-tuple-element.16.refs_0_, bf16[64,128,256]{2,1,0:T(8,128)(2,1)} %get-tuple-element.18.refs_1_, s32[1]{0:T(128)} %bitcast.refs_2_, bf16[256,256]{1,0:T(8,128)(2,1)S(1)} %maximum_select_fusion.4.refs_3_.refs_2_, ...), custom_call_target="tpu_custom_call" | custom-call | flops 1073741824 | bytes 4194304 | tf_op jit(solution)/shard_map/pallas_call | solution.py:224
  62.8 1.0 %collective-permute-start.17 = (f32[64,256]{1,0:T(8,128)S(1)}, f32[64,256]{1,0:T(8,128)S(1)}, u32[]{:S(2)}, u32[]{:S(2)}) collective-permute-start(f32[64,256]{1,0:T(8,128)S(1)} %add.142), channel_id=1, source_target_pairs={{0,2},{1,3},{2,0},{3,1},{4,6},{5,7},{6,4},{7,5},{8,10},{9,11},{10,... | collective-permute-start | bytes 196616 | tf_op jit(solution)/shard_map/ppermute | solution.py:297
  63.8 3.4 %collective-permute-start.18 = (f32[64,256]{1,0:T(8,128)S(1)}, f32[64,256]{1,0:T(8,128)S(1)}, u32[]{:S(2)}, u32[]{:S(2)}) collective-permute-start(f32[64,256]{1,0:T(8,128)S(1)} %add.142), channel_id=1, source_target_pairs={{0,3},{1,2},{2,1},{3,0},{4,7},{5,6},{6,5},{7,4},{8,11},{9,10},{10,... | collective-permute-start | bytes 196616 | tf_op jit(solution)/shard_map/ppermute | solution.py:297
  68.0 2.2 %collective-permute-done.17 = f32[64,256]{1,0:T(8,128)S(1)} collective-permute-done((f32[64,256]{1,0:T(8,128)S(1)}, f32[64,256]{1,0:T(8,128)S(1)}, u32[]{:S(2)}, u32[]{:S(2)}) %collective-permute-start.17) | collective-permute-done | bytes 65568 | tf_op jit(solution)/shard_map/ppermute | solution.py:297
  72.2 3.4 %collective-permute-done.22 = bf16[64,256]{1,0:T(8,128)(2,1)S(1)} collective-permute-done((bf16[64,256]{1,0:T(8,128)(2,1)S(1)}, bf16[64,256]{1,0:T(8,128)(2,1)S(1)}, u32[]{:S(2)}, u32[]{:S(2)}) %collective-permute-start.22) | collective-permute-done | bytes 32800 | tf_op jit(solution)/shard_map/ppermute | solution.py:297
  75.7 1.2 %collective-permute-start.27 = (bf16[128,256]{1,0:T(8,128)(2,1)S(1)}, bf16[128,256]{1,0:T(8,128)(2,1)S(1)}, u32[]{:S(2)}, u32[]{:S(2)}) collective-permute-start(bf16[128,256]{1,0:T(8,128)(2,1)S(1)} %maximum_select_fusion.9.refs_3_), channel_id=1, source_target_pairs={{0,8},{4,12},{8,0},{12,4},{1,9},{5,13},{9,1},{13,5},{2,10},{6,14},... | collective-permute-start | bytes 196616 | tf_op jit(solution)/shard_map/ppermute | solution.py:297
  76.8 4.9 %shard_map.90 = f32[128,256]{1,0:T(8,128)S(1)} custom-call(bf16[64,128,256]{2,1,0:T(8,128)(2,1)} %get-tuple-element.16.refs_0_, bf16[64,128,256]{2,1,0:T(8,128)(2,1)} %get-tuple-element.18.refs_1_, bf16[256,256]{1,0:T(8,128)(2,1)S(1)} %maximum_select_fusion.4.refs_3_.refs_2_, bf16[128,256]{1,0:T(8,128)(2,1)S(1)} %maximum_select_fusion.9.refs_3_), custom_call_target="tpu_custom_call" | custom-call | flops 2147483648 | bytes 8388608 | tf_op jit(solution)/shard_map/pallas_call | solution.py:269
  83.7 1.9 %collective-permute-start.26 = (f32[64,256]{1,0:T(8,128)S(1)}, f32[64,256]{1,0:T(8,128)S(1)}, u32[]{:S(2)}, u32[]{:S(2)}) collective-permute-start(f32[64,256]{1,0:T(8,128)S(1)} %dynamic-slice_add_fusion.3), channel_id=1, source_target_pairs={{0,24},{4,28},{8,16},{12,20},{16,8},{20,12},{24,0},{28,4},{1,25},{... | collective-permute-start | bytes 196616 | tf_op jit(solution)/shard_map/ppermute | solution.py:297
  85.6 1.1 %collective-permute-start.24 = (f32[64,256]{1,0:T(8,128)S(1)}, f32[64,256]{1,0:T(8,128)S(1)}, u32[]{:S(2)}, u32[]{:S(2)}) collective-permute-start(f32[64,256]{1,0:T(8,128)S(1)} %dynamic-slice_add_fusion.3), channel_id=1, source_target_pairs={{0,8},{4,12},{8,0},{12,4},{16,24},{20,28},{24,16},{28,20},{1,9},{5... | collective-permute-start | bytes 196616 | tf_op jit(solution)/shard_map/ppermute | solution.py:297
  88.1 1.3 %collective-permute-done.26 = f32[64,256]{1,0:T(8,128)S(1)} collective-permute-done((f32[64,256]{1,0:T(8,128)S(1)}, f32[64,256]{1,0:T(8,128)S(1)}, u32[]{:S(2)}, u32[]{:S(2)}) %collective-permute-start.26) | collective-permute-done | bytes 65568 | tf_op jit(solution)/shard_map/ppermute | solution.py:297
  89.3 0.9 %collective-permute-done.24 = f32[64,256]{1,0:T(8,128)S(1)} collective-permute-done((f32[64,256]{1,0:T(8,128)S(1)}, f32[64,256]{1,0:T(8,128)S(1)}, u32[]{:S(2)}, u32[]{:S(2)}) %collective-permute-start.24) | collective-permute-done | bytes 65568 | tf_op jit(solution)/shard_map/ppermute | solution.py:297
  90.4 1.2 %collective-permute-done.29 = bf16[64,256]{1,0:T(8,128)(2,1)S(1)} collective-permute-done((bf16[64,256]{1,0:T(8,128)(2,1)S(1)}, bf16[64,256]{1,0:T(8,128)(2,1)S(1)}, u32[]{:S(2)}, u32[]{:S(2)}) %collective-permute-start.29) | collective-permute-done | bytes 32800 | tf_op jit(solution)/shard_map/ppermute | solution.py:297
  (78 shorter events, 11.7 us)
Async XLA Ops:
  0.6 42.5 %copy-start = (bf16[256,256]{1,0:T(8,128)(2,1)S(1)}, bf16[256,256]{1,0:T(8,128)(2,1)}, u32[]{:S(2)}) copy-start(bf16[256,256]{1,0:T(8,128)(2,1)} %param.8) | copy-start | bytes 393220
  0.6 47.1 %collective-permute-start.20 = (bf16[128,256]{1,0:T(8,128)(2,1)}, bf16[128,256]{1,0:T(8,128)(2,1)S(1)}, u32[]{:S(2)}, u32[]{:S(2)}) collective-permute-start(bf16[128,256]{1,0:T(8,128)(2,1)} %refs_4_.3), channel_id=1, source_target_pairs={{0,1},{1,0},{2,3},{3,2},{4,5},{5,4},{6,7},{7,6},{8,9},{9,8},{10,11... | collective-permute-start | bytes 196616 | tf_op jit(solution)/shard_map/ppermute | solution.py:297
  6.2 12.1 %collective-permute-start.6 = (f32[128,512]{1,0:T(8,128)S(1)}, f32[128,512]{1,0:T(8,128)S(1)}, u32[]{:S(2)}, u32[]{:S(2)}) collective-permute-start(f32[128,512]{1,0:T(8,128)S(1)} %constant_dynamic-slice_fusion.3), channel_id=1, source_target_pairs={{0,4},{4,0},{8,12},{12,8},{1,5},{5,1},{9,13},{13,9},{2,6},{6,2},{1... | collective-permute-start | bytes 786440 | tf_op jit(solution)/shard_map/ppermute | solution.py:297
  6.3 13.7 %collective-permute-start = (f32[256,256]{1,0:T(8,128)S(1)}, f32[256,256]{1,0:T(8,128)S(1)}, u32[]{:S(2)}, u32[]{:S(2)}) collective-permute-start(f32[256,256]{1,0:T(8,128)S(1)} %constant_dynamic-slice_fusion.6), channel_id=1, source_target_pairs={{0,16},{16,0},{1,17},{17,1},{2,18},{18,2},{3,19},{19,3},{4,20},{20... | collective-permute-start | bytes 786440 | tf_op jit(solution)/shard_map/ppermute | solution.py:297
  18.3 29.5 %copy-start.1 = (bf16[128,256]{1,0:T(8,128)(2,1)S(1)}, bf16[128,256]{1,0:T(8,128)(2,1)}, u32[]{:S(2)}) copy-start(bf16[128,256]{1,0:T(8,128)(2,1)} %refs_4_.3) | copy-start | bytes 196612
  18.4 5.7 %collective-permute-start.7 = (f32[64,512]{1,0:T(8,128)S(1)}, f32[64,512]{1,0:T(8,128)S(1)}, u32[]{:S(2)}, u32[]{:S(2)}) collective-permute-start(f32[64,512]{1,0:T(8,128)S(1)} %constant_dynamic-slice_fusion.2), channel_id=1, source_target_pairs={{0,8},{4,12},{8,0},{12,4},{1,9},{5,13},{9,1},{13,5},{2,10},{6,14},... | collective-permute-start | bytes 393224 | tf_op jit(solution)/shard_map/ppermute | solution.py:297
  20.1 4.0 %collective-permute-start.1 = (f32[128,256]{1,0:T(8,128)S(1)}, f32[128,256]{1,0:T(8,128)S(1)}, u32[]{:S(2)}, u32[]{:S(2)}) collective-permute-start(f32[128,256]{1,0:T(8,128)S(1)} %constant_dynamic-slice_fusion.5), channel_id=1, source_target_pairs={{0,4},{4,0},{8,12},{12,8},{1,5},{5,1},{9,13},{13,9},{2,6},{6,2},{1... | collective-permute-start | bytes 393224 | tf_op jit(solution)/shard_map/ppermute | solution.py:297
  24.1 5.2 %collective-permute-start.2 = (f32[64,256]{1,0:T(8,128)S(1)}, f32[64,256]{1,0:T(8,128)S(1)}, u32[]{:S(2)}, u32[]{:S(2)}) collective-permute-start(f32[64,256]{1,0:T(8,128)S(1)} %constant_dynamic-slice_fusion.4), channel_id=1, source_target_pairs={{0,8},{4,12},{8,0},{12,4},{1,9},{5,13},{9,1},{13,5},{2,10},{6,14},... | collective-permute-start | bytes 196616 | tf_op jit(solution)/shard_map/ppermute | solution.py:297
  25.7 12.2 %collective-permute-start.9 = (f32[64,512]{1,0:T(8,128)S(1)}, f32[64,512]{1,0:T(8,128)S(1)}, u32[]{:S(2)}, u32[]{:S(2)}) collective-permute-start(f32[64,512]{1,0:T(8,128)S(1)} %pad_maximum_fusion), channel_id=1, source_target_pairs={{0,2},{1,3},{2,0},{3,1},{4,6},{5,7},{6,4},{7,5},{8,10},{9,11},{10,... | collective-permute-start | bytes 393224 | tf_op jit(solution)/shard_map/ppermute | solution.py:297
  28.4 12.7 %collective-permute-start.10 = (f32[64,512]{1,0:T(8,128)S(1)}, f32[64,512]{1,0:T(8,128)S(1)}, u32[]{:S(2)}, u32[]{:S(2)}) collective-permute-start(f32[64,512]{1,0:T(8,128)S(1)} %pad_maximum_fusion), channel_id=1, source_target_pairs={{0,3},{1,2},{2,1},{3,0},{4,7},{5,6},{6,5},{7,4},{8,11},{9,10},{10,... | collective-permute-start | bytes 393224 | tf_op jit(solution)/shard_map/ppermute | solution.py:297
  28.6 13.9 %collective-permute-start.8 = (f32[64,512]{1,0:T(8,128)S(1)}, f32[64,512]{1,0:T(8,128)S(1)}, u32[]{:S(2)}, u32[]{:S(2)}) collective-permute-start(f32[64,512]{1,0:T(8,128)S(1)} %pad_maximum_fusion), channel_id=1, source_target_pairs={{0,1},{1,0},{2,3},{3,2},{4,5},{5,4},{6,7},{7,6},{8,9},{9,8},{10,11... | collective-permute-start | bytes 393224 | tf_op jit(solution)/shard_map/ppermute | solution.py:297
  29.3 14.9 %collective-permute-start.4 = (f32[64,256]{1,0:T(8,128)S(1)}, f32[64,256]{1,0:T(8,128)S(1)}, u32[]{:S(2)}, u32[]{:S(2)}) collective-permute-start(f32[64,256]{1,0:T(8,128)S(1)} %dynamic-slice_add_fusion.4), channel_id=1, source_target_pairs={{0,2},{1,3},{2,0},{3,1},{4,6},{5,7},{6,4},{7,5},{8,10},{9,11},{10,... | collective-permute-start | bytes 196616 | tf_op jit(solution)/shard_map/ppermute | solution.py:297
  37.9 6.3 %collective-permute-start.5 = (f32[64,256]{1,0:T(8,128)S(1)}, f32[64,256]{1,0:T(8,128)S(1)}, u32[]{:S(2)}, u32[]{:S(2)}) collective-permute-start(f32[64,256]{1,0:T(8,128)S(1)} %dynamic-slice_add_fusion.4), channel_id=1, source_target_pairs={{0,3},{1,2},{2,1},{3,0},{4,7},{5,6},{6,5},{7,4},{8,11},{9,10},{10,... | collective-permute-start | bytes 196616 | tf_op jit(solution)/shard_map/ppermute | solution.py:297
  41.1 4.3 %collective-permute-start.3 = (f32[64,256]{1,0:T(8,128)S(1)}, f32[64,256]{1,0:T(8,128)S(1)}, u32[]{:S(2)}, u32[]{:S(2)}) collective-permute-start(f32[64,256]{1,0:T(8,128)S(1)} %dynamic-slice_add_fusion.4), channel_id=1, source_target_pairs={{0,1},{1,0},{2,3},{3,2},{4,5},{5,4},{6,7},{7,6},{8,9},{9,8},{10,11... | collective-permute-start | bytes 196616 | tf_op jit(solution)/shard_map/ppermute | solution.py:297
  42.5 4.3 %collective-permute-start.11 = (f32[64,256]{1,0:T(8,128)S(1)}, f32[64,256]{1,0:T(8,128)S(1)}, u32[]{:S(2)}, u32[]{:S(2)}) collective-permute-start(f32[64,256]{1,0:T(8,128)S(1)} %slice.19), channel_id=1, source_target_pairs={{0,16},{16,0},{1,17},{17,1},{2,18},{18,2},{3,19},{19,3},{4,20},{20... | collective-permute-start | bytes 196616 | tf_op jit(solution)/shard_map/ppermute | solution.py:297
  47.2 4.2 %collective-permute-start.12 = (bf16[64,256]{1,0:T(8,128)(2,1)S(1)}, bf16[64,256]{1,0:T(8,128)(2,1)S(1)}, u32[]{:S(2)}, u32[]{:S(2)}) collective-permute-start(bf16[64,256]{1,0:T(8,128)(2,1)S(1)} %fusion.17), channel_id=1, source_target_pairs={{0,8},{4,12},{8,0},{12,4},{1,9},{5,13},{9,1},{13,5},{2,10},{6,14},... | collective-permute-start | bytes 98312 | tf_op jit(solution)/shard_map/ppermute | solution.py:297
  47.8 19.7 %collective-permute-start.21 = (bf16[256,256]{1,0:T(8,128)(2,1)S(1)}, bf16[256,256]{1,0:T(8,128)(2,1)S(1)}, u32[]{:S(2)}, u32[]{:S(2)}) collective-permute-start(bf16[256,256]{1,0:T(8,128)(2,1)S(1)} %maximum_select_fusion.5), channel_id=1, source_target_pairs={{0,2},{1,3},{2,0},{3,1},{4,6},{5,7},{6,4},{7,5},{8,10},{9,11},{10,... | collective-permute-start | bytes 393224 | tf_op jit(solution)/shard_map/ppermute | solution.py:297
  49.8 3.6 %collective-permute-start.14 = (bf16[64,256]{1,0:T(8,128)(2,1)S(1)}, bf16[64,256]{1,0:T(8,128)(2,1)S(1)}, u32[]{:S(2)}, u32[]{:S(2)}) collective-permute-start(bf16[64,256]{1,0:T(8,128)(2,1)S(1)} %fusion.17), channel_id=1, source_target_pairs={{0,12},{4,8},{8,4},{12,0},{1,13},{5,9},{9,5},{13,1},{2,14},{6,10},... | collective-permute-start | bytes 98312 | tf_op jit(solution)/shard_map/ppermute | solution.py:297
  49.8 3.6 %collective-permute-start.13 = (bf16[64,256]{1,0:T(8,128)(2,1)S(1)}, bf16[64,256]{1,0:T(8,128)(2,1)S(1)}, u32[]{:S(2)}, u32[]{:S(2)}) collective-permute-start(bf16[64,256]{1,0:T(8,128)(2,1)S(1)} %fusion.17), channel_id=1, source_target_pairs={{0,4},{4,0},{8,12},{12,8},{1,5},{5,1},{9,13},{13,9},{2,6},{6,2},{1... | collective-permute-start | bytes 98312 | tf_op jit(solution)/shard_map/ppermute | solution.py:297
  53.7 13.6 %collective-permute-start.19 = (bf16[256,256]{1,0:T(8,128)(2,1)S(1)}, bf16[256,256]{1,0:T(8,128)(2,1)S(1)}, u32[]{:S(2)}, u32[]{:S(2)}) collective-permute-start(bf16[256,256]{1,0:T(8,128)(2,1)S(1)} %maximum_select_fusion.4.refs_3_.refs_2_), channel_id=1, source_target_pairs={{0,16},{16,0},{1,17},{17,1},{2,18},{18,2},{3,19},{19,3},{4,20},{20... | collective-permute-start | bytes 393224 | tf_op jit(solution)/shard_map/ppermute | solution.py:297
  57.4 5.4 %collective-permute-start.15 = (f32[64,256]{1,0:T(8,128)S(1)}, f32[64,256]{1,0:T(8,128)S(1)}, u32[]{:S(2)}, u32[]{:S(2)}) collective-permute-start(f32[64,256]{1,0:T(8,128)S(1)} %shard_map.89), channel_id=1, source_target_pairs={{0,16},{16,0},{1,17},{17,1},{2,18},{18,2},{3,19},{19,3},{4,20},{20... | collective-permute-start | bytes 196616 | tf_op jit(solution)/shard_map/ppermute | solution.py:297
  62.8 7.4 %collective-permute-start.17 = (f32[64,256]{1,0:T(8,128)S(1)}, f32[64,256]{1,0:T(8,128)S(1)}, u32[]{:S(2)}, u32[]{:S(2)}) collective-permute-start(f32[64,256]{1,0:T(8,128)S(1)} %add.142), channel_id=1, source_target_pairs={{0,2},{1,3},{2,0},{3,1},{4,6},{5,7},{6,4},{7,5},{8,10},{9,11},{10,... | collective-permute-start | bytes 196616 | tf_op jit(solution)/shard_map/ppermute | solution.py:297
  63.8 7.1 %collective-permute-start.18 = (f32[64,256]{1,0:T(8,128)S(1)}, f32[64,256]{1,0:T(8,128)S(1)}, u32[]{:S(2)}, u32[]{:S(2)}) collective-permute-start(f32[64,256]{1,0:T(8,128)S(1)} %add.142), channel_id=1, source_target_pairs={{0,3},{1,2},{2,1},{3,0},{4,7},{5,6},{6,5},{7,4},{8,11},{9,10},{10,... | collective-permute-start | bytes 196616 | tf_op jit(solution)/shard_map/ppermute | solution.py:297
  67.2 4.4 %collective-permute-start.16 = (f32[64,256]{1,0:T(8,128)S(1)}, f32[64,256]{1,0:T(8,128)S(1)}, u32[]{:S(2)}, u32[]{:S(2)}) collective-permute-start(f32[64,256]{1,0:T(8,128)S(1)} %add.142), channel_id=1, source_target_pairs={{0,1},{1,0},{2,3},{3,2},{4,5},{5,4},{6,7},{7,6},{8,9},{9,8},{10,11... | collective-permute-start | bytes 196616 | tf_op jit(solution)/shard_map/ppermute | solution.py:297
  71.7 4.0 %collective-permute-start.22 = (bf16[64,256]{1,0:T(8,128)(2,1)S(1)}, bf16[64,256]{1,0:T(8,128)(2,1)S(1)}, u32[]{:S(2)}, u32[]{:S(2)}) collective-permute-start(bf16[64,256]{1,0:T(8,128)(2,1)S(1)} %divide_convert_fusion.1), channel_id=1, source_target_pairs={{0,16},{16,0},{1,17},{17,1},{2,18},{18,2},{3,19},{19,3},{4,20},{20... | collective-permute-start | bytes 98312 | tf_op jit(solution)/shard_map/ppermute | solution.py:297
  75.7 6.2 %collective-permute-start.27 = (bf16[128,256]{1,0:T(8,128)(2,1)S(1)}, bf16[128,256]{1,0:T(8,128)(2,1)S(1)}, u32[]{:S(2)}, u32[]{:S(2)}) collective-permute-start(bf16[128,256]{1,0:T(8,128)(2,1)S(1)} %maximum_select_fusion.9.refs_3_), channel_id=1, source_target_pairs={{0,8},{4,12},{8,0},{12,4},{1,9},{5,13},{9,1},{13,5},{2,10},{6,14},... | collective-permute-start | bytes 196616 | tf_op jit(solution)/shard_map/ppermute | solution.py:297
  81.8 1.3 %collective-permute-start.23 = (f32[64,256]{1,0:T(8,128)S(1)}, f32[64,256]{1,0:T(8,128)S(1)}, u32[]{:S(2)}, u32[]{:S(2)}) collective-permute-start(f32[64,256]{1,0:T(8,128)S(1)} %constant_dynamic-slice_fusion), channel_id=1, source_target_pairs={{0,4},{4,0},{8,12},{12,8},{1,5},{5,1},{9,13},{13,9},{2,6},{6,2},{1... | collective-permute-start | bytes 196616 | tf_op jit(solution)/shard_map/ppermute | solution.py:297
  81.9 4.8 %collective-permute-start.28 = (bf16[256,256]{1,0:T(8,128)(2,1)S(1)}, bf16[256,256]{1,0:T(8,128)(2,1)S(1)}, u32[]{:S(2)}, u32[]{:S(2)}) collective-permute-start(bf16[256,256]{1,0:T(8,128)(2,1)S(1)} %maximum_select_fusion.6), channel_id=1, source_target_pairs={{0,4},{4,0},{8,12},{12,8},{1,5},{5,1},{9,13},{13,9},{2,6},{6,2},{1... | collective-permute-start | bytes 393224 | tf_op jit(solution)/shard_map/ppermute | solution.py:297
  83.1 4.9 %collective-permute-start.25 = (f32[64,256]{1,0:T(8,128)S(1)}, f32[64,256]{1,0:T(8,128)S(1)}, u32[]{:S(2)}, u32[]{:S(2)}) collective-permute-start(f32[64,256]{1,0:T(8,128)S(1)} %dynamic-slice_add_fusion.3), channel_id=1, source_target_pairs={{0,16},{4,20},{8,24},{12,28},{16,0},{20,4},{24,8},{28,12},{1,17},{... | collective-permute-start | bytes 196616 | tf_op jit(solution)/shard_map/ppermute | solution.py:297
  83.7 5.6 %collective-permute-start.26 = (f32[64,256]{1,0:T(8,128)S(1)}, f32[64,256]{1,0:T(8,128)S(1)}, u32[]{:S(2)}, u32[]{:S(2)}) collective-permute-start(f32[64,256]{1,0:T(8,128)S(1)} %dynamic-slice_add_fusion.3), channel_id=1, source_target_pairs={{0,24},{4,28},{8,16},{12,20},{16,8},{20,12},{24,0},{28,4},{1,25},{... | collective-permute-start | bytes 196616 | tf_op jit(solution)/shard_map/ppermute | solution.py:297
  85.6 4.6 %collective-permute-start.24 = (f32[64,256]{1,0:T(8,128)S(1)}, f32[64,256]{1,0:T(8,128)S(1)}, u32[]{:S(2)}, u32[]{:S(2)}) collective-permute-start(f32[64,256]{1,0:T(8,128)S(1)} %dynamic-slice_add_fusion.3), channel_id=1, source_target_pairs={{0,8},{4,12},{8,0},{12,4},{16,24},{20,28},{24,16},{28,20},{1,9},{5... | collective-permute-start | bytes 196616 | tf_op jit(solution)/shard_map/ppermute | solution.py:297
  90.3 1.3 %collective-permute-start.29 = (bf16[64,256]{1,0:T(8,128)(2,1)S(1)}, bf16[64,256]{1,0:T(8,128)(2,1)S(1)}, u32[]{:S(2)}, u32[]{:S(2)}) collective-permute-start(bf16[64,256]{1,0:T(8,128)(2,1)S(1)} %divide_convert_fusion), channel_id=1, source_target_pairs={{0,4},{4,0},{8,12},{12,8},{1,5},{5,1},{9,13},{13,9},{2,6},{6,2},{1... | collective-permute-start | bytes 98312 | tf_op jit(solution)/shard_map/ppermute | solution.py:297
  (2 other events, 15.1 us)
